TPU v7x, 512 devices: a whole 4x4x16 slice. The times are simulated.
512 devices in a mesh: mode: 8 (over x, core), band: 64 (over z, y).
Axes of the slice: x: 4, y: 4, z: 16, core: 2. Of those that a mesh axis runs over, the one named last changes fastest.
Arguments:
- mode_field: bfloat16 [8, 4096, 2, 4096], P('mode', 'band'), may hold values from -4 to 4
- figure: bfloat16 [4096, 4096], P('band'), may hold values from -6 to 6
- target: bfloat16 [4096, 4096], P('band'), may hold values from 0 to 2
- footprint: int32 [64, 64], replicated, may hold values from 0 to 4095, as said below
- approach_tiles: bfloat16 [3, 2, 128, 128], replicated, may hold values from -0.21875 to 0.21875
- focus_tiles: bfloat16 [3, 2, 128, 128], replicated, may hold values from -0.21875 to 0.21875
Outputs:
- sensitivity: float32 [4096, 4096], P('band')
Inputs may be any that keep to these rules, and one draw needn't show every extreme that they name: `footprint`: entry [d, j] is the surface tile band * 64 + block read by beam tile j of band d; for every beam band d and surface band s at most 2 entries of row d name band s, and some row reaches 2 in every draw.
All inputs are finite; a program needn't handle non-finite values.
Results may differ from a plain program's by a relative error of at most 0.0082.
Values may be sent and summed in bfloat16 or wider, within the bound.
No kernel may reach another device: no remote copies, remote signals or barrier semaphores. Data moves between devices by JAX's collectives and lax.ppermute only.
A program may use at most 64 MiB of HBM per device.

v0:
```python
import jax
import jax.numpy as jnp
from jax import lax
from jax.sharding import PartitionSpec as P

MIRROR_TILE = 64


PHASE_FACTOR = 4.0


def real_kernels(tile_set):
    real_part = tile_set[:, 0]
    imag_part = tile_set[:, 1]
    upper = jnp.stack([real_part, imag_part], axis=2)
    lower = jnp.stack([-imag_part, real_part], axis=2)
    return jnp.stack([upper, lower], axis=1)


def banded(grid_field, kernels):
    leading = grid_field.shape[:-1]
    tile_width = kernels.shape[2]
    mirror_block_list = grid_field.shape[-1] // tile_width
    reshaped_field = grid_field.reshape(leading + (mirror_block_list, tile_width))
    keep = [(0, 0)] * len(leading)
    centre = jnp.einsum(
        "mrcbk,ckel->mrebl", reshaped_field, kernels[1], preferred_element_type=jnp.float32
    )
    from_lower = jnp.einsum(
        "mrcbk,ckel->mrebl",
        reshaped_field[..., :-1, :],
        kernels[0],
        preferred_element_type=jnp.float32,
    )
    from_upper = jnp.einsum(
        "mrcbk,ckel->mrebl",
        reshaped_field[..., 1:, :],
        kernels[2],
        preferred_element_type=jnp.float32,
    )
    running = (
        centre
        + jnp.pad(from_lower, keep + [(1, 0), (0, 0)])
        + jnp.pad(from_upper, keep + [(0, 1), (0, 0)])
    )
    return running.reshape(grid_field.shape)


def tiles_out(beam_row_lines, receive_hot):
    count_of_rows = beam_row_lines.shape[0]
    reshaped_field = beam_row_lines.reshape(count_of_rows, -1, MIRROR_TILE)
    packed_tiles = jnp.einsum(
        "jsc,rjl->scrl", receive_hot, reshaped_field, precision=lax.Precision.HIGHEST
    )
    return packed_tiles.reshape(
        packed_tiles.shape[0], packed_tiles.shape[1], count_of_rows * MIRROR_TILE
    )


def tiles_in(received_tiles, slot_source):
    reshaped_field = received_tiles.reshape(
        received_tiles.shape[0], received_tiles.shape[1], -1, MIRROR_TILE
    )
    placed = jnp.einsum(
        "dck,dcrl->rkl", slot_source, reshaped_field, precision=lax.Precision.HIGHEST
    )
    return placed.reshape(placed.shape[0], -1)


def fetch_heights(surface_rows, slot_source):
    count_of_bands = slot_source.shape[0]
    subset_rows = surface_rows.shape[0]
    outbound_tiles = jnp.einsum(
        "dck,rkl->dcrl",
        slot_source.astype(jnp.bfloat16),
        surface_rows,
        preferred_element_type=jnp.float32,
    ).astype(jnp.bfloat16)
    outbound_tiles = outbound_tiles.reshape(
        count_of_bands, outbound_tiles.shape[1], subset_rows * MIRROR_TILE
    )
    return outbound_tiles


def shards(mode_field, figure, target, footprint, approach_tiles, focus_tiles):
    count_of_bands = lax.axis_size("band")
    band_index = lax.axis_index("band")
    count_of_rows = figure.shape[0]
    mirror_block_list = figure.shape[1] // MIRROR_TILE
    slot_capacity = max(2, 2 * mirror_block_list // count_of_bands)
    approach = real_kernels(approach_tiles)
    focus = real_kernels(focus_tiles)
    adjoint = jnp.transpose(focus, (0, 3, 4, 1, 2))[::-1]
    source_band = footprint // mirror_block_list
    source_block = footprint % mirror_block_list
    column = jnp.arange(mirror_block_list, dtype=jnp.int32)
    earlier = column[None, :] < column[:, None]
    same_band = source_band[:, :, None] == source_band[:, None, :]
    tile_rank = jnp.sum((same_band & earlier[None]).astype(jnp.int32), axis=2)
    slot_ids = jnp.arange(slot_capacity, dtype=jnp.int32)
    band_ids = jnp.arange(count_of_bands, dtype=jnp.int32)
    from_here = (source_band == band_index)[:, None, :] & (
        tile_rank[:, None, :] == slot_ids[None, :, None]
    )
    block_hot = (source_block[:, :, None] == column[None, None, :]).astype(jnp.float32)
    slot_source = jnp.einsum("dcj,djk->dck", from_here.astype(jnp.float32), block_hot)
    my_band = lax.dynamic_index_in_dim(source_band, band_index, 0, keepdims=False)
    my_rank = lax.dynamic_index_in_dim(tile_rank, band_index, 0, keepdims=False)
    receive_hot = (
        (my_band[:, None, None] == band_ids[None, :, None])
        & (my_rank[:, None, None] == slot_ids[None, None, :])
    ).astype(jnp.float32)
    receive_low = receive_hot.astype(jnp.bfloat16)
    surface_owned = figure.reshape(count_of_rows, mirror_block_list, MIRROR_TILE)
    outbound_tiles = fetch_heights(surface_owned, slot_source)
    inbound_tiles = lax.all_to_all(outbound_tiles, "band", split_axis=0, concat_axis=0, tiled=True)
    inbound_tiles = inbound_tiles.reshape(count_of_bands, slot_capacity, count_of_rows, MIRROR_TILE)
    phase_tile_stack = jnp.einsum(
        "jsc,scrl->rjl", receive_low, inbound_tiles, preferred_element_type=jnp.float32
    )
    phase_delay = PHASE_FACTOR * phase_tile_stack.reshape(
        count_of_rows, mirror_block_list * MIRROR_TILE
    )
    cosine = jnp.cos(phase_delay)
    sine_part = jnp.sin(phase_delay)
    propagated = banded(mode_field, approach).astype(jnp.bfloat16)
    moved = lax.all_to_all(propagated, "band", split_axis=3, concat_axis=1, tiled=True)
    turned = jnp.transpose(moved, (0, 3, 2, 1))
    advanced = banded(turned, approach).astype(jnp.bfloat16)
    real_part = advanced[:, :, 0].astype(jnp.float32)
    imag_part = advanced[:, :, 1].astype(jnp.float32)
    screened = jnp.stack(
        [real_part * cosine - imag_part * sine_part, real_part * sine_part + imag_part * cosine],
        axis=2,
    ).astype(jnp.bfloat16)
    detected = banded(screened, focus)
    local_power = jnp.sum(detected * detected, axis=(0, 2))
    intensity = lax.psum(local_power, "mode")
    residual = intensity - target.astype(jnp.float32)
    detector_grad = (detected * residual[None, :, None, :]).astype(jnp.bfloat16)
    mirror_grad = banded(detector_grad, adjoint)
    screen_real = screened[:, :, 0].astype(jnp.float32)
    screen_imag = screened[:, :, 1].astype(jnp.float32)
    local_sens = jnp.sum(
        2.0
        * PHASE_FACTOR
        * (mirror_grad[:, :, 1] * screen_real - mirror_grad[:, :, 0] * screen_imag),
        axis=0,
    )
    beam_sens = lax.psum(local_sens, "mode")
    returned = lax.all_to_all(
        tiles_out(beam_sens, receive_hot), "band", split_axis=0, concat_axis=0, tiled=True
    )
    sensitivity = tiles_in(returned, slot_source)
    return sensitivity


def solution(mesh):
    in_specs = (P("mode", "band", None, None), P("band", None), P("band", None), P(), P(), P())
    out_specs = P("band", None)
    return jax.shard_map(shards, mesh=mesh, in_specs=in_specs, out_specs=out_specs, check_vma=False)
```

profile of v0, /device:TPU:6, one launch (start us, length us, event | category | flops | bytes accessed | tf_op | source)
XLA Modules:
  0.0 494.1 jit_solution(12354892742826610591)
XLA Ops:
  15.8 3.1 copy.230
  18.9 2.3 reshape.412
  21.1 19.4 %all-to-all-start = ((bf16[64,2,4096]{2,1,0:T(2,128)(2,1)}), bf16[64,2,4096]{2,1,0:T(2,128)(2,1)S(1)}, u32[]{:S(2)}, u32[]{:S(2)}) async-start(bf16[64,2,4096]{2,1,0:T(2,128)(2,1)} %reshape.412), calls=%async_computation | async-start | bytes 2097152 | tf_op jit(solution)/shard_map/all_to_all | solution.py:127
  47.8 2.3 reshape.409
  50.1 45.7 %all-to-all-done = bf16[64,2,4096]{2,1,0:T(2,128)(2,1)S(1)} async-done(((bf16[64,2,4096]{2,1,0:T(2,128)(2,1)}), bf16[64,2,4096]{2,1,0:T(2,128)(2,1)S(1)}, u32[]{:S(2)}, u32[]{:S(2)}) %all-to-all-start) | async-done | bytes 1048608 | tf_op jit(solution)/shard_map/all_to_all | solution.py:127
  95.8 6.1 %all-to-all-start.1 = ((bf16[64,2,4096]{2,1,0:T(2,128)(2,1)}), bf16[64,2,4096]{2,1,0:T(2,128)(2,1)}, u32[]{:S(2)}, u32[]{:S(2)}) async-start(bf16[64,2,4096]{2,1,0:T(2,128)(2,1)} %reshape.409), calls=%async_computation.1 | async-start | bytes 2097152 | tf_op jit(solution)/shard_map/all_to_all | solution.py:116
  103.6 5.1 %reshape.413 = bf16[4096,1,2,64]{3,2,1,0:T(2,128)(2,1)S(1)} reshape(bf16[64,2,4096]{2,1,0:T(2,128)(2,1)} %copy-done) | data formatting | bytes 2097152
  108.7 2.7 copy.326
  111.4 3.3 all_to_all.22
  118.4 37.7 %all-to-all-done.1 = bf16[64,2,4096]{2,1,0:T(2,128)(2,1)} async-done(((bf16[64,2,4096]{2,1,0:T(2,128)(2,1)}), bf16[64,2,4096]{2,1,0:T(2,128)(2,1)}, u32[]{:S(2)}, u32[]{:S(2)}) %all-to-all-start.1) | async-done | bytes 1048608 | tf_op jit(solution)/shard_map/all_to_all | solution.py:116
  156.2 4.8 reshape.410
  161.0 10.4 %sine_bitcast_fusion = (f32[64,64,64]{1,2,0:T(8,128)}, f32[64,64,64]{1,2,0:T(8,128)S(1)}) fusion(pred[64,2]{0,1:T(4,128)(4,1)S(1)} %iota_compare_fusion.4, pred[64,64]{0,1:T(8,128)(4,1)S(1)} %iota_compare_fusion.3, bf16[64,2,64,64]{3,2,1,0:T(8,128)(2,1)} %reshape.410), kind=kOutput, calls=%fused_computation.18 | convolution fusion | flops 67395584 | bytes 3149952 | tf_op jit(solution)/shard_map/jsc,scrl->rjl/dot_general | solution.py:118
  171.3 2.9 copy.178
  174.2 2.9 sin.21
  178.9 2.4 cos.21
  186.4 67.3 %all-reduce.11.cloned.1.call-done = f32[64,4096]{1,0:T(8,128)} async-done(((f32[64,4096]{1,0:T(8,128)}), f32[64,4096]{1,0:T(8,128)}) %all-reduce.11.cloned.1.call-update) | async-done | bytes 1048592 | tf_op jit(solution)/shard_map/psum | solution.py:138
  258.8 2.8 fusion.22
  263.8 2.5 copy.194
  266.4 2.9 dot_general.107
  269.3 77.5 %all-reduce.13.cloned.1.call-done = f32[4096,64]{0,1:T(8,128)} async-done(((f32[4096,64]{0,1:T(8,128)}), f32[4096,64]{0,1:T(8,128)}) %all-reduce.13.cloned.1.call-update) | async-done | bytes 1048592 | tf_op jit(solution)/shard_map/psum | solution.py:150
  350.6 117.1 %all_to_all.28 = f32[64,2,4096]{2,1,0:T(2,128)S(1)} all-to-all(f32[64,2,4096]{2,1,0:T(2,128)S(1)} %copy.195), channel_id=1, replica_groups=mesh['mode'=8,'band'=64] {'band'}, dimensions={0} | all-to-all | bytes 4194304 | tf_op jit(solution)/shard_map/all_to_all | solution.py:151
  467.8 3.7 reshape.411
  471.4 10.7 %fusion.11 = f32[64,64,64]{1,2,0:T(8,128)S(1)} fusion(f32[64,2,64,64]{3,2,1,0:T(8,128)} %reshape.411, f32[64,2,64]{2,1,0:T(2,128)S(1)} %copy-done.7), kind=kOutput, calls=%fused_computation.24 | convolution fusion | flops 402653184 | bytes 3178496 | tf_op jit(solution)/shard_map/dck,dcrl->rkl/dot_general | solution.py:64
  483.9 2.9 reshape.365
  (80 shorter events, 41.4 us)
Async XLA Ops:
  6.5 3.8 copy-start.1
  21.1 19.4 %copy-start.3 = (bf16[64,4096]{1,0:T(8,128)(2,1)S(1)}, bf16[64,4096]{1,0:T(8,128)(2,1)}, u32[]{:S(2)}) copy-start(bf16[64,4096]{1,0:T(8,128)(2,1)} %param.7) | copy-start | bytes 1572868
  21.1 20.5 %copy-start.8 = (s32[64,64]{1,0:T(8,128)S(1)}, s32[64,64]{1,0:T(8,128)}, u32[]{:S(2)}) copy-start(s32[64,64]{1,0:T(8,128)} %param.9) | copy-start | bytes 49156
  21.1 74.7 %all-to-all-start = ((bf16[64,2,4096]{2,1,0:T(2,128)(2,1)}), bf16[64,2,4096]{2,1,0:T(2,128)(2,1)S(1)}, u32[]{:S(2)}, u32[]{:S(2)}) async-start(bf16[64,2,4096]{2,1,0:T(2,128)(2,1)} %reshape.412), calls=%async_computation | async-start | bytes 2097152 | tf_op jit(solution)/shard_map/all_to_all | solution.py:127
  41.7 3.4 copy-start.5
  43.6 0.6 copy-start.9
  45.1 0.6 copy-start.6
  50.1 53.4 %copy-start.4 = (bf16[3,2,128,128]{3,2,1,0:T(8,128)(2,1)S(1)}, bf16[3,2,128,128]{3,2,1,0:T(8,128)(2,1)}, u32[]{:S(2)}) copy-start(bf16[3,2,128,128]{3,2,1,0:T(8,128)(2,1)} %param.11) | copy-start | bytes 589828
  95.8 7.7 %copy-start = (bf16[64,2,4096]{2,1,0:T(2,128)(2,1)}, bf16[64,2,4096]{2,1,0:T(2,128)(2,1)S(1)}, u32[]{:S(2)}) copy-start(bf16[64,2,4096]{2,1,0:T(2,128)(2,1)S(1)} %all-to-all-done) | copy-start | bytes 3145732
  95.8 60.4 %all-to-all-start.1 = ((bf16[64,2,4096]{2,1,0:T(2,128)(2,1)}), bf16[64,2,4096]{2,1,0:T(2,128)(2,1)}, u32[]{:S(2)}, u32[]{:S(2)}) async-start(bf16[64,2,4096]{2,1,0:T(2,128)(2,1)} %reshape.409), calls=%async_computation.1 | async-start | bytes 2097152 | tf_op jit(solution)/shard_map/all_to_all | solution.py:116
  101.9 151.8 %all-reduce.11.cloned.1.call-start = ((), (), s32[]{:S(2)}) async-start(), calls=%async_computation.3 | async-start | bytes 2097152 | tf_op jit(solution)/shard_map/psum | solution.py:138
  178.9 2.4 copy-start.2
  186.3 160.5 %all-reduce.13.cloned.1.call-start = ((), (), s32[]{:S(2)}) async-start(), calls=%async_computation.4 | async-start | bytes 2097152 | tf_op jit(solution)/shard_map/psum | solution.py:150
  467.8 3.7 copy-start.7
Sparse Core Ops, SparseCore 0:
  186.4 67.2 all-reduce.10
  269.4 77.3 all-reduce.12
where the time goes:
time: 501 us; the launch traced here: 494 us
  waiting for transfers between devices  228 us (46%)
  blocking collectives  117 us (23%)
  local copies, waits for them, and re-layouts  66.2 us (13%)
  matrix products  33.2 us (7%)
  starting transfers between devices  25.7 us (5%)
  between operations  14.4 us (3%)
  other arithmetic  9.21 us (2%)
    all_to_all x1, blocking collectives, shards(): lax.all_to_all(tiles_out(beam_sens, receive_hot), 'band', split_axis=0, c...  117 us
    psum x1, waiting for transfers between devices, shards(): beam_sens = lax.psum(local_sens, 'mode')  77.5 us
    psum x1, waiting for transfers between devices, shards(): intensity = lax.psum(local_power, 'mode')  67.3 us
    all_to_all x1, waiting for transfers between devices, shards(): lax.all_to_all(propagated, 'band', split_axis=3, concat_axis=1, tiled=True)  45.7 us
    all_to_all x1, waiting for transfers between devices, shards(): lax.all_to_all(outbound_tiles, 'band', split_axis=0, concat_axis=0, tiled...  37.7 us
    all_to_all x1, starting transfers between devices, shards(): lax.all_to_all(propagated, 'band', split_axis=3, concat_axis=1, tiled=True)  19.4 us
    dot_general x1, matrix products, tiles_in(): jnp.einsum('dck,dcrl->rkl', slot_source, reshaped_field, precision=lax.Pr...  10.7 us
    dot_general x1, matrix products, shards(): jnp.einsum('jsc,scrl->rjl', receive_low, inbound_tiles, preferred_element...  10.4 us
  transfers between devices with their start and end apart: 4, of which 4 were waited for; matrix products, arithmetic and copies ran while one was open for 4% of the time, Pallas kernels for 0%

commit v1 on v0

v1 whole, which is shorter than its diff:
```python
import functools

import jax
import jax.numpy as jnp
from jax import lax
from jax.experimental import pallas as pl
from jax.experimental.pallas import tpu as pltpu
from jax.sharding import PartitionSpec as P

TILE = 128
HALF = 64
MIRROR_TILE = 64
PHASE_FACTOR = 4.0
F32 = jnp.float32
BF16 = jnp.bfloat16


def whole(*_):
    return pl.BlockSpec(memory_space=pltpu.VMEM)


def write_weights(tiles_ref, w_ref, split):
    for o in range(3):
        re = tiles_ref[o, 0].astype(F32)
        im = tiles_ref[o, 1].astype(F32)
        upper = jnp.concatenate([re, im], axis=1).astype(BF16)
        lower = jnp.concatenate([-im, re], axis=1).astype(BF16)
        if split:
            w_ref[o, 0:64] = upper[0:64]
            w_ref[o, 64:128] = lower[0:64]
            w_ref[o, 128:192] = upper[64:128]
            w_ref[o, 192:256] = lower[64:128]
        else:
            w_ref[o, 0:128] = upper
            w_ref[o, 128:256] = lower


def banded_rows(x_ref, w_ref, row, count, rows, flip=False):
    total = None
    for o in range(3):
        x = x_ref[pl.ds(pl.multiple_of(row + o * rows, 64), count)]
        if flip:
            part = lax.dot_general(x, w_ref[2 - o], (((1,), (1,)), ((), ())), preferred_element_type=F32)
        else:
            part = jnp.dot(x, w_ref[o], preferred_element_type=F32)
        total = part if total is None else total + part
    return total


def first_kernel(field_ref, tiles_ref, out_ref, x_ref, w_ref):
    rows = field_ref.shape[1]
    count_tiles = field_ref.shape[3] // TILE
    write_weights(tiles_ref, w_ref, False)
    x_ref[0:rows] = jnp.zeros((rows, 256), BF16)
    x_ref[(count_tiles + 1) * rows : (count_tiles + 2) * rows] = jnp.zeros((rows, 256), BF16)

    def fill(j, carry):
        at = pl.ds(pl.multiple_of(j * TILE, TILE), TILE)
        to = pl.ds(pl.multiple_of((j + 1) * rows, 64), rows)
        both = field_ref[0, :, :, at].astype(F32)
        x_ref[to, 0:128] = both[:, 0].astype(BF16)
        x_ref[to, 128:256] = both[:, 1].astype(BF16)
        return carry

    lax.fori_loop(0, count_tiles, fill, 0, unroll=4)
    step = 4

    def chunk(q, carry):
        got = banded_rows(x_ref, w_ref, q * (step * rows), step * rows, rows)
        for t in range(step):
            mine = got[t * rows : (t + 1) * rows]
            stacked = jnp.concatenate([mine[:, 0:128], mine[:, 128:256]], axis=0)
            turned = jnp.transpose(stacked).astype(BF16)
            at = (q * step + t) * 2
            for h in range(2):
                out_ref[:, pl.ds(at + h, 1)] = turned[h * 64 : (h + 1) * 64].reshape(8, 1, 8, 128)
        return carry

    lax.fori_loop(0, count_tiles // step, chunk, 0)


def first_stage(field, tiles):
    rows, length = field.shape[1], field.shape[3]
    tiles_count = length // TILE
    return pl.pallas_call(
        first_kernel,
        out_shape=jax.ShapeDtypeStruct((8, length // 64, 8, 128), BF16),
        in_specs=[whole(), whole()],
        out_specs=whole(),
        scratch_shapes=[pltpu.VMEM(((tiles_count + 2) * rows, 256), BF16), pltpu.VMEM((3, 256, 256), BF16)],
        cost_estimate=pl.CostEstimate(flops=2 * rows * tiles_count * 768 * 256, bytes_accessed=1 << 21, transcendentals=0),
        name="first",
    )(field, tiles)


def half_of(x, want, lane):
    return jnp.where(want, pltpu.roll(x, 64, 1), x)


def heights_out_kernel(index_ref, mine_ref, figure_ref, out_ref, wide_ref):
    count = out_ref.shape[0]
    pairs = figure_ref.shape[1] // 128
    lane = lax.broadcasted_iota(jnp.int32, (8, 128), 1)
    for p in range(pairs):
        wide_ref[p] = figure_ref[:, p * 128 : (p + 1) * 128].astype(F32)

    def slot(d, carry):
        k0 = index_ref[0, d]
        k1 = index_ref[1, d]
        a = half_of(wide_ref[k0 // 2], k0 % 2 != 0, lane)
        b = half_of(wide_ref[k1 // 2], k1 % 2 != 1, lane)
        out_ref[d] = jnp.where(lane < 64, a, b).astype(BF16)
        return carry

    lax.fori_loop(0, count, slot, 0, unroll=8)


def heights_out(index, mine, figure):
    bands = figure.shape[1] // 64
    return pl.pallas_call(
        heights_out_kernel,
        out_shape=jax.ShapeDtypeStruct((bands, 8, 128), BF16),
        grid_spec=pltpu.PrefetchScalarGridSpec(
            num_scalar_prefetch=2,
            grid=(1,),
            in_specs=[pl.BlockSpec((8, figure.shape[1]), lambda g, index, mine: (mine[0], 0))],
            out_specs=pl.BlockSpec((bands, 8, 128), lambda g, index, mine: (0, 0, 0)),
            scratch_shapes=[pltpu.VMEM((figure.shape[1] // 128, 8, 128), F32)],
        ),
        name="heights_out",
    )(index, mine, figure)


def phase_kernel(index_ref, tiles_ref, cos_ref, sin_ref):
    lane = lax.broadcasted_iota(jnp.int32, (8, 128), 1)
    pairs = cos_ref.shape[0]

    def pair(p, carry):
        s0, c0 = index_ref[0, 2 * p], index_ref[1, 2 * p]
        s1, c1 = index_ref[0, 2 * p + 1], index_ref[1, 2 * p + 1]
        a = half_of(tiles_ref[s0].astype(F32), c0 != 0, lane)
        b = half_of(tiles_ref[s1].astype(F32), c1 != 1, lane)
        phase = PHASE_FACTOR * jnp.where(lane < 64, a, b)
        cos_ref[p] = jnp.cos(phase)
        sin_ref[p] = jnp.sin(phase)
        return carry

    lax.fori_loop(0, pairs, pair, 0, unroll=2)


def phases(index, tiles):
    pairs = tiles.shape[0] // 2
    return pl.pallas_call(
        phase_kernel,
        out_shape=[jax.ShapeDtypeStruct((pairs, 8, 128), F32)] * 2,
        in_specs=[pl.BlockSpec(memory_space=pltpu.SMEM), whole()],
        out_specs=[whole(), whole()],
        name="phases",
    )(index, tiles)


def second_kernel(index_ref, mine_ref, got_ref, approach_ref, focus_ref, cos_ref, sin_ref, target_ref, out_ref,
                  x_ref, y_ref, g_ref, wp_ref, wf_ref):
    pairs = cos_ref.shape[0]
    rows = 64
    write_weights(approach_ref, wp_ref, True)
    write_weights(focus_ref, wf_ref, False)
    blank = jnp.zeros((rows, 256), BF16)
    for ref in (x_ref, y_ref, g_ref):
        ref[0:rows] = blank
        ref[(pairs + 1) * rows : (pairs + 2) * rows] = blank

    def fill(p, carry):
        to = pl.ds(pl.multiple_of((p + 1) * rows, 64), rows)
        for h in range(2):
            x = got_ref[:, 2 * p + h].astype(F32).reshape(rows, 128)
            x_ref[to, h * 128 : (h + 1) * 128] = x.astype(BF16)
        return carry

    lax.fori_loop(0, pairs, fill, 0, unroll=4)
    step = 4

    def mirror(q, carry):
        row = q * (step * rows)
        a2 = banded_rows(x_ref, wp_ref, row, step * rows, rows).astype(BF16).astype(F32)
        re = a2[:, 0:128].reshape(step, 8, 8, 128)
        im = a2[:, 128:256].reshape(step, 8, 8, 128)
        cos = cos_ref[pl.ds(q * step, step)][:, None]
        sin = sin_ref[pl.ds(q * step, step)][:, None]
        to = pl.ds(pl.multiple_of(row + rows, 64), step * rows)
        y_ref[to, 0:128] = (re * cos - im * sin).reshape(step * rows, 128).astype(BF16)
        y_ref[to, 128:256] = (re * sin + im * cos).reshape(step * rows, 128).astype(BF16)
        return carry

    lax.fori_loop(0, pairs // step, mirror, 0)

    def detect(q, carry):
        row = q * (step * rows)
        a4 = banded_rows(y_ref, wf_ref, row, step * rows, rows)
        re = a4[:, 0:128].reshape(step, 8, 8, 128)
        im = a4[:, 128:256].reshape(step, 8, 8, 128)
        power = jnp.sum(re * re + im * im, axis=1)
        to = pl.ds(pl.multiple_of(row + rows, 64), step * rows)
        for t in range(step):
            at = pl.ds(pl.multiple_of((q * step + t) * 128, 128), 128)
            left = (power[t] - target_ref[:, at].astype(F32))[None]
            to = pl.ds(pl.multiple_of(row + rows + t * rows, 64), rows)
            g_ref[to, 0:128] = (re[t] * left).reshape(rows, 128).astype(BF16)
            g_ref[to, 128:256] = (im[t] * left).reshape(rows, 128).astype(BF16)
        return carry

    lax.fori_loop(0, pairs // step, detect, 0)
    lane = lax.broadcasted_iota(jnp.int32, (8, 128), 1)
    out_ref[...] = jnp.zeros_like(out_ref)

    def adjoint(q, carry):
        row = q * (step * rows)
        g3 = banded_rows(g_ref, wf_ref, row, step * rows, rows, flip=True)
        own = pl.ds(pl.multiple_of(row + rows, 64), step * rows)
        re = y_ref[own, 0:128].astype(F32)
        im = y_ref[own, 128:256].astype(F32)
        terms = g3[:, 128:256] * re - g3[:, 0:128] * im
        sens = 2.0 * PHASE_FACTOR * jnp.sum(terms.reshape(step, 8, 8, 128), axis=1)
        for t in range(step):
            turned = pltpu.roll(sens[t], 64, 1)
            for h in range(2):
                j = (q * step + t) * 2 + h
                s, c = index_ref[0, j], index_ref[1, j]
                tile = jnp.where(c != h, turned, sens[t])
                out_ref[s] = jnp.where((lane < 64) == (c == 0), tile, out_ref[s].astype(F32)).astype(BF16)
        return carry

    lax.fori_loop(0, pairs // step, adjoint, 0)


def second_stage(index, mine, got, approach, focus, cos, sin, target):
    bands = got.shape[1]
    pairs = bands // 2
    keep = lambda *shape: pl.BlockSpec(shape, lambda g, index, mine: (0,) * len(shape))
    return pl.pallas_call(
        second_kernel,
        out_shape=jax.ShapeDtypeStruct((bands, 8, 128), BF16),
        grid_spec=pltpu.PrefetchScalarGridSpec(
            num_scalar_prefetch=2,
            grid=(1,),
            in_specs=[
                keep(*got.shape),
                keep(*approach.shape),
                keep(*focus.shape),
                keep(*cos.shape),
                keep(*sin.shape),
                pl.BlockSpec((8, target.shape[1]), lambda g, index, mine: (mine[0], 0)),
            ],
            out_specs=keep(bands, 8, 128),
            scratch_shapes=[pltpu.VMEM(((pairs + 2) * 64, 256), BF16)] * 3 + [pltpu.VMEM((3, 256, 256), BF16)] * 2,
        ),
        cost_estimate=pl.CostEstimate(flops=6 * 64 * pairs * 768 * 256, bytes_accessed=1 << 20, transcendentals=0),
        name="second",
    )(index, mine, got, approach, focus, cos, sin, target)


def collect_kernel(index_ref, tiles_ref, out_ref, sum_ref):
    lane = lax.broadcasted_iota(jnp.int32, (8, 128), 1)
    pairs = out_ref.shape[1] // 128
    sum_ref[...] = jnp.zeros_like(sum_ref)

    def slot(d, carry):
        x = tiles_ref[d].astype(F32)
        turned = pltpu.roll(x, 64, 1)
        for c in range(2):
            k = index_ref[c, d]
            tile = jnp.where(k % 2 != c, turned, x)
            sum_ref[k // 2] += jnp.where((lane < 64) == (k % 2 == 0), tile, 0.0)
        return carry

    lax.fori_loop(0, tiles_ref.shape[0], slot, 0, unroll=8)
    for p in range(pairs):
        out_ref[:, p * 128 : (p + 1) * 128] = sum_ref[p].astype(out_ref.dtype)


def collect(index, tiles, dtype):
    bands = tiles.shape[0]
    return pl.pallas_call(
        collect_kernel,
        out_shape=jax.ShapeDtypeStruct((8, bands * 64), dtype),
        in_specs=[pl.BlockSpec(memory_space=pltpu.SMEM), whole()],
        out_specs=whole(),
        scratch_shapes=[pltpu.VMEM((bands // 2 + 1, 8, 128), F32)],
        name="collect",
    )(index, tiles)


def shards(mode_field, figure, target, footprint, approach_tiles, focus_tiles):
    band = lax.axis_index("band")
    mine = lax.axis_index("mode").astype(jnp.int32).reshape(1)
    blocks = footprint.shape[1]
    source_band = footprint // blocks
    code = lax.broadcasted_iota(jnp.int32, footprint.shape, 1) * blocks + footprint % blocks
    here = source_band == band
    low = jnp.min(jnp.where(here, code, blocks * blocks), axis=1)
    high = jnp.max(jnp.where(here, code, -1), axis=1)
    send_index = jnp.stack([jnp.where(high >= 0, low % blocks, 0), jnp.maximum(high, 0) % blocks])
    add_index = jnp.stack([jnp.where(high >= 0, low % blocks, blocks), jnp.where(high > low, high % blocks, blocks)])
    my_band = lax.dynamic_index_in_dim(source_band, band, 0, keepdims=False)
    column = jnp.arange(blocks, dtype=jnp.int32)
    same = (my_band[:, None] == my_band[None, :]) & (column[None, :] < column[:, None])
    beam_index = jnp.stack([my_band, jnp.any(same, axis=1).astype(jnp.int32)])

    heights = heights_out(send_index, mine, figure)
    heights = lax.all_to_all(heights, "band", split_axis=0, concat_axis=0, tiled=True)
    out = first_stage(mode_field, approach_tiles)
    got = lax.all_to_all(out.reshape(-1, 8, 128), ("mode", "band"), split_axis=0, concat_axis=0, tiled=True)
    cos, sin = phases(beam_index, heights)
    got = got.reshape(out.shape)
    tiles = second_stage(beam_index, mine, got, approach_tiles, focus_tiles, cos, sin, target)
    tiles = lax.all_to_all(tiles, "band", split_axis=0, concat_axis=0, tiled=True)
    own = collect(add_index, tiles, BF16)
    return lax.all_gather(own, "mode", axis=0, tiled=True).astype(F32)


def solution(mesh):
    in_specs = (P("mode", "band", None, None), P("band", None), P("band", None), P(), P(), P())
    out_specs = P("band", None)
    return jax.shard_map(shards, mesh=mesh, in_specs=in_specs, out_specs=out_specs, check_vma=False)
```

time: 501 us -> 163 us (0.33)
  the two profiles are of different devices: /device:TPU:6 before, /device:TPU:1 now
where the time goes in v1:
time: 163 us; the launch traced here: 162 us
  waiting for transfers between devices  73.6 us (45%)
  starting transfers between devices  38.3 us (23%)
  Pallas kernels  27.4 us (17%)
  blocking collectives  16.7 us (10%)
  other arithmetic  3.95 us (2%)
  local copies, waits for them, and re-layouts  2.3 us (1%)
    all_to_all x1, waiting for transfers between devices, shards(): lax.all_to_all(out.reshape(-1, 8, 128), ('mode', 'band'), split_axis=0, c...  50.9 us
    all_to_all x1, starting transfers between devices, shards(): lax.all_to_all(heights, 'band', split_axis=0, concat_axis=0, tiled=True)  19.3 us
    all_gather x1, blocking collectives, shards(): return lax.all_gather(own, 'mode', axis=0, tiled=True).astype(F32)  16.7 us
    all_to_all x1, waiting for transfers between devices, shards(): lax.all_to_all(tiles, 'band', split_axis=0, concat_axis=0, tiled=True)  14.5 us
    all_to_all x1, starting transfers between devices, shards(): lax.all_to_all(out.reshape(-1, 8, 128), ('mode', 'band'), split_axis=0, c...  11.9 us
    pallas_call x1, Pallas kernels, second_stage(): pl.pallas_call(second_kernel, out_shape=jax.ShapeDtypeStruct((bands, 8, 1...  10.8 us
    all_to_all x1, waiting for transfers between devices, shards(): lax.all_to_all(heights, 'band', split_axis=0, concat_axis=0, tiled=True)  8.22 us
    all_to_all x1, starting transfers between devices, shards(): lax.all_to_all(tiles, 'band', split_axis=0, concat_axis=0, tiled=True)  7.12 us
  transfers between devices with their start and end apart: 3, of which 3 were waited for; matrix products, arithmetic and copies ran while one was open for 1% of the time, Pallas kernels for 6%

profile of v1, /device:TPU:1, one launch (start us, length us, event | category | flops | bytes accessed | tf_op | source)
XLA Modules:
  0.0 162.3 jit_solution(2669980071013711818)
XLA Ops:
  0.0 0.0 copy-start.3
  0.0 0.9 broadcast_compare_fusion
  0.9 0.0 copy-done.3
  0.9 0.1 select_reduce_fusion.1
  1.0 0.6 pad_add_fusion.2.index_ref
  1.6 3.4 %heights_out.1 = bf16[64,8,128]{2,1,0:T(8,128)(2,1)} custom-call(s32[2,64]{1,0:T(2,128)} %pad_add_fusion.2.index_ref, s32[1]{0:T(128)} %bitcast.4.mine_ref, bf16[64,4096]{1,0:T(8,128)(2,1)} %figure_ref.1), custom_call_target="tpu_custom_call" | custom-call | tf_op jit(solution)/shard_map/heights_out/pallas_call | solution.py:120
  5.0 19.3 %all-to-all-start.1 = ((bf16[64,8,128]{2,1,0:T(8,128)(2,1)}), bf16[64,8,128]{2,1,0:T(8,128)(2,1)S(1)}, u32[]{:S(2)}, u32[]{:S(2)}) async-start(bf16[64,8,128]{2,1,0:T(8,128)(2,1)} %heights_out.1), calls=%async_computation.1 | async-start | bytes 262144 | tf_op jit(solution)/shard_map/all_to_all | solution.py:310
  24.2 6.8 %first.1 = bf16[8,64,8,128]{3,2,1,0:T(8,128)(2,1)} custom-call(bf16[1,64,2,4096]{3,2,1,0:T(2,128)(2,1)} %field_ref.1, bf16[3,2,128,128]{3,2,1,0:T(8,128)(2,1)} %approach_ref.1), custom_call_target="tpu_custom_call" | custom-call | flops 805306368 | bytes 2097152 | tf_op jit(solution)/shard_map/first/pallas_call | solution.py:85
  31.1 8.2 %all-to-all-done.1.tiles_ref = bf16[64,8,128]{2,1,0:T(8,128)(2,1)S(1)} async-done(((bf16[64,8,128]{2,1,0:T(8,128)(2,1)}), bf16[64,8,128]{2,1,0:T(8,128)(2,1)S(1)}, u32[]{:S(2)}, u32[]{:S(2)}) %all-to-all-start.1) | async-done | bytes 131104 | tf_op jit(solution)/shard_map/all_to_all | solution.py:310
  39.3 0.6 copy-done.1
  39.9 11.9 %all-to-all-start = ((bf16[512,8,128]{2,1,0:T(8,128)(2,1)}), bf16[512,8,128]{2,1,0:T(8,128)(2,1)S(1)}, u32[]{:S(2)}, u32[]{:S(2)}) async-start(bf16[512,8,128]{2,1,0:T(8,128)(2,1)} %bitcast.24), calls=%async_computation | async-start | bytes 2097152 | tf_op jit(solution)/shard_map/all_to_all | solution.py:312
  51.9 0.2 fusion.3
  52.1 0.6 pad_add_fusion.1.index_ref
  52.6 3.6 %phases.1 = (f32[32,8,128]{2,1,0:T(8,128)}, f32[32,8,128]{2,1,0:T(8,128)}) custom-call(s32[2,64]{1,0:T(2,128)} %pad_add_fusion.1.index_ref, bf16[64,8,128]{2,1,0:T(8,128)(2,1)} %copy-done.1), custom_call_target="tpu_custom_call" | custom-call | tf_op jit(solution)/shard_map/phases/pallas_call | solution.py:153
  56.2 50.9 %all-to-all-done = bf16[512,8,128]{2,1,0:T(8,128)(2,1)S(1)} async-done(((bf16[512,8,128]{2,1,0:T(8,128)(2,1)}), bf16[512,8,128]{2,1,0:T(8,128)(2,1)S(1)}, u32[]{:S(2)}, u32[]{:S(2)}) %all-to-all-start) | async-done | bytes 1048608 | tf_op jit(solution)/shard_map/all_to_all | solution.py:312
  107.2 1.0 copy-done
  108.1 10.8 %second.1 = bf16[64,8,128]{2,1,0:T(8,128)(2,1)} custom-call(s32[2,64]{1,0:T(2,128)} %pad_add_fusion.1.index_ref, s32[1]{0:T(128)} %bitcast.4.mine_ref, bf16[8,64,8,128]{3,2,1,0:T(8,128)(2,1)} %bitcast.23, bf16[3,2,128,128]{3,2,1,0:T(8,128)(2,1)} %approach_ref.1, bf16[3,2,128,128]{3,2,1,0:T(8,128)(2,1)} %focus_ref.1, f32[32,8,128]{2,1,0:T(8,128)} %get-tuple-element.7.cos_ref, ...), custom_call_target="tpu_custom_call" | custom-call | flops 2415919104 | bytes 1048576 | tf_op jit(solution)/shard_map/second/pallas_call | solution.py:240
  118.9 7.1 %all-to-all-start.2 = ((bf16[64,8,128]{2,1,0:T(8,128)(2,1)}), bf16[64,8,128]{2,1,0:T(8,128)(2,1)S(1)}, u32[]{:S(2)}, u32[]{:S(2)}) async-start(bf16[64,8,128]{2,1,0:T(8,128)(2,1)} %second.1), calls=%async_computation.2 | async-start | bytes 262144 | tf_op jit(solution)/shard_map/all_to_all | solution.py:316
  126.1 0.6 pad_add_fusion.index_ref
  126.6 14.5 %all-to-all-done.2.tiles_ref = bf16[64,8,128]{2,1,0:T(8,128)(2,1)S(1)} async-done(((bf16[64,8,128]{2,1,0:T(8,128)(2,1)}), bf16[64,8,128]{2,1,0:T(8,128)(2,1)S(1)}, u32[]{:S(2)}, u32[]{:S(2)}) %all-to-all-start.2) | async-done | bytes 131104 | tf_op jit(solution)/shard_map/all_to_all | solution.py:316
  141.1 0.7 copy-done.2
  141.8 2.8 %collect.1 = bf16[8,4096]{1,0:T(8,128)(2,1)} custom-call(s32[2,64]{1,0:T(2,128)} %pad_add_fusion.index_ref, bf16[64,8,128]{2,1,0:T(8,128)(2,1)} %copy-done.2), custom_call_target="tpu_custom_call" | custom-call | tf_op jit(solution)/shard_map/collect/pallas_call | solution.py:283
  144.5 16.7 %all_gather.3 = bf16[64,4096]{1,0:T(8,128)(2,1)S(1)} all-gather(bf16[8,4096]{1,0:T(8,128)(2,1)} %collect.1), channel_id=1, replica_groups=mesh['mode'=8,'band'=64] {'mode'}, dimensions={0}, use_global_device_ids=true | all-gather | bytes 589824 | tf_op jit(solution)/shard_map/all_gather | solution.py:318
  161.3 1.0 convert_element_type.18
  (8 shorter events, 0.1 us)
Async XLA Ops:
  0.0 0.9 copy-start.3
  5.0 34.3 %all-to-all-start.1 = ((bf16[64,8,128]{2,1,0:T(8,128)(2,1)}), bf16[64,8,128]{2,1,0:T(8,128)(2,1)S(1)}, u32[]{:S(2)}, u32[]{:S(2)}) async-start(bf16[64,8,128]{2,1,0:T(8,128)(2,1)} %heights_out.1), calls=%async_computation.1 | async-start | bytes 262144 | tf_op jit(solution)/shard_map/all_to_all | solution.py:310
  39.3 0.6 copy-start.1
  39.9 67.2 %all-to-all-start = ((bf16[512,8,128]{2,1,0:T(8,128)(2,1)}), bf16[512,8,128]{2,1,0:T(8,128)(2,1)S(1)}, u32[]{:S(2)}, u32[]{:S(2)}) async-start(bf16[512,8,128]{2,1,0:T(8,128)(2,1)} %bitcast.24), calls=%async_computation | async-start | bytes 2097152 | tf_op jit(solution)/shard_map/all_to_all | solution.py:312
  107.2 1.0 copy-start
  118.9 22.2 %all-to-all-start.2 = ((bf16[64,8,128]{2,1,0:T(8,128)(2,1)}), bf16[64,8,128]{2,1,0:T(8,128)(2,1)S(1)}, u32[]{:S(2)}, u32[]{:S(2)}) async-start(bf16[64,8,128]{2,1,0:T(8,128)(2,1)} %second.1), calls=%async_computation.2 | async-start | bytes 262144 | tf_op jit(solution)/shard_map/all_to_all | solution.py:316
  141.1 0.7 copy-start.2

commit v2 on v1

--- a/solution.py
+++ b/solution.py
@@ -1,5 +1,3 @@
-import functools
-
 import jax
 import jax.numpy as jnp
 from jax import lax
@@ -7,9 +5,8 @@
 from jax.experimental.pallas import tpu as pltpu
 from jax.sharding import PartitionSpec as P
 
+
 TILE = 128
-HALF = 64
-MIRROR_TILE = 64
 PHASE_FACTOR = 4.0
 F32 = jnp.float32
 BF16 = jnp.bfloat16
@@ -93,53 +90,114 @@
     )(field, tiles)
 
 
-def half_of(x, want, lane):
+def half_of(x, want):
     return jnp.where(want, pltpu.roll(x, 64, 1), x)
 
 
-def heights_out_kernel(index_ref, mine_ref, figure_ref, out_ref, wide_ref):
-    count = out_ref.shape[0]
+def heights_out_kernel(index_ref, mine_ref, figure_ref, *refs):
+    outs, wide_ref = refs[:4], refs[4]
     pairs = figure_ref.shape[1] // 128
     lane = lax.broadcasted_iota(jnp.int32, (8, 128), 1)
     for p in range(pairs):
         wide_ref[p] = figure_ref[:, p * 128 : (p + 1) * 128].astype(F32)
 
-    def slot(d, carry):
-        k0 = index_ref[0, d]
-        k1 = index_ref[1, d]
-        a = half_of(wide_ref[k0 // 2], k0 % 2 != 0, lane)
-        b = half_of(wide_ref[k1 // 2], k1 % 2 != 1, lane)
-        out_ref[d] = jnp.where(lane < 64, a, b).astype(BF16)
-        return carry
-
-    lax.fori_loop(0, count, slot, 0, unroll=8)
+    z, y = mine_ref[1], mine_ref[2]
+    for low in range(4):
+
+        def slot(at, carry):
+            d = ((z + 4 * (at >> 2) + low + 11) & 15) * 4 + ((y + at + 3) & 3)
+            k0 = index_ref[0, d]
+            k1 = index_ref[1, d]
+            a = half_of(wide_ref[k0 >> 1], (k0 & 1) != 0)
+            b = half_of(wide_ref[k1 >> 1], (k1 & 1) != 1)
+            outs[low][at] = jnp.where(lane < 64, a, b).astype(BF16)
+            return carry
+
+        lax.fori_loop(0, 16, slot, 0, unroll=8)
 
 
 def heights_out(index, mine, figure):
-    bands = figure.shape[1] // 64
+    out = pl.BlockSpec((16, 8, 128), lambda g, index, mine: (0, 0, 0))
     return pl.pallas_call(
         heights_out_kernel,
-        out_shape=jax.ShapeDtypeStruct((bands, 8, 128), BF16),
+        out_shape=[jax.ShapeDtypeStruct((16, 8, 128), BF16)] * 4,
         grid_spec=pltpu.PrefetchScalarGridSpec(
             num_scalar_prefetch=2,
             grid=(1,),
             in_specs=[pl.BlockSpec((8, figure.shape[1]), lambda g, index, mine: (mine[0], 0))],
-            out_specs=pl.BlockSpec((bands, 8, 128), lambda g, index, mine: (0, 0, 0)),
+            out_specs=[out] * 4,
             scratch_shapes=[pltpu.VMEM((figure.shape[1] // 128, 8, 128), F32)],
         ),
         name="heights_out",
     )(index, mine, figure)
 
 
-def phase_kernel(index_ref, tiles_ref, cos_ref, sin_ref):
+def regroup_kernel(*refs):
+    for a in range(4):
+        for b in range(4):
+            refs[4 + b][4 * a : 4 * a + 4] = refs[a][4 * b : 4 * b + 4]
+
+
+def regroup(parts):
+    return pl.pallas_call(
+        regroup_kernel,
+        out_shape=[jax.ShapeDtypeStruct(parts[0].shape, BF16)] * 4,
+        in_specs=[whole()] * 4,
+        out_specs=[whole()] * 4,
+        name="regroup",
+    )(*parts)
+
+
+def regroup_last_kernel(*refs):
+    for b in range(4):
+        for a in range(4):
+            for c in range(4):
+                refs[4 + c][4 * a + b] = refs[b][4 * a + c]
+
+
+def regroup_last(parts):
+    return pl.pallas_call(
+        regroup_last_kernel,
+        out_shape=[jax.ShapeDtypeStruct(parts[0].shape, BF16)] * 4,
+        in_specs=[whole()] * 4,
+        out_specs=[whole()] * 4,
+        name="regroup_last",
+    )(*parts)
+
+
+DIGITS = (-1, 0, 1, 2)
+
+
+def moved(parts, bands, way):
+    spots = bands // 4
+
+    def target(b, step):
+        z, y = b // 4, b % 4
+        if way == "low":
+            return (z + step) % spots * 4 + y
+        if way == "high":
+            return (z + 4 * step) % spots * 4 + y
+        return z * 4 + (y + step) % 4
+
+    return [
+        part if step == 0 else lax.ppermute(part, "band", [(b, target(b, step)) for b in range(bands)])
+        for part, step in zip(parts, DIGITS)
+    ]
+
+
+def phase_kernel(index_ref, *refs):
+    cos_ref, sin_ref, wide_ref = refs[4:]
     lane = lax.broadcasted_iota(jnp.int32, (8, 128), 1)
     pairs = cos_ref.shape[0]
+    for a in range(4):
+        for b in range(16):
+            wide_ref[16 * a + b] = refs[a][b].astype(F32)
 
     def pair(p, carry):
         s0, c0 = index_ref[0, 2 * p], index_ref[1, 2 * p]
         s1, c1 = index_ref[0, 2 * p + 1], index_ref[1, 2 * p + 1]
-        a = half_of(tiles_ref[s0].astype(F32), c0 != 0, lane)
-        b = half_of(tiles_ref[s1].astype(F32), c1 != 1, lane)
+        a = half_of(wide_ref[s0], c0 != 0)
+        b = half_of(wide_ref[s1], c1 != 1)
         phase = PHASE_FACTOR * jnp.where(lane < 64, a, b)
         cos_ref[p] = jnp.cos(phase)
         sin_ref[p] = jnp.sin(phase)
@@ -148,15 +206,15 @@
     lax.fori_loop(0, pairs, pair, 0, unroll=2)
 
 
-def phases(index, tiles):
-    pairs = tiles.shape[0] // 2
+def phases(index, parts, pairs):
     return pl.pallas_call(
         phase_kernel,
         out_shape=[jax.ShapeDtypeStruct((pairs, 8, 128), F32)] * 2,
-        in_specs=[pl.BlockSpec(memory_space=pltpu.SMEM), whole()],
+        in_specs=[pl.BlockSpec(memory_space=pltpu.SMEM)] + [whole()] * 4,
         out_specs=[whole(), whole()],
+        scratch_shapes=[pltpu.VMEM((64, 8, 128), F32)],
         name="phases",
-    )(index, tiles)
+    )(index, *parts)
 
 
 def second_kernel(index_ref, mine_ref, got_ref, approach_ref, focus_ref, cos_ref, sin_ref, target_ref, out_ref,
@@ -269,8 +327,8 @@
         turned = pltpu.roll(x, 64, 1)
         for c in range(2):
             k = index_ref[c, d]
-            tile = jnp.where(k % 2 != c, turned, x)
-            sum_ref[k // 2] += jnp.where((lane < 64) == (k % 2 == 0), tile, 0.0)
+            tile = jnp.where((k & 1) != c, turned, x)
+            sum_ref[k >> 1] += jnp.where((lane < 64) == ((k & 1) == 0), tile, 0.0)
         return carry
 
     lax.fori_loop(0, tiles_ref.shape[0], slot, 0, unroll=8)
@@ -291,27 +349,36 @@
 
 
 def shards(mode_field, figure, target, footprint, approach_tiles, focus_tiles):
-    band = lax.axis_index("band")
-    mine = lax.axis_index("mode").astype(jnp.int32).reshape(1)
-    blocks = footprint.shape[1]
-    source_band = footprint // blocks
-    code = lax.broadcasted_iota(jnp.int32, footprint.shape, 1) * blocks + footprint % blocks
+    band = lax.axis_index("band").astype(jnp.int32)
+    z, y = band >> 2, band & 3
+    mine = jnp.stack([lax.axis_index("mode").astype(jnp.int32), z, y])
+    bands, blocks = footprint.shape
+    out = first_stage(mode_field, approach_tiles)
+    got = lax.all_to_all(out.reshape(-1, 8, 128), ("mode", "band"), split_axis=0, concat_axis=0, tiled=True)
+    got = got.reshape(out.shape)
+    source_band = lax.div(footprint, blocks)
+    code = lax.broadcasted_iota(jnp.int32, footprint.shape, 1) * blocks + lax.rem(footprint, blocks)
     here = source_band == band
     low = jnp.min(jnp.where(here, code, blocks * blocks), axis=1)
     high = jnp.max(jnp.where(here, code, -1), axis=1)
-    send_index = jnp.stack([jnp.where(high >= 0, low % blocks, 0), jnp.maximum(high, 0) % blocks])
-    add_index = jnp.stack([jnp.where(high >= 0, low % blocks, blocks), jnp.where(high > low, high % blocks, blocks)])
+    add_index = jnp.stack([jnp.where(high >= 0, low & (blocks - 1), blocks), jnp.where(high > low, high & (blocks - 1), blocks)])
     my_band = lax.dynamic_index_in_dim(source_band, band, 0, keepdims=False)
     column = jnp.arange(blocks, dtype=jnp.int32)
     same = (my_band[:, None] == my_band[None, :]) & (column[None, :] < column[:, None])
-    beam_index = jnp.stack([my_band, jnp.any(same, axis=1).astype(jnp.int32)])
-
-    heights = heights_out(send_index, mine, figure)
-    heights = lax.all_to_all(heights, "band", split_axis=0, concat_axis=0, tiled=True)
-    out = first_stage(mode_field, approach_tiles)
-    got = lax.all_to_all(out.reshape(-1, 8, 128), ("mode", "band"), split_axis=0, concat_axis=0, tiled=True)
-    cos, sin = phases(beam_index, heights)
-    got = got.reshape(out.shape)
+    my_slot = jnp.any(same, axis=1).astype(jnp.int32)
+    beam_index = jnp.stack([my_band, my_slot])
+    dz = z - (my_band >> 2)
+    step_low = (dz + 1) & 3
+    step_high = (((dz + 1 - step_low) >> 2) + 1) & 3
+    step_y = (y - my_band + 1) & 3
+    read_index = jnp.stack([16 * step_y + 4 * step_low + step_high, my_slot])
+    parts = heights_out(add_index & (blocks - 1), mine, figure)
+    parts = moved(parts, bands, "low")
+    parts = regroup(parts)
+    parts = moved(parts, bands, "high")
+    parts = regroup_last(parts)
+    parts = moved(parts, bands, "y")
+    cos, sin = phases(read_index, parts, bands // 2)
     tiles = second_stage(beam_index, mine, got, approach_tiles, focus_tiles, cos, sin, target)
     tiles = lax.all_to_all(tiles, "band", split_axis=0, concat_axis=0, tiled=True)
     own = collect(add_index, tiles, BF16)

time: 163 us -> 187 us (1.15)
  waiting for transfers between devices: 73.6 us -> 40.8 us
  blocking collectives: 16.7 us -> 45.6 us
  starting transfers between devices: 38.3 us -> 63.4 us
  Pallas kernels: 27.4 us -> 30 us
    all_to_all x1, waiting for transfers between devices: 50.9 us -> 0.01 us  [shards(): lax.all_to_all(out.reshape(-1, 8, 128), ('mode', 'band'), split_axis=0, c...]
    ppermute x0 -> x9, waiting for transfers between devices: none -> 40.8 us  [moved(): lax.ppermute(part, 'band', [(b, target(b, step)) for b in range(bands)])]
    ppermute x0 -> x9, starting transfers between devices: none -> 39.1 us  [moved(): lax.ppermute(part, 'band', [(b, target(b, step)) for b in range(bands)])]
    all_to_all x0 -> x1, blocking collectives: none -> 27.2 us  [shards(): lax.all_to_all(tiles, 'band', split_axis=0, concat_axis=0, tiled=True)]
    all_to_all x2 -> x0, starting transfers between devices: 26.4 us -> none  [the longest x1 19.3 us: shards(): lax.all_to_all(heights, 'band', split_axis=0, concat_axis=0, tiled=True)]
    all_to_all x2 -> x0, waiting for transfers between devices: 22.7 us -> none  [the longest x1 14.5 us: shards(): lax.all_to_all(tiles, 'band', split_axis=0, concat_axis=0, tiled=True)]
    all_to_all x1, starting transfers between devices: 11.9 us -> 24.3 us  [shards(): lax.all_to_all(out.reshape(-1, 8, 128), ('mode', 'band'), split_axis=0, c...]
    pallas_call x1 -> x3, Pallas kernels: 3.37 us -> 6.09 us  [the longest x1 3.13 us: heights_out(): pl.pallas_call(heights_out_kernel, out_shape=[jax.ShapeDtypeStruct((16, 8...]
  transfers between devices with their start and end apart: 3 -> 10, of which waited for: 3 -> 5; matrix products, arithmetic and copies ran while one was open for 1% -> 1% of each run, Pallas kernels for 6% -> 5%
where the time goes in v2:
time: 187 us; the launch traced here: 186 us
  starting transfers between devices  63.4 us (34%)
  blocking collectives  45.6 us (24%)
  waiting for transfers between devices  40.8 us (22%)
  Pallas kernels  30 us (16%)
  other arithmetic  3.17 us (2%)
  local copies, waits for them, and re-layouts  2.83 us (2%)
    ppermute x9, waiting for transfers between devices, moved(): lax.ppermute(part, 'band', [(b, target(b, step)) for b in range(bands)])  40.8 us
    ppermute x9, starting transfers between devices, moved(): lax.ppermute(part, 'band', [(b, target(b, step)) for b in range(bands)])  39.1 us
    all_to_all x1, blocking collectives, shards(): lax.all_to_all(tiles, 'band', split_axis=0, concat_axis=0, tiled=True)  27.2 us
    all_to_all x1, starting transfers between devices, shards(): lax.all_to_all(out.reshape(-1, 8, 128), ('mode', 'band'), split_axis=0, c...  24.3 us
    all_gather x1, blocking collectives, shards(): return lax.all_gather(own, 'mode', axis=0, tiled=True).astype(F32)  18.4 us
    pallas_call x1, Pallas kernels, second_stage(): pl.pallas_call(second_kernel, out_shape=jax.ShapeDtypeStruct((bands, 8, 1...  10.8 us
    pallas_call x1, Pallas kernels, first_stage(): pl.pallas_call(first_kernel, out_shape=jax.ShapeDtypeStruct((8, length //...  6.83 us
  transfers between devices with their start and end apart: 10, of which 5 were waited for; matrix products, arithmetic and copies ran while one was open for 1% of the time, Pallas kernels for 5%

profile of v2, /device:TPU:1, one launch (start us, length us, event | category | flops | bytes accessed | tf_op | source)
XLA Modules:
  0.0 186.0 jit_solution(6759282489958748431)
XLA Ops:
  0.0 6.8 %first.1 = bf16[8,64,8,128]{3,2,1,0:T(8,128)(2,1)} custom-call(bf16[1,64,2,4096]{3,2,1,0:T(2,128)(2,1)} %field_ref.1, bf16[3,2,128,128]{3,2,1,0:T(8,128)(2,1)} %approach_ref.1), custom_call_target="tpu_custom_call" | custom-call | flops 805306368 | bytes 2097152 | tf_op jit(solution)/shard_map/first/pallas_call | solution.py:82
  6.8 24.3 %all-to-all-start = ((bf16[512,8,128]{2,1,0:T(8,128)(2,1)}), bf16[512,8,128]{2,1,0:T(8,128)(2,1)S(1)}, u32[]{:S(2)}, u32[]{:S(2)}) async-start(bf16[512,8,128]{2,1,0:T(8,128)(2,1)} %bitcast.13), calls=%async_computation | async-start | bytes 2097152 | tf_op jit(solution)/shard_map/all_to_all | solution.py:357
  32.5 3.1 %heights_out.1 = (bf16[16,8,128]{2,1,0:T(8,128)(2,1)}, bf16[16,8,128]{2,1,0:T(8,128)(2,1)}, bf16[16,8,128]{2,1,0:T(8,128)(2,1)}, bf16[16,8,128]{2,1,0:T(8,128)(2,1)}) custom-call(s32[2,64]{1,0:T(2,128)} %get-tuple-element.38.index_ref, s32[3]{0:T(128)} %pad_add_fusion.3.mine_ref, bf16[64,4096]{1,0:T(8,128)(2,1)} %figure_ref.1), custom_call_target="tpu_custom_call" | custom-call | tf_op jit(solution)/shard_map/heights_out/pallas_call | solution.py:121
  35.6 8.4 %collective-permute-start = (bf16[16,8,128]{2,1,0:T(8,128)(2,1)}, bf16[16,8,128]{2,1,0:T(8,128)(2,1)S(1)}, u32[]{:S(2)}, u32[]{:S(2)}) collective-permute-start(bf16[16,8,128]{2,1,0:T(8,128)(2,1)} %get-tuple-element.19), channel_id=1, source_target_pairs={{0,60},{1,61},{2,62},{3,63},{4,0},{5,1},{6,2},{7,3},{8,4},{9,5},{1... | collective-permute-start | bytes 98312 | tf_op jit(solution)/shard_map/ppermute | solution.py:183
  44.0 1.9 %collective-permute-start.1 = (bf16[16,8,128]{2,1,0:T(8,128)(2,1)}, bf16[16,8,128]{2,1,0:T(8,128)(2,1)S(1)}, u32[]{:S(2)}, u32[]{:S(2)}) collective-permute-start(bf16[16,8,128]{2,1,0:T(8,128)(2,1)} %get-tuple-element.21), channel_id=1, source_target_pairs={{0,4},{1,5},{2,6},{3,7},{4,8},{5,9},{6,10},{7,11},{8,12},{9,13},{1... | collective-permute-start | bytes 98312 | tf_op jit(solution)/shard_map/ppermute | solution.py:183
  45.9 1.9 %collective-permute-start.2 = (bf16[16,8,128]{2,1,0:T(8,128)(2,1)}, bf16[16,8,128]{2,1,0:T(8,128)(2,1)S(1)}, u32[]{:S(2)}, u32[]{:S(2)}) collective-permute-start(bf16[16,8,128]{2,1,0:T(8,128)(2,1)} %get-tuple-element.22), channel_id=1, source_target_pairs={{0,8},{1,9},{2,10},{3,11},{4,12},{5,13},{6,14},{7,15},{8,16},{9,17... | collective-permute-start | bytes 98312 | tf_op jit(solution)/shard_map/ppermute | solution.py:183
  48.0 25.2 %collective-permute-done.refs_0_ = bf16[16,8,128]{2,1,0:T(8,128)(2,1)S(1)} collective-permute-done((bf16[16,8,128]{2,1,0:T(8,128)(2,1)}, bf16[16,8,128]{2,1,0:T(8,128)(2,1)S(1)}, u32[]{:S(2)}, u32[]{:S(2)}) %collective-permute-start) | collective-permute-done | bytes 32800 | tf_op jit(solution)/shard_map/ppermute | solution.py:183
  73.2 5.3 %collective-permute-done.1.refs_2_ = bf16[16,8,128]{2,1,0:T(8,128)(2,1)S(1)} collective-permute-done((bf16[16,8,128]{2,1,0:T(8,128)(2,1)}, bf16[16,8,128]{2,1,0:T(8,128)(2,1)S(1)}, u32[]{:S(2)}, u32[]{:S(2)}) %collective-permute-start.1) | collective-permute-done | bytes 32800 | tf_op jit(solution)/shard_map/ppermute | solution.py:183
  78.5 2.4 %collective-permute-done.2.refs_3_ = bf16[16,8,128]{2,1,0:T(8,128)(2,1)S(1)} collective-permute-done((bf16[16,8,128]{2,1,0:T(8,128)(2,1)}, bf16[16,8,128]{2,1,0:T(8,128)(2,1)S(1)}, u32[]{:S(2)}, u32[]{:S(2)}) %collective-permute-start.2) | collective-permute-done | bytes 32800 | tf_op jit(solution)/shard_map/ppermute | solution.py:183
  81.5 1.5 regroup.1
  83.0 6.5 %collective-permute-start.3 = (bf16[16,8,128]{2,1,0:T(8,128)(2,1)}, bf16[16,8,128]{2,1,0:T(8,128)(2,1)S(1)}, u32[]{:S(2)}, u32[]{:S(2)}) collective-permute-start(bf16[16,8,128]{2,1,0:T(8,128)(2,1)} %get-tuple-element.23), channel_id=1, source_target_pairs={{0,48},{1,49},{2,50},{3,51},{4,52},{5,53},{6,54},{7,55},{8,56},{9,... | collective-permute-start | bytes 98312 | tf_op jit(solution)/shard_map/ppermute | solution.py:183
  89.5 2.7 %collective-permute-start.4 = (bf16[16,8,128]{2,1,0:T(8,128)(2,1)}, bf16[16,8,128]{2,1,0:T(8,128)(2,1)S(1)}, u32[]{:S(2)}, u32[]{:S(2)}) collective-permute-start(bf16[16,8,128]{2,1,0:T(8,128)(2,1)} %get-tuple-element.25), channel_id=1, source_target_pairs={{0,16},{1,17},{2,18},{3,19},{4,20},{5,21},{6,22},{7,23},{8,24},{9,... | collective-permute-start | bytes 98312 | tf_op jit(solution)/shard_map/ppermute | solution.py:183
  92.2 7.7 %collective-permute-start.5 = (bf16[16,8,128]{2,1,0:T(8,128)(2,1)}, bf16[16,8,128]{2,1,0:T(8,128)(2,1)S(1)}, u32[]{:S(2)}, u32[]{:S(2)}) collective-permute-start(bf16[16,8,128]{2,1,0:T(8,128)(2,1)} %get-tuple-element.26), channel_id=1, source_target_pairs={{0,32},{1,33},{2,34},{3,35},{4,36},{5,37},{6,38},{7,39},{8,40},{9,... | collective-permute-start | bytes 98312 | tf_op jit(solution)/shard_map/ppermute | solution.py:183
  100.0 5.8 %collective-permute-done.5.refs_3_ = bf16[16,8,128]{2,1,0:T(8,128)(2,1)S(1)} collective-permute-done((bf16[16,8,128]{2,1,0:T(8,128)(2,1)}, bf16[16,8,128]{2,1,0:T(8,128)(2,1)S(1)}, u32[]{:S(2)}, u32[]{:S(2)}) %collective-permute-start.5) | collective-permute-done | bytes 32800 | tf_op jit(solution)/shard_map/ppermute | solution.py:183
  106.4 1.5 regroup_last.1
  107.9 4.5 %collective-permute-start.6 = (bf16[16,8,128]{2,1,0:T(8,128)(2,1)}, bf16[16,8,128]{2,1,0:T(8,128)(2,1)S(1)}, u32[]{:S(2)}, u32[]{:S(2)}) collective-permute-start(bf16[16,8,128]{2,1,0:T(8,128)(2,1)} %get-tuple-element.27), channel_id=1, source_target_pairs={{0,3},{1,0},{2,1},{3,2},{4,7},{5,4},{6,5},{7,6},{8,11},{9,8},{10,9... | collective-permute-start | bytes 98312 | tf_op jit(solution)/shard_map/ppermute | solution.py:183
  112.4 1.9 %collective-permute-start.7 = (bf16[16,8,128]{2,1,0:T(8,128)(2,1)}, bf16[16,8,128]{2,1,0:T(8,128)(2,1)S(1)}, u32[]{:S(2)}, u32[]{:S(2)}) collective-permute-start(bf16[16,8,128]{2,1,0:T(8,128)(2,1)} %get-tuple-element.29), channel_id=1, source_target_pairs={{0,1},{1,2},{2,3},{3,0},{4,5},{5,6},{6,7},{7,4},{8,9},{9,10},{10,1... | collective-permute-start | bytes 98312 | tf_op jit(solution)/shard_map/ppermute | solution.py:183
  114.3 3.6 %collective-permute-start.8 = (bf16[16,8,128]{2,1,0:T(8,128)(2,1)}, bf16[16,8,128]{2,1,0:T(8,128)(2,1)S(1)}, u32[]{:S(2)}, u32[]{:S(2)}) collective-permute-start(bf16[16,8,128]{2,1,0:T(8,128)(2,1)} %get-tuple-element.30), channel_id=1, source_target_pairs={{0,2},{1,3},{2,0},{3,1},{4,6},{5,7},{6,4},{7,5},{8,10},{9,11},{10,... | collective-permute-start | bytes 98312 | tf_op jit(solution)/shard_map/ppermute | solution.py:183
  118.5 2.2 %collective-permute-done.8.refs_3_ = bf16[16,8,128]{2,1,0:T(8,128)(2,1)S(1)} collective-permute-done((bf16[16,8,128]{2,1,0:T(8,128)(2,1)}, bf16[16,8,128]{2,1,0:T(8,128)(2,1)S(1)}, u32[]{:S(2)}, u32[]{:S(2)}) %collective-permute-start.8) | collective-permute-done | bytes 32800 | tf_op jit(solution)/shard_map/ppermute | solution.py:183
  121.3 3.5 %phases.1 = (f32[32,8,128]{2,1,0:T(8,128)}, f32[32,8,128]{2,1,0:T(8,128)}) custom-call(s32[2,64]{1,0:T(2,128)} %get-tuple-element.42.index_ref, bf16[16,8,128]{2,1,0:T(8,128)(2,1)} %copy-done.5, bf16[16,8,128]{2,1,0:T(8,128)(2,1)} %get-tuple-element.28.refs_1_, bf16[16,8,128]{2,1,0:T(8,128)(2,1)} %copy-done.7, bf16[16,8,128]{2,1,0:T(8,128)(2,1)} %copy-done.9), custom_call_target="tpu_custom_call" | custom-call | tf_op jit(solution)/shard_map/phases/pallas_call | solution.py:210
  125.8 10.8 %second.1 = bf16[64,8,128]{2,1,0:T(8,128)(2,1)} custom-call(s32[2,64]{1,0:T(2,128)} %get-tuple-element.43.index_ref, s32[3]{0:T(128)} %pad_add_fusion.3.mine_ref, bf16[8,64,8,128]{3,2,1,0:T(8,128)(2,1)} %bitcast.12, bf16[3,2,128,128]{3,2,1,0:T(8,128)(2,1)} %approach_ref.1, bf16[3,2,128,128]{3,2,1,0:T(8,128)(2,1)} %focus_ref.1, ...), custom_call_target="tpu_custom_call" | custom-call | flops 2415919104 | bytes 1048576 | tf_op jit(solution)/shard_map/second/pallas_call | solution.py:298
  136.6 27.2 %all_to_all.10.tiles_ref = bf16[64,8,128]{2,1,0:T(8,128)(2,1)} all-to-all(bf16[64,8,128]{2,1,0:T(8,128)(2,1)} %second.1), channel_id=1, replica_groups=mesh['mode'=8,'band'=64] {'band'}, dimensions={0} | all-to-all | bytes 262144 | tf_op jit(solution)/shard_map/all_to_all | solution.py:383
  163.8 2.8 %collect.1 = bf16[8,4096]{1,0:T(8,128)(2,1)} custom-call(s32[2,64]{1,0:T(2,128)} %get-tuple-element.39.index_ref, bf16[64,8,128]{2,1,0:T(8,128)(2,1)} %all_to_all.10.tiles_ref), custom_call_target="tpu_custom_call" | custom-call | tf_op jit(solution)/shard_map/collect/pallas_call | solution.py:341
  166.6 18.4 %all_gather.3 = bf16[64,4096]{1,0:T(8,128)(2,1)S(1)} all-gather(bf16[8,4096]{1,0:T(8,128)(2,1)} %collect.1), channel_id=1, replica_groups=mesh['mode'=8,'band'=64] {'mode'}, dimensions={0}, use_global_device_ids=true | all-gather | bytes 589824 | tf_op jit(solution)/shard_map/all_gather | solution.py:385
  (37 shorter events, 6.0 us)
Async XLA Ops:
  6.8 24.9 %copy-start.1 = (s32[64,64]{1,0:T(8,128)S(1)}, s32[64,64]{1,0:T(8,128)}, u32[]{:S(2)}) copy-start(s32[64,64]{1,0:T(8,128)} %param.9) | copy-start | bytes 49156
  6.8 118.0 %all-to-all-start = ((bf16[512,8,128]{2,1,0:T(8,128)(2,1)}), bf16[512,8,128]{2,1,0:T(8,128)(2,1)S(1)}, u32[]{:S(2)}, u32[]{:S(2)}) async-start(bf16[512,8,128]{2,1,0:T(8,128)(2,1)} %bitcast.13), calls=%async_computation | async-start | bytes 2097152 | tf_op jit(solution)/shard_map/all_to_all | solution.py:357
  35.6 37.6 %collective-permute-start = (bf16[16,8,128]{2,1,0:T(8,128)(2,1)}, bf16[16,8,128]{2,1,0:T(8,128)(2,1)S(1)}, u32[]{:S(2)}, u32[]{:S(2)}) collective-permute-start(bf16[16,8,128]{2,1,0:T(8,128)(2,1)} %get-tuple-element.19), channel_id=1, source_target_pairs={{0,60},{1,61},{2,62},{3,63},{4,0},{5,1},{6,2},{7,3},{8,4},{9,5},{1... | collective-permute-start | bytes 98312 | tf_op jit(solution)/shard_map/ppermute | solution.py:183
  44.0 34.5 %collective-permute-start.1 = (bf16[16,8,128]{2,1,0:T(8,128)(2,1)}, bf16[16,8,128]{2,1,0:T(8,128)(2,1)S(1)}, u32[]{:S(2)}, u32[]{:S(2)}) collective-permute-start(bf16[16,8,128]{2,1,0:T(8,128)(2,1)} %get-tuple-element.21), channel_id=1, source_target_pairs={{0,4},{1,5},{2,6},{3,7},{4,8},{5,9},{6,10},{7,11},{8,12},{9,13},{1... | collective-permute-start | bytes 98312 | tf_op jit(solution)/shard_map/ppermute | solution.py:183
  45.9 35.0 %collective-permute-start.2 = (bf16[16,8,128]{2,1,0:T(8,128)(2,1)}, bf16[16,8,128]{2,1,0:T(8,128)(2,1)S(1)}, u32[]{:S(2)}, u32[]{:S(2)}) collective-permute-start(bf16[16,8,128]{2,1,0:T(8,128)(2,1)} %get-tuple-element.22), channel_id=1, source_target_pairs={{0,8},{1,9},{2,10},{3,11},{4,12},{5,13},{6,14},{7,15},{8,16},{9,17... | collective-permute-start | bytes 98312 | tf_op jit(solution)/shard_map/ppermute | solution.py:183
  73.2 7.7 %copy-start.2 = (bf16[16,8,128]{2,1,0:T(8,128)(2,1)}, bf16[16,8,128]{2,1,0:T(8,128)(2,1)S(1)}, u32[]{:S(2)}) copy-start(bf16[16,8,128]{2,1,0:T(8,128)(2,1)S(1)} %collective-permute-done.refs_0_) | copy-start | bytes 98308
  78.5 2.4 %copy-start.3 = (bf16[16,8,128]{2,1,0:T(8,128)(2,1)}, bf16[16,8,128]{2,1,0:T(8,128)(2,1)S(1)}, u32[]{:S(2)}) copy-start(bf16[16,8,128]{2,1,0:T(8,128)(2,1)S(1)} %collective-permute-done.1.refs_2_) | copy-start | bytes 98308
  80.9 0.6 copy-start.4
  83.0 16.9 %collective-permute-start.3 = (bf16[16,8,128]{2,1,0:T(8,128)(2,1)}, bf16[16,8,128]{2,1,0:T(8,128)(2,1)S(1)}, u32[]{:S(2)}, u32[]{:S(2)}) collective-permute-start(bf16[16,8,128]{2,1,0:T(8,128)(2,1)} %get-tuple-element.23), channel_id=1, source_target_pairs={{0,48},{1,49},{2,50},{3,51},{4,52},{5,53},{6,54},{7,55},{8,56},{9,... | collective-permute-start | bytes 98312 | tf_op jit(solution)/shard_map/ppermute | solution.py:183
  89.5 10.4 %collective-permute-start.4 = (bf16[16,8,128]{2,1,0:T(8,128)(2,1)}, bf16[16,8,128]{2,1,0:T(8,128)(2,1)S(1)}, u32[]{:S(2)}, u32[]{:S(2)}) collective-permute-start(bf16[16,8,128]{2,1,0:T(8,128)(2,1)} %get-tuple-element.25), channel_id=1, source_target_pairs={{0,16},{1,17},{2,18},{3,19},{4,20},{5,21},{6,22},{7,23},{8,24},{9,... | collective-permute-start | bytes 98312 | tf_op jit(solution)/shard_map/ppermute | solution.py:183
  92.2 13.6 %collective-permute-start.5 = (bf16[16,8,128]{2,1,0:T(8,128)(2,1)}, bf16[16,8,128]{2,1,0:T(8,128)(2,1)S(1)}, u32[]{:S(2)}, u32[]{:S(2)}) collective-permute-start(bf16[16,8,128]{2,1,0:T(8,128)(2,1)} %get-tuple-element.26), channel_id=1, source_target_pairs={{0,32},{1,33},{2,34},{3,35},{4,36},{5,37},{6,38},{7,39},{8,40},{9,... | collective-permute-start | bytes 98312 | tf_op jit(solution)/shard_map/ppermute | solution.py:183
  99.9 5.8 %copy-start.6 = (bf16[16,8,128]{2,1,0:T(8,128)(2,1)}, bf16[16,8,128]{2,1,0:T(8,128)(2,1)S(1)}, u32[]{:S(2)}) copy-start(bf16[16,8,128]{2,1,0:T(8,128)(2,1)S(1)} %collective-permute-done.3.refs_0_) | copy-start | bytes 98308
  100.0 5.8 %copy-start.8 = (bf16[16,8,128]{2,1,0:T(8,128)(2,1)}, bf16[16,8,128]{2,1,0:T(8,128)(2,1)S(1)}, u32[]{:S(2)}) copy-start(bf16[16,8,128]{2,1,0:T(8,128)(2,1)S(1)} %collective-permute-done.4.refs_2_) | copy-start | bytes 98308
  105.8 0.6 copy-start.10
  107.9 10.7 %collective-permute-start.6 = (bf16[16,8,128]{2,1,0:T(8,128)(2,1)}, bf16[16,8,128]{2,1,0:T(8,128)(2,1)S(1)}, u32[]{:S(2)}, u32[]{:S(2)}) collective-permute-start(bf16[16,8,128]{2,1,0:T(8,128)(2,1)} %get-tuple-element.27), channel_id=1, source_target_pairs={{0,3},{1,0},{2,1},{3,2},{4,7},{5,4},{6,5},{7,6},{8,11},{9,8},{10,9... | collective-permute-start | bytes 98312 | tf_op jit(solution)/shard_map/ppermute | solution.py:183
  112.4 6.1 %collective-permute-start.7 = (bf16[16,8,128]{2,1,0:T(8,128)(2,1)}, bf16[16,8,128]{2,1,0:T(8,128)(2,1)S(1)}, u32[]{:S(2)}, u32[]{:S(2)}) collective-permute-start(bf16[16,8,128]{2,1,0:T(8,128)(2,1)} %get-tuple-element.29), channel_id=1, source_target_pairs={{0,1},{1,2},{2,3},{3,0},{4,5},{5,6},{6,7},{7,4},{8,9},{9,10},{10,1... | collective-permute-start | bytes 98312 | tf_op jit(solution)/shard_map/ppermute | solution.py:183
  114.3 6.4 %collective-permute-start.8 = (bf16[16,8,128]{2,1,0:T(8,128)(2,1)}, bf16[16,8,128]{2,1,0:T(8,128)(2,1)S(1)}, u32[]{:S(2)}, u32[]{:S(2)}) collective-permute-start(bf16[16,8,128]{2,1,0:T(8,128)(2,1)} %get-tuple-element.30), channel_id=1, source_target_pairs={{0,2},{1,3},{2,0},{3,1},{4,6},{5,7},{6,4},{7,5},{8,10},{9,11},{10,... | collective-permute-start | bytes 98312 | tf_op jit(solution)/shard_map/ppermute | solution.py:183
  118.5 2.2 %copy-start.5 = (bf16[16,8,128]{2,1,0:T(8,128)(2,1)}, bf16[16,8,128]{2,1,0:T(8,128)(2,1)S(1)}, u32[]{:S(2)}) copy-start(bf16[16,8,128]{2,1,0:T(8,128)(2,1)S(1)} %collective-permute-done.6.refs_0_) | copy-start | bytes 98308
  118.5 2.2 %copy-start.7 = (bf16[16,8,128]{2,1,0:T(8,128)(2,1)}, bf16[16,8,128]{2,1,0:T(8,128)(2,1)S(1)}, u32[]{:S(2)}) copy-start(bf16[16,8,128]{2,1,0:T(8,128)(2,1)S(1)} %collective-permute-done.7.refs_2_) | copy-start | bytes 98308
  120.7 0.6 copy-start.9
  124.8 1.0 copy-start

commit v3 on v2

--- a/solution.py
+++ b/solution.py
@@ -44,23 +44,20 @@
     return total
 
 
-def first_kernel(field_ref, tiles_ref, out_ref, x_ref, w_ref):
-    rows = field_ref.shape[1]
-    count_tiles = field_ref.shape[3] // TILE
+def first_kernel(field_ref, tiles_ref, out_ref, wide_ref, x_ref, w_ref):
+    rows = x_ref.shape[0] // (field_ref.shape[0] // 128 + 2)
+    count_tiles = field_ref.shape[0] // 128
     write_weights(tiles_ref, w_ref, False)
     x_ref[0:rows] = jnp.zeros((rows, 256), BF16)
     x_ref[(count_tiles + 1) * rows : (count_tiles + 2) * rows] = jnp.zeros((rows, 256), BF16)
-
-    def fill(j, carry):
-        at = pl.ds(pl.multiple_of(j * TILE, TILE), TILE)
-        to = pl.ds(pl.multiple_of((j + 1) * rows, 64), rows)
-        both = field_ref[0, :, :, at].astype(F32)
-        x_ref[to, 0:128] = both[:, 0].astype(BF16)
-        x_ref[to, 128:256] = both[:, 1].astype(BF16)
-        return carry
-
-    lax.fori_loop(0, count_tiles, fill, 0, unroll=4)
-    step = 4
+    for u in range(rows):
+        wide_ref[u * 65 : u * 65 + 64] = field_ref[u * 64 : (u + 1) * 64].astype(F32)
+    for j in range(count_tiles):
+        for c in range(2):
+            x_ref[(j + 1) * rows : (j + 2) * rows, c * 128 : (c + 1) * 128] = wide_ref[
+                pl.ds(2 * j + c, rows, stride=65)
+            ].astype(BF16)
+    step = 16
 
     def chunk(q, carry):
         got = banded_rows(x_ref, w_ref, q * (step * rows), step * rows, rows)
@@ -79,19 +76,25 @@
 def first_stage(field, tiles):
     rows, length = field.shape[1], field.shape[3]
     tiles_count = length // TILE
+    field = field.reshape(rows, 2, tiles_count, TILE).transpose(0, 2, 1, 3).reshape(rows * tiles_count * 2, TILE)
     return pl.pallas_call(
         first_kernel,
         out_shape=jax.ShapeDtypeStruct((8, length // 64, 8, 128), BF16),
         in_specs=[whole(), whole()],
         out_specs=whole(),
-        scratch_shapes=[pltpu.VMEM(((tiles_count + 2) * rows, 256), BF16), pltpu.VMEM((3, 256, 256), BF16)],
+        scratch_shapes=[
+            pltpu.VMEM((64 * 65, 128), F32),
+            pltpu.VMEM(((tiles_count + 2) * rows, 256), BF16),
+            pltpu.VMEM((3, 256, 256), BF16),
+        ],
         cost_estimate=pl.CostEstimate(flops=2 * rows * tiles_count * 768 * 256, bytes_accessed=1 << 21, transcendentals=0),
         name="first",
     )(field, tiles)
 
 
-def half_of(x, want):
-    return jnp.where(want, pltpu.roll(x, 64, 1), x)
+def both_ways(wide_ref, at, x):
+    wide_ref[2 * at] = x
+    wide_ref[2 * at + 1] = pltpu.roll(x, 64, 1)
 
 
 def heights_out_kernel(index_ref, mine_ref, figure_ref, *refs):
@@ -99,21 +102,12 @@
     pairs = figure_ref.shape[1] // 128
     lane = lax.broadcasted_iota(jnp.int32, (8, 128), 1)
     for p in range(pairs):
-        wide_ref[p] = figure_ref[:, p * 128 : (p + 1) * 128].astype(F32)
-
+        both_ways(wide_ref, p, figure_ref[:, p * 128 : (p + 1) * 128].astype(F32))
     z, y = mine_ref[1], mine_ref[2]
-    for low in range(4):
-
-        def slot(at, carry):
-            d = ((z + 4 * (at >> 2) + low + 11) & 15) * 4 + ((y + at + 3) & 3)
-            k0 = index_ref[0, d]
-            k1 = index_ref[1, d]
-            a = half_of(wide_ref[k0 >> 1], (k0 & 1) != 0)
-            b = half_of(wide_ref[k1 >> 1], (k1 & 1) != 1)
-            outs[low][at] = jnp.where(lane < 64, a, b).astype(BF16)
-            return carry
-
-        lax.fori_loop(0, 16, slot, 0, unroll=8)
+    for leg in range(4):
+        for at in range(16):
+            d = ((z + at) & 15) * 4 + ((y + leg + 3) & 3)
+            outs[leg][at] = jnp.where(lane < 64, wide_ref[index_ref[0, d]], wide_ref[index_ref[1, d]]).astype(BF16)
 
 
 def heights_out(index, mine, figure):
@@ -126,93 +120,60 @@
             grid=(1,),
             in_specs=[pl.BlockSpec((8, figure.shape[1]), lambda g, index, mine: (mine[0], 0))],
             out_specs=[out] * 4,
-            scratch_shapes=[pltpu.VMEM((figure.shape[1] // 128, 8, 128), F32)],
+            scratch_shapes=[pltpu.VMEM((figure.shape[1] // 64, 8, 128), F32)],
         ),
         name="heights_out",
     )(index, mine, figure)
 
 
 def regroup_kernel(*refs):
-    for a in range(4):
-        for b in range(4):
-            refs[4 + b][4 * a : 4 * a + 4] = refs[a][4 * b : 4 * b + 4]
+    for y in range(4):
+        for z in range(16):
+            refs[4 + z][y] = refs[y][z]
 
 
 def regroup(parts):
     return pl.pallas_call(
         regroup_kernel,
-        out_shape=[jax.ShapeDtypeStruct(parts[0].shape, BF16)] * 4,
+        out_shape=[jax.ShapeDtypeStruct((4, 8, 128), BF16)] * 16,
         in_specs=[whole()] * 4,
-        out_specs=[whole()] * 4,
+        out_specs=[whole()] * 16,
         name="regroup",
     )(*parts)
 
 
-def regroup_last_kernel(*refs):
-    for b in range(4):
-        for a in range(4):
-            for c in range(4):
-                refs[4 + c][4 * a + b] = refs[b][4 * a + c]
-
-
-def regroup_last(parts):
-    return pl.pallas_call(
-        regroup_last_kernel,
-        out_shape=[jax.ShapeDtypeStruct(parts[0].shape, BF16)] * 4,
-        in_specs=[whole()] * 4,
-        out_specs=[whole()] * 4,
-        name="regroup_last",
-    )(*parts)
-
-
-DIGITS = (-1, 0, 1, 2)
-
-
-def moved(parts, bands, way):
+def moved(part, bands, z_step, y_step):
     spots = bands // 4
-
-    def target(b, step):
-        z, y = b // 4, b % 4
-        if way == "low":
-            return (z + step) % spots * 4 + y
-        if way == "high":
-            return (z + 4 * step) % spots * 4 + y
-        return z * 4 + (y + step) % 4
-
-    return [
-        part if step == 0 else lax.ppermute(part, "band", [(b, target(b, step)) for b in range(bands)])
-        for part, step in zip(parts, DIGITS)
-    ]
+    if z_step == 0 and y_step == 0:
+        return part
+    target = lambda b: (b // 4 + z_step) % spots * 4 + (b + y_step) % 4
+    return lax.ppermute(part, "band", [(b, target(b)) for b in range(bands)])
 
 
 def phase_kernel(index_ref, *refs):
-    cos_ref, sin_ref, wide_ref = refs[4:]
+    cos_ref, sin_ref, wide_ref = refs[16:]
     lane = lax.broadcasted_iota(jnp.int32, (8, 128), 1)
     pairs = cos_ref.shape[0]
-    for a in range(4):
-        for b in range(16):
-            wide_ref[16 * a + b] = refs[a][b].astype(F32)
+    for z in range(16):
+        for y in range(4):
+            both_ways(wide_ref, 4 * z + y, refs[z][y].astype(F32))
 
     def pair(p, carry):
-        s0, c0 = index_ref[0, 2 * p], index_ref[1, 2 * p]
-        s1, c1 = index_ref[0, 2 * p + 1], index_ref[1, 2 * p + 1]
-        a = half_of(wide_ref[s0], c0 != 0)
-        b = half_of(wide_ref[s1], c1 != 1)
-        phase = PHASE_FACTOR * jnp.where(lane < 64, a, b)
+        phase = PHASE_FACTOR * jnp.where(lane < 64, wide_ref[index_ref[2 * p]], wide_ref[index_ref[2 * p + 1]])
         cos_ref[p] = jnp.cos(phase)
         sin_ref[p] = jnp.sin(phase)
         return carry
 
-    lax.fori_loop(0, pairs, pair, 0, unroll=2)
+    lax.fori_loop(0, pairs, pair, 0, unroll=4)
 
 
 def phases(index, parts, pairs):
     return pl.pallas_call(
         phase_kernel,
         out_shape=[jax.ShapeDtypeStruct((pairs, 8, 128), F32)] * 2,
-        in_specs=[pl.BlockSpec(memory_space=pltpu.SMEM)] + [whole()] * 4,
+        in_specs=[pl.BlockSpec(memory_space=pltpu.SMEM)] + [whole()] * 16,
         out_specs=[whole(), whole()],
-        scratch_shapes=[pltpu.VMEM((64, 8, 128), F32)],
+        scratch_shapes=[pltpu.VMEM((128, 8, 128), F32)],
         name="phases",
     )(index, *parts)
 
@@ -236,7 +197,7 @@
         return carry
 
     lax.fori_loop(0, pairs, fill, 0, unroll=4)
-    step = 4
+    step = 16
 
     def mirror(q, carry):
         row = q * (step * rows)
@@ -317,33 +278,35 @@
     )(index, mine, got, approach, focus, cos, sin, target)
 
 
-def collect_kernel(index_ref, tiles_ref, out_ref, sum_ref):
+def collect_kernel(index_ref, tiles_ref, out_ref, wide_ref, *sums):
     lane = lax.broadcasted_iota(jnp.int32, (8, 128), 1)
-    pairs = out_ref.shape[1] // 128
-    sum_ref[...] = jnp.zeros_like(sum_ref)
-
-    def slot(d, carry):
-        x = tiles_ref[d].astype(F32)
-        turned = pltpu.roll(x, 64, 1)
+    pairs = out_ref.shape[2] // 128
+    bands = tiles_ref.shape[0]
+    for part in sums:
+        part[...] = jnp.zeros_like(part)
+    for d in range(bands):
+        both_ways(wide_ref, d, tiles_ref[d].astype(F32))
+    for d in range(bands):
         for c in range(2):
+            part = sums[2 * (d % 2) + c]
             k = index_ref[c, d]
-            tile = jnp.where((k & 1) != c, turned, x)
-            sum_ref[k >> 1] += jnp.where((lane < 64) == ((k & 1) == 0), tile, 0.0)
-        return carry
-
-    lax.fori_loop(0, tiles_ref.shape[0], slot, 0, unroll=8)
+            part[k] += wide_ref[2 * d + ((k & 1) ^ c)]
     for p in range(pairs):
-        out_ref[:, p * 128 : (p + 1) * 128] = sum_ref[p].astype(out_ref.dtype)
-
-
-def collect(index, tiles, dtype):
+        low = sums[0][2 * p] + sums[1][2 * p] + sums[2][2 * p] + sums[3][2 * p]
+        high = sums[0][2 * p + 1] + sums[1][2 * p + 1] + sums[2][2 * p + 1] + sums[3][2 * p + 1]
+        tile = jnp.where(lane < 64, low, high).astype(out_ref.dtype)
+        for copy in range(out_ref.shape[0]):
+            out_ref[copy, :, p * 128 : (p + 1) * 128] = tile
+
+
+def collect(index, tiles, copies, dtype):
     bands = tiles.shape[0]
     return pl.pallas_call(
         collect_kernel,
-        out_shape=jax.ShapeDtypeStruct((8, bands * 64), dtype),
+        out_shape=jax.ShapeDtypeStruct((copies, 8, bands * 64), dtype),
         in_specs=[pl.BlockSpec(memory_space=pltpu.SMEM), whole()],
         out_specs=whole(),
-        scratch_shapes=[pltpu.VMEM((bands // 2 + 1, 8, 128), F32)],
+        scratch_shapes=[pltpu.VMEM((2 * bands, 8, 128), F32)] + [pltpu.VMEM((bands + 8, 8, 128), F32)] * 4,
         name="collect",
     )(index, tiles)
 
@@ -361,28 +324,30 @@
     here = source_band == band
     low = jnp.min(jnp.where(here, code, blocks * blocks), axis=1)
     high = jnp.max(jnp.where(here, code, -1), axis=1)
-    add_index = jnp.stack([jnp.where(high >= 0, low & (blocks - 1), blocks), jnp.where(high > low, high & (blocks - 1), blocks)])
+    add_index = jnp.stack(
+        [
+            jnp.where(high >= 0, low & (blocks - 1), blocks),
+            jnp.where(high > low, high & (blocks - 1), blocks),
+        ]
+    )
+    send_index = (add_index & (blocks - 1)) ^ lax.broadcasted_iota(jnp.int32, add_index.shape, 0)
     my_band = lax.dynamic_index_in_dim(source_band, band, 0, keepdims=False)
     column = jnp.arange(blocks, dtype=jnp.int32)
     same = (my_band[:, None] == my_band[None, :]) & (column[None, :] < column[:, None])
     my_slot = jnp.any(same, axis=1).astype(jnp.int32)
     beam_index = jnp.stack([my_band, my_slot])
-    dz = z - (my_band >> 2)
-    step_low = (dz + 1) & 3
-    step_high = (((dz + 1 - step_low) >> 2) + 1) & 3
-    step_y = (y - my_band + 1) & 3
-    read_index = jnp.stack([16 * step_y + 4 * step_low + step_high, my_slot])
-    parts = heights_out(add_index & (blocks - 1), mine, figure)
-    parts = moved(parts, bands, "low")
+    stands = 4 * ((z - (my_band >> 2)) & (bands // 4 - 1)) + ((y - my_band + 1) & 3)
+    read_index = 2 * stands + (my_slot ^ (column & 1))
+    parts = heights_out(send_index, mine, figure)
+    parts = [moved(part, bands, 0, step - 1) for step, part in enumerate(parts)]
     parts = regroup(parts)
-    parts = moved(parts, bands, "high")
-    parts = regroup_last(parts)
-    parts = moved(parts, bands, "y")
+    parts = [moved(part, bands, step, 0) for step, part in enumerate(parts)]
     cos, sin = phases(read_index, parts, bands // 2)
     tiles = second_stage(beam_index, mine, got, approach_tiles, focus_tiles, cos, sin, target)
     tiles = lax.all_to_all(tiles, "band", split_axis=0, concat_axis=0, tiled=True)
-    own = collect(add_index, tiles, BF16)
-    return lax.all_gather(own, "mode", axis=0, tiled=True).astype(F32)
+    own = collect(add_index, tiles, out.shape[0], BF16)
+    whole_band = lax.all_to_all(own, "mode", split_axis=0, concat_axis=0, tiled=True)
+    return whole_band.reshape(figure.shape).astype(F32)
 
 
 def solution(mesh):

time: 187 us -> 189 us (1.011)
  starting transfers between devices: 63.4 us -> 115 us
  waiting for transfers between devices: 40.8 us -> 4.24 us
  Pallas kernels: 30 us -> 19.1 us
  blocking collectives: 45.6 us -> 43.3 us
    ppermute x9 -> x18, starting transfers between devices: 39.1 us -> 90.5 us  [moved(): return lax.ppermute(part, 'band', [(b, target(b)) for b in range(bands)])]
    ppermute x9 -> x18, waiting for transfers between devices: 40.8 us -> 4.24 us  [moved(): return lax.ppermute(part, 'band', [(b, target(b)) for b in range(bands)])]
    all_to_all x0 -> x1, blocking collectives: none -> 20.1 us  [shards(): lax.all_to_all(own, 'mode', split_axis=0, concat_axis=0, tiled=True)]
    all_gather x1 -> x0, blocking collectives: 18.4 us -> none  [shards(): return lax.all_gather(own, 'mode', axis=0, tiled=True).astype(F32)]
    all_to_all x1, blocking collectives: 27.2 us -> 23.2 us  [shards(): lax.all_to_all(tiles, 'band', split_axis=0, concat_axis=0, tiled=True)]
    pallas_call x1, Pallas kernels: 10.8 us -> 6.84 us  [second_stage(): pl.pallas_call(second_kernel, out_shape=jax.ShapeDtypeStruct((bands, 8, 1...]
    pallas_call x1, Pallas kernels: 6.83 us -> 3.9 us  [first_stage(): pl.pallas_call(first_kernel, out_shape=jax.ShapeDtypeStruct((8, length //...]
    pallas_call x3 -> x2, Pallas kernels: 5.75 us -> 3.65 us  [the longest x1 2.15 us: collect(): pl.pallas_call(collect_kernel, out_shape=jax.ShapeDtypeStruct((copies, 8,...]
  transfers between devices with their start and end apart: 10 -> 19, of which waited for: 5 -> 4; matrix products, arithmetic and copies ran while one was open for 1% -> 1% of each run, Pallas kernels for 5% -> 3%
where the time goes in v3:
time: 189 us; the launch traced here: 188 us
  starting transfers between devices  115 us (61%)
  blocking collectives  43.3 us (23%)
  Pallas kernels  19.1 us (10%)
  waiting for transfers between devices  4.24 us (2%)
  other arithmetic  3.7 us (2%)
  local copies, waits for them, and re-layouts  2.19 us (1%)
    ppermute x18, starting transfers between devices, moved(): return lax.ppermute(part, 'band', [(b, target(b)) for b in range(bands)])  90.5 us
    all_to_all x1, starting transfers between devices, shards(): lax.all_to_all(out.reshape(-1, 8, 128), ('mode', 'band'), split_axis=0, c...  24.3 us
    all_to_all x1, blocking collectives, shards(): lax.all_to_all(tiles, 'band', split_axis=0, concat_axis=0, tiled=True)  23.2 us
    all_to_all x1, blocking collectives, shards(): lax.all_to_all(own, 'mode', split_axis=0, concat_axis=0, tiled=True)  20.1 us
    pallas_call x1, Pallas kernels, second_stage(): pl.pallas_call(second_kernel, out_shape=jax.ShapeDtypeStruct((bands, 8, 1...  6.84 us
    ppermute x18, waiting for transfers between devices, moved(): return lax.ppermute(part, 'band', [(b, target(b)) for b in range(bands)])  4.24 us
    pallas_call x1, Pallas kernels, first_stage(): pl.pallas_call(first_kernel, out_shape=jax.ShapeDtypeStruct((8, length //...  3.9 us
  transfers between devices with their start and end apart: 19, of which 4 were waited for; matrix products, arithmetic and copies ran while one was open for 1% of the time, Pallas kernels for 3%

profile of v3, /device:TPU:1, one launch (start us, length us, event | category | flops | bytes accessed | tf_op | source)
XLA Modules:
  0.0 187.9 jit_solution(9406277950416680605)
XLA Ops:
  0.0 3.9 %first.1 = bf16[8,64,8,128]{3,2,1,0:T(8,128)(2,1)} custom-call(bf16[4096,128]{1,0:T(8,128)(2,1)} %bitcast.24, bf16[3,2,128,128]{3,2,1,0:T(8,128)(2,1)} %approach_ref.1), custom_call_target="tpu_custom_call" | custom-call | flops 805306368 | bytes 2097152 | tf_op jit(solution)/shard_map/first/pallas_call | solution.py:80
  3.9 24.3 %all-to-all-start = ((bf16[512,8,128]{2,1,0:T(8,128)(2,1)}), bf16[512,8,128]{2,1,0:T(8,128)(2,1)S(1)}, u32[]{:S(2)}, u32[]{:S(2)}) async-start(bf16[512,8,128]{2,1,0:T(8,128)(2,1)} %bitcast.23), calls=%async_computation | async-start | bytes 2097152 | tf_op jit(solution)/shard_map/all_to_all | solution.py:320
  29.5 2.4 %heights_out.1 = (bf16[16,8,128]{2,1,0:T(8,128)(2,1)}, bf16[16,8,128]{2,1,0:T(8,128)(2,1)}, bf16[16,8,128]{2,1,0:T(8,128)(2,1)}, bf16[16,8,128]{2,1,0:T(8,128)(2,1)}) custom-call(s32[2,64]{1,0:T(2,128)} %get-tuple-element.52.index_ref, s32[3]{0:T(128)} %pad_add_fusion.2.mine_ref, bf16[64,4096]{1,0:T(8,128)(2,1)} %figure_ref.1), custom_call_target="tpu_custom_call" | custom-call | tf_op jit(solution)/shard_map/heights_out/pallas_call | solution.py:115
  31.9 4.5 %collective-permute-start = (bf16[16,8,128]{2,1,0:T(8,128)(2,1)}, bf16[16,8,128]{2,1,0:T(8,128)(2,1)S(1)}, u32[]{:S(2)}, u32[]{:S(2)}) collective-permute-start(bf16[16,8,128]{2,1,0:T(8,128)(2,1)} %get-tuple-element.27), channel_id=1, source_target_pairs={{0,3},{1,0},{2,1},{3,2},{4,7},{5,4},{6,5},{7,6},{8,11},{9,8},{10,9... | collective-permute-start | bytes 98312 | tf_op jit(solution)/shard_map/ppermute | solution.py:150
  38.4 3.6 %collective-permute-start.2 = (bf16[16,8,128]{2,1,0:T(8,128)(2,1)}, bf16[16,8,128]{2,1,0:T(8,128)(2,1)S(1)}, u32[]{:S(2)}, u32[]{:S(2)}) collective-permute-start(bf16[16,8,128]{2,1,0:T(8,128)(2,1)} %get-tuple-element.30), channel_id=1, source_target_pairs={{0,2},{1,3},{2,0},{3,1},{4,6},{5,7},{6,4},{7,5},{8,10},{9,11},{10,... | collective-permute-start | bytes 98312 | tf_op jit(solution)/shard_map/ppermute | solution.py:150
  43.0 2.2 %collective-permute-done.2.refs_3_ = bf16[16,8,128]{2,1,0:T(8,128)(2,1)S(1)} collective-permute-done((bf16[16,8,128]{2,1,0:T(8,128)(2,1)}, bf16[16,8,128]{2,1,0:T(8,128)(2,1)S(1)}, u32[]{:S(2)}, u32[]{:S(2)}) %collective-permute-start.2) | collective-permute-done | bytes 32800 | tf_op jit(solution)/shard_map/ppermute | solution.py:150
  47.3 3.3 %collective-permute-start.3 = (bf16[4,8,128]{2,1,0:T(8,128)(2,1)}, bf16[4,8,128]{2,1,0:T(8,128)(2,1)S(1)}, u32[]{:S(2)}, u32[]{:S(2)}) collective-permute-start(bf16[4,8,128]{2,1,0:T(8,128)(2,1)} %get-tuple-element.32), channel_id=1, source_target_pairs={{0,4},{1,5},{2,6},{3,7},{4,8},{5,9},{6,10},{7,11},{8,12},{9,13},{1... | collective-permute-start | bytes 24584 | tf_op jit(solution)/shard_map/ppermute | solution.py:150
  50.6 4.5 %collective-permute-start.4 = (bf16[4,8,128]{2,1,0:T(8,128)(2,1)}, bf16[4,8,128]{2,1,0:T(8,128)(2,1)S(1)}, u32[]{:S(2)}, u32[]{:S(2)}) collective-permute-start(bf16[4,8,128]{2,1,0:T(8,128)(2,1)} %get-tuple-element.33), channel_id=1, source_target_pairs={{0,8},{1,9},{2,10},{3,11},{4,12},{5,13},{6,14},{7,15},{8,16},{9,17... | collective-permute-start | bytes 24584 | tf_op jit(solution)/shard_map/ppermute | solution.py:150
  55.1 7.0 %collective-permute-start.5 = (bf16[4,8,128]{2,1,0:T(8,128)(2,1)}, bf16[4,8,128]{2,1,0:T(8,128)(2,1)S(1)}, u32[]{:S(2)}, u32[]{:S(2)}) collective-permute-start(bf16[4,8,128]{2,1,0:T(8,128)(2,1)} %get-tuple-element.34), channel_id=1, source_target_pairs={{0,12},{1,13},{2,14},{3,15},{4,16},{5,17},{6,18},{7,19},{8,20},{9,... | collective-permute-start | bytes 24584 | tf_op jit(solution)/shard_map/ppermute | solution.py:150
  62.1 6.2 %collective-permute-start.6 = (bf16[4,8,128]{2,1,0:T(8,128)(2,1)}, bf16[4,8,128]{2,1,0:T(8,128)(2,1)S(1)}, u32[]{:S(2)}, u32[]{:S(2)}) collective-permute-start(bf16[4,8,128]{2,1,0:T(8,128)(2,1)} %get-tuple-element.35), channel_id=1, source_target_pairs={{0,16},{1,17},{2,18},{3,19},{4,20},{5,21},{6,22},{7,23},{8,24},{9,... | collective-permute-start | bytes 24584 | tf_op jit(solution)/shard_map/ppermute | solution.py:150
  68.4 3.5 %collective-permute-start.7 = (bf16[4,8,128]{2,1,0:T(8,128)(2,1)}, bf16[4,8,128]{2,1,0:T(8,128)(2,1)S(1)}, u32[]{:S(2)}, u32[]{:S(2)}) collective-permute-start(bf16[4,8,128]{2,1,0:T(8,128)(2,1)} %get-tuple-element.36), channel_id=1, source_target_pairs={{0,20},{1,21},{2,22},{3,23},{4,24},{5,25},{6,26},{7,27},{8,28},{9,... | collective-permute-start | bytes 24584 | tf_op jit(solution)/shard_map/ppermute | solution.py:150
  73.6 7.5 %collective-permute-start.8 = (bf16[4,8,128]{2,1,0:T(8,128)(2,1)}, bf16[4,8,128]{2,1,0:T(8,128)(2,1)S(1)}, u32[]{:S(2)}, u32[]{:S(2)}) collective-permute-start(bf16[4,8,128]{2,1,0:T(8,128)(2,1)} %get-tuple-element.37), channel_id=1, source_target_pairs={{0,24},{1,25},{2,26},{3,27},{4,28},{5,29},{6,30},{7,31},{8,32},{9,... | collective-permute-start | bytes 24584 | tf_op jit(solution)/shard_map/ppermute | solution.py:150
  81.1 4.7 %collective-permute-start.9 = (bf16[4,8,128]{2,1,0:T(8,128)(2,1)}, bf16[4,8,128]{2,1,0:T(8,128)(2,1)S(1)}, u32[]{:S(2)}, u32[]{:S(2)}) collective-permute-start(bf16[4,8,128]{2,1,0:T(8,128)(2,1)} %get-tuple-element.38), channel_id=1, source_target_pairs={{0,28},{1,29},{2,30},{3,31},{4,32},{5,33},{6,34},{7,35},{8,36},{9,... | collective-permute-start | bytes 24584 | tf_op jit(solution)/shard_map/ppermute | solution.py:150
  85.8 8.1 %collective-permute-start.10 = (bf16[4,8,128]{2,1,0:T(8,128)(2,1)}, bf16[4,8,128]{2,1,0:T(8,128)(2,1)S(1)}, u32[]{:S(2)}, u32[]{:S(2)}) collective-permute-start(bf16[4,8,128]{2,1,0:T(8,128)(2,1)} %get-tuple-element.39), channel_id=1, source_target_pairs={{0,32},{1,33},{2,34},{3,35},{4,36},{5,37},{6,38},{7,39},{8,40},{9,... | collective-permute-start | bytes 24584 | tf_op jit(solution)/shard_map/ppermute | solution.py:150
  93.9 5.5 %collective-permute-start.11 = (bf16[4,8,128]{2,1,0:T(8,128)(2,1)}, bf16[4,8,128]{2,1,0:T(8,128)(2,1)S(1)}, u32[]{:S(2)}, u32[]{:S(2)}) collective-permute-start(bf16[4,8,128]{2,1,0:T(8,128)(2,1)} %get-tuple-element.40), channel_id=1, source_target_pairs={{0,36},{1,37},{2,38},{3,39},{4,40},{5,41},{6,42},{7,43},{8,44},{9,... | collective-permute-start | bytes 24584 | tf_op jit(solution)/shard_map/ppermute | solution.py:150
  99.5 10.0 %collective-permute-start.12 = (bf16[4,8,128]{2,1,0:T(8,128)(2,1)}, bf16[4,8,128]{2,1,0:T(8,128)(2,1)S(1)}, u32[]{:S(2)}, u32[]{:S(2)}) collective-permute-start(bf16[4,8,128]{2,1,0:T(8,128)(2,1)} %get-tuple-element.41), channel_id=1, source_target_pairs={{0,40},{1,41},{2,42},{3,43},{4,44},{5,45},{6,46},{7,47},{8,48},{9,... | collective-permute-start | bytes 24584 | tf_op jit(solution)/shard_map/ppermute | solution.py:150
  111.4 4.8 %collective-permute-start.14 = (bf16[4,8,128]{2,1,0:T(8,128)(2,1)S(1)}, bf16[4,8,128]{2,1,0:T(8,128)(2,1)S(1)}, u32[]{:S(2)}, u32[]{:S(2)}) collective-permute-start(bf16[4,8,128]{2,1,0:T(8,128)(2,1)S(1)} %copy-done.23), channel_id=1, source_target_pairs={{0,48},{1,49},{2,50},{3,51},{4,52},{5,53},{6,54},{7,55},{8,56},{9,... | collective-permute-start | bytes 24584 | tf_op jit(solution)/shard_map/ppermute | solution.py:150
  116.3 4.7 %collective-permute-start.15 = (bf16[4,8,128]{2,1,0:T(8,128)(2,1)S(1)}, bf16[4,8,128]{2,1,0:T(8,128)(2,1)S(1)}, u32[]{:S(2)}, u32[]{:S(2)}) collective-permute-start(bf16[4,8,128]{2,1,0:T(8,128)(2,1)S(1)} %copy-done.22), channel_id=1, source_target_pairs={{0,52},{1,53},{2,54},{3,55},{4,56},{5,57},{6,58},{7,59},{8,60},{9,... | collective-permute-start | bytes 24584 | tf_op jit(solution)/shard_map/ppermute | solution.py:150
  121.0 3.4 %collective-permute-start.16 = (bf16[4,8,128]{2,1,0:T(8,128)(2,1)S(1)}, bf16[4,8,128]{2,1,0:T(8,128)(2,1)S(1)}, u32[]{:S(2)}, u32[]{:S(2)}) collective-permute-start(bf16[4,8,128]{2,1,0:T(8,128)(2,1)S(1)} %copy-done.21), channel_id=1, source_target_pairs={{0,56},{1,57},{2,58},{3,59},{4,60},{5,61},{6,62},{7,63},{8,0},{9,1... | collective-permute-start | bytes 24584 | tf_op jit(solution)/shard_map/ppermute | solution.py:150
  124.5 5.3 %collective-permute-start.17 = (bf16[4,8,128]{2,1,0:T(8,128)(2,1)S(1)}, bf16[4,8,128]{2,1,0:T(8,128)(2,1)S(1)}, u32[]{:S(2)}, u32[]{:S(2)}) collective-permute-start(bf16[4,8,128]{2,1,0:T(8,128)(2,1)S(1)} %copy-done.20), channel_id=1, source_target_pairs={{0,60},{1,61},{2,62},{3,63},{4,0},{5,1},{6,2},{7,3},{8,4},{9,5},{1... | collective-permute-start | bytes 24584 | tf_op jit(solution)/shard_map/ppermute | solution.py:150
  131.2 2.3 %phases.1 = (f32[32,8,128]{2,1,0:T(8,128)}, f32[32,8,128]{2,1,0:T(8,128)}) custom-call(s32[64]{0:T(128)} %fusion.5.index_ref, bf16[4,8,128]{2,1,0:T(8,128)(2,1)} %get-tuple-element.31.refs_0_, bf16[4,8,128]{2,1,0:T(8,128)(2,1)} %copy-done.5, bf16[4,8,128]{2,1,0:T(8,128)(2,1)} %copy-done.6, bf16[4,8,128]{2,1,0:T(8,128)(2,1)} %copy-done.7, ...), custom_call_target="tpu_custom_call" | custom-call | tf_op jit(solution)/shard_map/phases/pallas_call | solution.py:171
  134.5 6.8 %second.1 = bf16[64,8,128]{2,1,0:T(8,128)(2,1)} custom-call(s32[2,64]{1,0:T(2,128)} %pad_add_fusion.1.index_ref, s32[3]{0:T(128)} %pad_add_fusion.2.mine_ref, bf16[8,64,8,128]{3,2,1,0:T(8,128)(2,1)} %bitcast.22, bf16[3,2,128,128]{3,2,1,0:T(8,128)(2,1)} %approach_ref.1, bf16[3,2,128,128]{3,2,1,0:T(8,128)(2,1)} %focus_ref.1, ...), custom_call_target="tpu_custom_call" | custom-call | flops 2415919104 | bytes 1048576 | tf_op jit(solution)/shard_map/second/pallas_call | solution.py:259
  141.4 23.2 %all_to_all.15.tiles_ref = bf16[64,8,128]{2,1,0:T(8,128)(2,1)} all-to-all(bf16[64,8,128]{2,1,0:T(8,128)(2,1)} %second.1), channel_id=1, replica_groups=mesh['mode'=8,'band'=64] {'band'}, dimensions={0} | all-to-all | bytes 262144 | tf_op jit(solution)/shard_map/all_to_all | solution.py:347
  166.7 20.1 %all_to_all.16 = bf16[8,8,4096]{2,1,0:T(8,128)(2,1)S(1)} all-to-all(bf16[8,8,4096]{2,1,0:T(8,128)(2,1)} %collect.1), channel_id=1, replica_groups=mesh['mode'=8,'band'=64] {'mode'}, dimensions={0} | all-to-all | bytes 1048576 | tf_op jit(solution)/shard_map/all_to_all | solution.py:349
  (82 shorter events, 15.4 us)
Async XLA Ops:
  3.9 129.7 %all-to-all-start = ((bf16[512,8,128]{2,1,0:T(8,128)(2,1)}), bf16[512,8,128]{2,1,0:T(8,128)(2,1)S(1)}, u32[]{:S(2)}, u32[]{:S(2)}) async-start(bf16[512,8,128]{2,1,0:T(8,128)(2,1)} %bitcast.23), calls=%async_computation | async-start | bytes 2097152 | tf_op jit(solution)/shard_map/all_to_all | solution.py:320
  31.9 10.3 %collective-permute-start = (bf16[16,8,128]{2,1,0:T(8,128)(2,1)}, bf16[16,8,128]{2,1,0:T(8,128)(2,1)S(1)}, u32[]{:S(2)}, u32[]{:S(2)}) collective-permute-start(bf16[16,8,128]{2,1,0:T(8,128)(2,1)} %get-tuple-element.27), channel_id=1, source_target_pairs={{0,3},{1,0},{2,1},{3,2},{4,7},{5,4},{6,5},{7,6},{8,11},{9,8},{10,9... | collective-permute-start | bytes 98312 | tf_op jit(solution)/shard_map/ppermute | solution.py:150
  36.4 6.5 %collective-permute-start.1 = (bf16[16,8,128]{2,1,0:T(8,128)(2,1)}, bf16[16,8,128]{2,1,0:T(8,128)(2,1)S(1)}, u32[]{:S(2)}, u32[]{:S(2)}) collective-permute-start(bf16[16,8,128]{2,1,0:T(8,128)(2,1)} %get-tuple-element.29), channel_id=1, source_target_pairs={{0,1},{1,2},{2,3},{3,0},{4,5},{5,6},{6,7},{7,4},{8,9},{9,10},{10,1... | collective-permute-start | bytes 98312 | tf_op jit(solution)/shard_map/ppermute | solution.py:150
  38.4 6.8 %collective-permute-start.2 = (bf16[16,8,128]{2,1,0:T(8,128)(2,1)}, bf16[16,8,128]{2,1,0:T(8,128)(2,1)S(1)}, u32[]{:S(2)}, u32[]{:S(2)}) collective-permute-start(bf16[16,8,128]{2,1,0:T(8,128)(2,1)} %get-tuple-element.30), channel_id=1, source_target_pairs={{0,2},{1,3},{2,0},{3,1},{4,6},{5,7},{6,4},{7,5},{8,10},{9,11},{10,... | collective-permute-start | bytes 98312 | tf_op jit(solution)/shard_map/ppermute | solution.py:150
  47.3 64.1 %copy-start.23 = (bf16[4,8,128]{2,1,0:T(8,128)(2,1)S(1)}, bf16[4,8,128]{2,1,0:T(8,128)(2,1)}, u32[]{:S(2)}) copy-start(bf16[4,8,128]{2,1,0:T(8,128)(2,1)} %get-tuple-element.43) | copy-start | bytes 24580
  47.3 26.3 %collective-permute-start.3 = (bf16[4,8,128]{2,1,0:T(8,128)(2,1)}, bf16[4,8,128]{2,1,0:T(8,128)(2,1)S(1)}, u32[]{:S(2)}, u32[]{:S(2)}) collective-permute-start(bf16[4,8,128]{2,1,0:T(8,128)(2,1)} %get-tuple-element.32), channel_id=1, source_target_pairs={{0,4},{1,5},{2,6},{3,7},{4,8},{5,9},{6,10},{7,11},{8,12},{9,13},{1... | collective-permute-start | bytes 24584 | tf_op jit(solution)/shard_map/ppermute | solution.py:150
  50.6 30.5 %collective-permute-start.4 = (bf16[4,8,128]{2,1,0:T(8,128)(2,1)}, bf16[4,8,128]{2,1,0:T(8,128)(2,1)S(1)}, u32[]{:S(2)}, u32[]{:S(2)}) collective-permute-start(bf16[4,8,128]{2,1,0:T(8,128)(2,1)} %get-tuple-element.33), channel_id=1, source_target_pairs={{0,8},{1,9},{2,10},{3,11},{4,12},{5,13},{6,14},{7,15},{8,16},{9,17... | collective-permute-start | bytes 24584 | tf_op jit(solution)/shard_map/ppermute | solution.py:150
  55.1 30.7 %collective-permute-start.5 = (bf16[4,8,128]{2,1,0:T(8,128)(2,1)}, bf16[4,8,128]{2,1,0:T(8,128)(2,1)S(1)}, u32[]{:S(2)}, u32[]{:S(2)}) collective-permute-start(bf16[4,8,128]{2,1,0:T(8,128)(2,1)} %get-tuple-element.34), channel_id=1, source_target_pairs={{0,12},{1,13},{2,14},{3,15},{4,16},{5,17},{6,18},{7,19},{8,20},{9,... | collective-permute-start | bytes 24584 | tf_op jit(solution)/shard_map/ppermute | solution.py:150
  62.1 31.8 %collective-permute-start.6 = (bf16[4,8,128]{2,1,0:T(8,128)(2,1)}, bf16[4,8,128]{2,1,0:T(8,128)(2,1)S(1)}, u32[]{:S(2)}, u32[]{:S(2)}) collective-permute-start(bf16[4,8,128]{2,1,0:T(8,128)(2,1)} %get-tuple-element.35), channel_id=1, source_target_pairs={{0,16},{1,17},{2,18},{3,19},{4,20},{5,21},{6,22},{7,23},{8,24},{9,... | collective-permute-start | bytes 24584 | tf_op jit(solution)/shard_map/ppermute | solution.py:150
  68.4 47.9 %copy-start.22 = (bf16[4,8,128]{2,1,0:T(8,128)(2,1)S(1)}, bf16[4,8,128]{2,1,0:T(8,128)(2,1)}, u32[]{:S(2)}) copy-start(bf16[4,8,128]{2,1,0:T(8,128)(2,1)} %get-tuple-element.44) | copy-start | bytes 24580
  68.4 31.1 %collective-permute-start.7 = (bf16[4,8,128]{2,1,0:T(8,128)(2,1)}, bf16[4,8,128]{2,1,0:T(8,128)(2,1)S(1)}, u32[]{:S(2)}, u32[]{:S(2)}) collective-permute-start(bf16[4,8,128]{2,1,0:T(8,128)(2,1)} %get-tuple-element.36), channel_id=1, source_target_pairs={{0,20},{1,21},{2,22},{3,23},{4,24},{5,25},{6,26},{7,27},{8,28},{9,... | collective-permute-start | bytes 24584 | tf_op jit(solution)/shard_map/ppermute | solution.py:150
  73.6 42.7 %copy-start.5 = (bf16[4,8,128]{2,1,0:T(8,128)(2,1)}, bf16[4,8,128]{2,1,0:T(8,128)(2,1)S(1)}, u32[]{:S(2)}) copy-start(bf16[4,8,128]{2,1,0:T(8,128)(2,1)S(1)} %collective-permute-done.3.refs_1_) | copy-start | bytes 24580
  73.6 35.9 %collective-permute-start.8 = (bf16[4,8,128]{2,1,0:T(8,128)(2,1)}, bf16[4,8,128]{2,1,0:T(8,128)(2,1)S(1)}, u32[]{:S(2)}, u32[]{:S(2)}) collective-permute-start(bf16[4,8,128]{2,1,0:T(8,128)(2,1)} %get-tuple-element.37), channel_id=1, source_target_pairs={{0,24},{1,25},{2,26},{3,27},{4,28},{5,29},{6,30},{7,31},{8,32},{9,... | collective-permute-start | bytes 24584 | tf_op jit(solution)/shard_map/ppermute | solution.py:150
  81.1 40.0 %copy-start.6 = (bf16[4,8,128]{2,1,0:T(8,128)(2,1)}, bf16[4,8,128]{2,1,0:T(8,128)(2,1)S(1)}, u32[]{:S(2)}) copy-start(bf16[4,8,128]{2,1,0:T(8,128)(2,1)S(1)} %collective-permute-done.4.refs_2_) | copy-start | bytes 24580
  81.1 30.3 %collective-permute-start.9 = (bf16[4,8,128]{2,1,0:T(8,128)(2,1)}, bf16[4,8,128]{2,1,0:T(8,128)(2,1)S(1)}, u32[]{:S(2)}, u32[]{:S(2)}) collective-permute-start(bf16[4,8,128]{2,1,0:T(8,128)(2,1)} %get-tuple-element.38), channel_id=1, source_target_pairs={{0,28},{1,29},{2,30},{3,31},{4,32},{5,33},{6,34},{7,35},{8,36},{9,... | collective-permute-start | bytes 24584 | tf_op jit(solution)/shard_map/ppermute | solution.py:150
  85.8 44.8 %copy-start.7 = (bf16[4,8,128]{2,1,0:T(8,128)(2,1)}, bf16[4,8,128]{2,1,0:T(8,128)(2,1)S(1)}, u32[]{:S(2)}) copy-start(bf16[4,8,128]{2,1,0:T(8,128)(2,1)S(1)} %collective-permute-done.5.refs_3_) | copy-start | bytes 24580
  85.8 30.5 %collective-permute-start.10 = (bf16[4,8,128]{2,1,0:T(8,128)(2,1)}, bf16[4,8,128]{2,1,0:T(8,128)(2,1)S(1)}, u32[]{:S(2)}, u32[]{:S(2)}) collective-permute-start(bf16[4,8,128]{2,1,0:T(8,128)(2,1)} %get-tuple-element.39), channel_id=1, source_target_pairs={{0,32},{1,33},{2,34},{3,35},{4,36},{5,37},{6,38},{7,39},{8,40},{9,... | collective-permute-start | bytes 24584 | tf_op jit(solution)/shard_map/ppermute | solution.py:150
  93.9 27.1 %collective-permute-start.11 = (bf16[4,8,128]{2,1,0:T(8,128)(2,1)}, bf16[4,8,128]{2,1,0:T(8,128)(2,1)S(1)}, u32[]{:S(2)}, u32[]{:S(2)}) collective-permute-start(bf16[4,8,128]{2,1,0:T(8,128)(2,1)} %get-tuple-element.40), channel_id=1, source_target_pairs={{0,36},{1,37},{2,38},{3,39},{4,40},{5,41},{6,42},{7,43},{8,44},{9,... | collective-permute-start | bytes 24584 | tf_op jit(solution)/shard_map/ppermute | solution.py:150
  99.5 25.0 %collective-permute-start.12 = (bf16[4,8,128]{2,1,0:T(8,128)(2,1)}, bf16[4,8,128]{2,1,0:T(8,128)(2,1)S(1)}, u32[]{:S(2)}, u32[]{:S(2)}) collective-permute-start(bf16[4,8,128]{2,1,0:T(8,128)(2,1)} %get-tuple-element.41), channel_id=1, source_target_pairs={{0,40},{1,41},{2,42},{3,43},{4,44},{5,45},{6,46},{7,47},{8,48},{9,... | collective-permute-start | bytes 24584 | tf_op jit(solution)/shard_map/ppermute | solution.py:150
  109.5 21.0 %collective-permute-start.13 = (bf16[4,8,128]{2,1,0:T(8,128)(2,1)}, bf16[4,8,128]{2,1,0:T(8,128)(2,1)S(1)}, u32[]{:S(2)}, u32[]{:S(2)}) collective-permute-start(bf16[4,8,128]{2,1,0:T(8,128)(2,1)} %get-tuple-element.42), channel_id=1, source_target_pairs={{0,44},{1,45},{2,46},{3,47},{4,48},{5,49},{6,50},{7,51},{8,52},{9,... | collective-permute-start | bytes 24584 | tf_op jit(solution)/shard_map/ppermute | solution.py:150
  111.4 19.0 %collective-permute-start.14 = (bf16[4,8,128]{2,1,0:T(8,128)(2,1)S(1)}, bf16[4,8,128]{2,1,0:T(8,128)(2,1)S(1)}, u32[]{:S(2)}, u32[]{:S(2)}) collective-permute-start(bf16[4,8,128]{2,1,0:T(8,128)(2,1)S(1)} %copy-done.23), channel_id=1, source_target_pairs={{0,48},{1,49},{2,50},{3,51},{4,52},{5,53},{6,54},{7,55},{8,56},{9,... | collective-permute-start | bytes 24584 | tf_op jit(solution)/shard_map/ppermute | solution.py:150
  116.3 14.2 %collective-permute-start.15 = (bf16[4,8,128]{2,1,0:T(8,128)(2,1)S(1)}, bf16[4,8,128]{2,1,0:T(8,128)(2,1)S(1)}, u32[]{:S(2)}, u32[]{:S(2)}) collective-permute-start(bf16[4,8,128]{2,1,0:T(8,128)(2,1)S(1)} %copy-done.22), channel_id=1, source_target_pairs={{0,52},{1,53},{2,54},{3,55},{4,56},{5,57},{6,58},{7,59},{8,60},{9,... | collective-permute-start | bytes 24584 | tf_op jit(solution)/shard_map/ppermute | solution.py:150
  121.0 9.4 %collective-permute-start.16 = (bf16[4,8,128]{2,1,0:T(8,128)(2,1)S(1)}, bf16[4,8,128]{2,1,0:T(8,128)(2,1)S(1)}, u32[]{:S(2)}, u32[]{:S(2)}) collective-permute-start(bf16[4,8,128]{2,1,0:T(8,128)(2,1)S(1)} %copy-done.21), channel_id=1, source_target_pairs={{0,56},{1,57},{2,58},{3,59},{4,60},{5,61},{6,62},{7,63},{8,0},{9,1... | collective-permute-start | bytes 24584 | tf_op jit(solution)/shard_map/ppermute | solution.py:150
  124.5 6.1 %collective-permute-start.17 = (bf16[4,8,128]{2,1,0:T(8,128)(2,1)S(1)}, bf16[4,8,128]{2,1,0:T(8,128)(2,1)S(1)}, u32[]{:S(2)}, u32[]{:S(2)}) collective-permute-start(bf16[4,8,128]{2,1,0:T(8,128)(2,1)S(1)} %copy-done.20), channel_id=1, source_target_pairs={{0,60},{1,61},{2,62},{3,63},{4,0},{5,1},{6,2},{7,3},{8,4},{9,5},{1... | collective-permute-start | bytes 24584 | tf_op jit(solution)/shard_map/ppermute | solution.py:150
  (19 other events, 251.9 us)

commit v4 on v3

v4 whole, which is shorter than its diff:
```python
import functools

import jax
import jax.numpy as jnp
from jax import lax
from jax.experimental import pallas as pl
from jax.experimental.pallas import tpu as pltpu
from jax.sharding import PartitionSpec as P

TILE = 128
HALF = 64
MIRROR_TILE = 64
PHASE_FACTOR = 4.0
F32 = jnp.float32
BF16 = jnp.bfloat16


def whole(*_):
    return pl.BlockSpec(memory_space=pltpu.VMEM)


def write_weights(tiles_ref, w_ref, split):
    for o in range(3):
        re = tiles_ref[o, 0].astype(F32)
        im = tiles_ref[o, 1].astype(F32)
        upper = jnp.concatenate([re, im], axis=1).astype(BF16)
        lower = jnp.concatenate([-im, re], axis=1).astype(BF16)
        if split:
            w_ref[o, 0:64] = upper[0:64]
            w_ref[o, 64:128] = lower[0:64]
            w_ref[o, 128:192] = upper[64:128]
            w_ref[o, 192:256] = lower[64:128]
        else:
            w_ref[o, 0:128] = upper
            w_ref[o, 128:256] = lower


def banded_rows(x_ref, w_ref, row, count, rows, flip=False):
    total = None
    for o in range(3):
        x = x_ref[pl.ds(pl.multiple_of(row + o * rows, 64), count)]
        if flip:
            part = lax.dot_general(x, w_ref[2 - o], (((1,), (1,)), ((), ())), preferred_element_type=F32)
        else:
            part = jnp.dot(x, w_ref[o], preferred_element_type=F32)
        total = part if total is None else total + part
    return total


def first_kernel(field_ref, tiles_ref, out_ref, field_buf, out_buf, wide_ref, x_ref, w_ref, in_sem, out_sem):
    count_tiles = field_ref.shape[0] // 128
    rows = 64
    pitch = 2 * count_tiles + 1
    parts = 4
    lines = rows // parts
    size = lines * 2 * count_tiles
    loads = [
        pltpu.make_async_copy(
            field_ref.at[pl.ds(i * size, size)], field_buf.at[pl.ds(i * size, size)], in_sem.at[i]
        )
        for i in range(parts)
    ]
    for load in loads:
        load.start()
    write_weights(tiles_ref, w_ref, False)
    x_ref[0:rows] = jnp.zeros((rows, 256), BF16)
    x_ref[(count_tiles + 1) * rows : (count_tiles + 2) * rows] = jnp.zeros((rows, 256), BF16)
    for u in range(rows):
        if u % lines == 0:
            loads[u // lines].wait()
        wide_ref[u * pitch : u * pitch + 2 * count_tiles] = field_buf[
            u * 2 * count_tiles : (u + 1) * 2 * count_tiles
        ].astype(F32)
    for j in range(count_tiles):
        for c in range(2):
            x_ref[(j + 1) * rows : (j + 2) * rows, c * 128 : (c + 1) * 128] = wide_ref[
                pl.ds(2 * j + c, rows, stride=pitch)
            ].astype(BF16)
    step = 16
    stores = []
    for q in range(count_tiles // step):
        got = banded_rows(x_ref, w_ref, q * (step * rows), step * rows, rows)
        for t in range(step):
            mine = got[t * rows : (t + 1) * rows]
            stacked = jnp.concatenate([mine[:, 0:128], mine[:, 128:256]], axis=0)
            turned = jnp.transpose(stacked).astype(BF16)
            at = (q * step + t) * 2
            for h in range(2):
                out_buf[:, at + h : at + h + 1] = turned[h * 64 : (h + 1) * 64].reshape(8, 1, 8, 128)
        span = pl.ds(q * 2 * step, 2 * step)
        store = pltpu.make_async_copy(out_buf.at[:, span], out_ref.at[:, span], out_sem.at[q])
        store.start()
        stores.append(store)
    for store in stores:
        store.wait()


def first_stage(field, tiles):
    rows, length = field.shape[1], field.shape[3]
    count = length // TILE
    field = field.reshape(rows, 2, count, TILE).transpose(0, 2, 1, 3).reshape(rows * count * 2, TILE)
    shape = (8, length // 64, 8, 128)
    return pl.pallas_call(
        first_kernel,
        out_shape=jax.ShapeDtypeStruct(shape, BF16),
        in_specs=[pl.BlockSpec(memory_space=pl.ANY), whole()],
        out_specs=pl.BlockSpec(memory_space=pl.ANY),
        scratch_shapes=[
            pltpu.VMEM(field.shape, BF16),
            pltpu.VMEM(shape, BF16),
            pltpu.VMEM((rows * (2 * count + 1), 128), F32),
            pltpu.VMEM(((count + 2) * rows, 256), BF16),
            pltpu.VMEM((3, 256, 256), BF16),
            pltpu.SemaphoreType.DMA((4,)),
            pltpu.SemaphoreType.DMA((count // 16,)),
        ],
        cost_estimate=pl.CostEstimate(flops=2 * rows * count * 768 * 256, bytes_accessed=1 << 21, transcendentals=0),
        name="first",
    )(field, tiles)


def both_ways(wide_ref, at, x):
    wide_ref[2 * at] = x
    wide_ref[2 * at + 1] = pltpu.roll(x, 64, 1)


def heights_out_kernel(mine_ref, footprint_ref, figure_ref, out_ref, rows_ref, tiles_ref):
    bands, blocks = footprint_ref.shape
    pairs = figure_ref.shape[1] // 128
    for p in range(pairs):
        x = figure_ref[:, p * 128 : (p + 1) * 128].astype(F32)
        rows_ref[pl.ds(2 * p * 9, 8)] = x
        rows_ref[pl.ds((2 * p + 1) * 9, 8)] = pltpu.roll(x, 64, 1)
    for r in range(8):
        tiles_ref[:, r * 128 : (r + 1) * 128] = rows_ref[pl.ds(r, blocks, stride=9)].astype(BF16)
    footprint = footprint_ref[...]
    column = lax.broadcasted_iota(jnp.int32, (bands, blocks), 1)
    code = (column * blocks + (footprint & (blocks - 1))).astype(F32)
    here = (footprint >> (blocks.bit_length() - 1)) == mine_ref[1]
    low = jnp.min(jnp.where(here, code, float(blocks * blocks)), axis=1, keepdims=True).astype(jnp.int32)
    high = jnp.max(jnp.where(here, code, 0.0), axis=1, keepdims=True).astype(jnp.int32)
    picked = []
    for c, chosen in enumerate((low, high)):
        hot = column == ((chosen & (blocks - 1)) ^ c)
        hot = jnp.where(hot, 1.0, 0.0).astype(BF16)
        picked.append(jnp.dot(hot, tiles_ref[...], preferred_element_type=F32))
    lane = lax.broadcasted_iota(jnp.int32, (bands, 128), 1)
    for r in range(8):
        at = slice(r * 128, (r + 1) * 128)
        rows_ref[pl.ds(r, bands, stride=9)] = jnp.where(lane < 64, picked[0][:, at], picked[1][:, at])
    for d in range(bands):
        out_ref[d] = rows_ref[pl.ds(9 * d, 8)].astype(BF16)


def heights_out(mine, footprint, figure):
    bands = footprint.shape[0]
    return pl.pallas_call(
        heights_out_kernel,
        out_shape=jax.ShapeDtypeStruct((bands, 8, 128), BF16),
        grid_spec=pltpu.PrefetchScalarGridSpec(
            num_scalar_prefetch=1,
            grid=(1,),
            in_specs=[
                pl.BlockSpec(footprint.shape, lambda g, mine: (0, 0)),
                pl.BlockSpec((8, figure.shape[1]), lambda g, mine: (mine[0], 0)),
            ],
            out_specs=pl.BlockSpec((bands, 8, 128), lambda g, mine: (0, 0, 0)),
            scratch_shapes=[
                pltpu.VMEM((bands * 9, 128), F32),
                pltpu.VMEM((figure.shape[1] // 64, 8 * 128), BF16),
            ],
        ),
        name="heights_out",
    )(mine, footprint, figure)


def phase_kernel(index_ref, tiles_ref, cos_ref, sin_ref, wide_ref):
    lane = lax.broadcasted_iota(jnp.int32, (8, 128), 1)
    pairs = cos_ref.shape[0]
    for s in range(tiles_ref.shape[0]):
        both_ways(wide_ref, s, tiles_ref[s].astype(F32))

    def pair(p, carry):
        phase = PHASE_FACTOR * jnp.where(lane < 64, wide_ref[index_ref[2 * p]], wide_ref[index_ref[2 * p + 1]])
        cos_ref[p] = jnp.cos(phase)
        sin_ref[p] = jnp.sin(phase)
        return carry

    lax.fori_loop(0, pairs, pair, 0, unroll=4)


def phases(index, tiles):
    bands = tiles.shape[0]
    return pl.pallas_call(
        phase_kernel,
        out_shape=[jax.ShapeDtypeStruct((bands // 2, 8, 128), F32)] * 2,
        in_specs=[pl.BlockSpec(memory_space=pltpu.SMEM), whole()],
        out_specs=[whole(), whole()],
        scratch_shapes=[pltpu.VMEM((2 * bands, 8, 128), F32)],
        compiler_params=pltpu.CompilerParams(vmem_limit_bytes=8 << 20),
        name="phases",
    )(index, tiles)


def second_kernel(index_ref, mine_ref, given_ref, approach_ref, focus_ref, cos_ref, sin_ref, target_ref, out_ref,
                  got_ref, x_ref, y_ref, g_ref, wp_ref, wf_ref, sem):
    pairs = cos_ref.shape[0]
    rows = 64
    parts = 4
    size = 2 * pairs // parts
    loads = [
        pltpu.make_async_copy(
            given_ref.at[:, pl.ds(i * size, size)], got_ref.at[:, pl.ds(i * size, size)], sem.at[i]
        )
        for i in range(parts)
    ]
    for load in loads:
        load.start()
    write_weights(approach_ref, wp_ref, True)
    write_weights(focus_ref, wf_ref, False)
    blank = jnp.zeros((rows, 256), BF16)
    for ref in (x_ref, y_ref, g_ref):
        ref[0:rows] = blank
        ref[(pairs + 1) * rows : (pairs + 2) * rows] = blank

    def fill(p, carry):
        to = pl.ds(pl.multiple_of((p + 1) * rows, 64), rows)
        for h in range(2):
            x = got_ref[:, 2 * p + h].astype(F32).reshape(rows, 128)
            x_ref[to, h * 128 : (h + 1) * 128] = x.astype(BF16)
        return carry

    for i in range(parts):
        loads[i].wait()
        lax.fori_loop(i * pairs // parts, (i + 1) * pairs // parts, fill, 0, unroll=4)
    step = 16

    def mirror(q, carry):
        row = q * (step * rows)
        a2 = banded_rows(x_ref, wp_ref, row, step * rows, rows).astype(BF16).astype(F32)
        re = a2[:, 0:128].reshape(step, 8, 8, 128)
        im = a2[:, 128:256].reshape(step, 8, 8, 128)
        cos = cos_ref[pl.ds(q * step, step)][:, None]
        sin = sin_ref[pl.ds(q * step, step)][:, None]
        to = pl.ds(pl.multiple_of(row + rows, 64), step * rows)
        y_ref[to, 0:128] = (re * cos - im * sin).reshape(step * rows, 128).astype(BF16)
        y_ref[to, 128:256] = (re * sin + im * cos).reshape(step * rows, 128).astype(BF16)
        return carry

    lax.fori_loop(0, pairs // step, mirror, 0)

    def detect(q, carry):
        row = q * (step * rows)
        a4 = banded_rows(y_ref, wf_ref, row, step * rows, rows)
        re = a4[:, 0:128].reshape(step, 8, 8, 128)
        im = a4[:, 128:256].reshape(step, 8, 8, 128)
        power = jnp.sum(re * re + im * im, axis=1)
        to = pl.ds(pl.multiple_of(row + rows, 64), step * rows)
        for t in range(step):
            at = pl.ds(pl.multiple_of((q * step + t) * 128, 128), 128)
            left = (power[t] - target_ref[:, at].astype(F32))[None]
            to = pl.ds(pl.multiple_of(row + rows + t * rows, 64), rows)
            g_ref[to, 0:128] = (re[t] * left).reshape(rows, 128).astype(BF16)
            g_ref[to, 128:256] = (im[t] * left).reshape(rows, 128).astype(BF16)
        return carry

    lax.fori_loop(0, pairs // step, detect, 0)
    lane = lax.broadcasted_iota(jnp.int32, (8, 128), 1)
    out_ref[...] = jnp.zeros_like(out_ref)

    def adjoint(q, carry):
        row = q * (step * rows)
        g3 = banded_rows(g_ref, wf_ref, row, step * rows, rows, flip=True)
        own = pl.ds(pl.multiple_of(row + rows, 64), step * rows)
        re = y_ref[own, 0:128].astype(F32)
        im = y_ref[own, 128:256].astype(F32)
        terms = g3[:, 128:256] * re - g3[:, 0:128] * im
        sens = 2.0 * PHASE_FACTOR * jnp.sum(terms.reshape(step, 8, 8, 128), axis=1)
        for t in range(step):
            turned = pltpu.roll(sens[t], 64, 1)
            for h in range(2):
                j = (q * step + t) * 2 + h
                s, c = index_ref[0, j], index_ref[1, j]
                tile = jnp.where(c != h, turned, sens[t])
                out_ref[s] = jnp.where((lane < 64) == (c == 0), tile, out_ref[s].astype(F32)).astype(BF16)
        return carry

    lax.fori_loop(0, pairs // step, adjoint, 0)


def second_stage(index, mine, got, approach, focus, cos, sin, target):
    bands = got.shape[1]
    pairs = bands // 2
    keep = lambda *shape: pl.BlockSpec(shape, lambda g, index, mine: (0,) * len(shape))
    return pl.pallas_call(
        second_kernel,
        out_shape=jax.ShapeDtypeStruct((bands, 8, 128), BF16),
        grid_spec=pltpu.PrefetchScalarGridSpec(
            num_scalar_prefetch=2,
            grid=(1,),
            in_specs=[
                pl.BlockSpec(memory_space=pl.ANY),
                keep(*approach.shape),
                keep(*focus.shape),
                keep(*cos.shape),
                keep(*sin.shape),
                pl.BlockSpec((8, target.shape[1]), lambda g, index, mine: (mine[0], 0)),
            ],
            out_specs=keep(bands, 8, 128),
            scratch_shapes=[pltpu.VMEM(got.shape, BF16)]
            + [pltpu.VMEM(((pairs + 2) * 64, 256), BF16)] * 3
            + [pltpu.VMEM((3, 256, 256), BF16)] * 2
            + [pltpu.SemaphoreType.DMA((4,))],
        ),
        cost_estimate=pl.CostEstimate(flops=6 * 64 * pairs * 768 * 256, bytes_accessed=1 << 20, transcendentals=0),
        compiler_params=pltpu.CompilerParams(vmem_limit_bytes=24 << 20),
        name="second",
    )(index, mine, got, approach, focus, cos, sin, target)


def collect_kernel(index_ref, given_ref, out_ref, tiles_ref, wide_ref, sem, *sums):
    lane = lax.broadcasted_iota(jnp.int32, (8, 128), 1)
    pairs = out_ref.shape[1] // 128
    bands = tiles_ref.shape[0]
    load = pltpu.make_async_copy(given_ref, tiles_ref, sem)
    load.start()
    for part in sums:
        part[...] = jnp.zeros_like(part)
    load.wait()
    for d in range(bands):
        both_ways(wide_ref, d, tiles_ref[d].astype(F32))
    for d in range(bands):
        for c in range(2):
            part = sums[2 * (d % 2) + c]
            k = index_ref[c, d]
            part[k] += wide_ref[2 * d + ((k & 1) ^ c)]
    for p in range(pairs):
        low = sums[0][2 * p] + sums[1][2 * p] + sums[2][2 * p] + sums[3][2 * p]
        high = sums[0][2 * p + 1] + sums[1][2 * p + 1] + sums[2][2 * p + 1] + sums[3][2 * p + 1]
        out_ref[:, p * 128 : (p + 1) * 128] = jnp.where(lane < 64, low, high).astype(out_ref.dtype)


def collect(index, tiles, dtype):
    bands = tiles.shape[0]
    return pl.pallas_call(
        collect_kernel,
        out_shape=jax.ShapeDtypeStruct((8, bands * 64), dtype),
        in_specs=[pl.BlockSpec(memory_space=pltpu.SMEM), pl.BlockSpec(memory_space=pl.ANY)],
        out_specs=whole(),
        scratch_shapes=[
            pltpu.VMEM(tiles.shape, BF16),
            pltpu.VMEM((2 * bands, 8, 128), F32),
            pltpu.SemaphoreType.DMA,
        ]
        + [pltpu.VMEM((bands + 8, 8, 128), F32)] * 4,
        compiler_params=pltpu.CompilerParams(vmem_limit_bytes=8 << 20),
        name="collect",
    )(index, tiles)


def shards(mode_field, figure, target, footprint, approach_tiles, focus_tiles):
    band = lax.axis_index("band").astype(jnp.int32)
    mine = jnp.stack([lax.axis_index("mode").astype(jnp.int32), band])
    blocks = footprint.shape[1]
    heights = heights_out(mine, footprint, figure)
    heights = lax.all_to_all(heights, "band", split_axis=0, concat_axis=0, tiled=True)
    out = first_stage(mode_field, approach_tiles)
    got = lax.all_to_all(out.reshape(-1, 8, 128), ("mode", "band"), split_axis=0, concat_axis=0, tiled=True)
    got = got.reshape(out.shape)
    source_band = lax.div(footprint, blocks)
    code = lax.broadcasted_iota(jnp.int32, footprint.shape, 1) * blocks + lax.rem(footprint, blocks)
    here = source_band == band
    low = jnp.min(jnp.where(here, code, blocks * blocks), axis=1)
    high = jnp.max(jnp.where(here, code, -1), axis=1)
    add_index = jnp.stack(
        [
            jnp.where(high >= 0, low & (blocks - 1), blocks),
            jnp.where(high > low, high & (blocks - 1), blocks),
        ]
    )
    my_band = lax.dynamic_index_in_dim(source_band, band, 0, keepdims=False)
    column = jnp.arange(blocks, dtype=jnp.int32)
    same = (my_band[:, None] == my_band[None, :]) & (column[None, :] < column[:, None])
    my_slot = jnp.any(same, axis=1).astype(jnp.int32)
    cos, sin = phases(2 * my_band + (my_slot ^ (column & 1)), heights)
    beam_index = jnp.stack([my_band, my_slot])
    tiles = second_stage(beam_index, mine, got, approach_tiles, focus_tiles, cos, sin, target)
    tiles = lax.all_to_all(tiles, "band", split_axis=0, concat_axis=0, tiled=True)
    own = collect(add_index, tiles, BF16)
    return lax.all_gather(own, "mode", axis=0, tiled=True).astype(F32)


def solution(mesh):
    in_specs = (P("mode", "band", None, None), P("band", None), P("band", None), P(), P(), P())
    out_specs = P("band", None)
    return jax.shard_map(shards, mesh=mesh, in_specs=in_specs, out_specs=out_specs, check_vma=False)
```

time: 189 us -> 152 us (0.80)
  starting transfers between devices: 115 us -> 38.4 us
  waiting for transfers between devices: 4.24 us -> 79.5 us
  blocking collectives: 43.3 us -> 16.5 us
  Pallas kernels: 19.1 us -> 14.7 us
    ppermute x18 -> x0, starting transfers between devices: 90.5 us -> none  [moved(): return lax.ppermute(part, 'band', [(b, target(b)) for b in range(bands)])]
    all_to_all x1, waiting for transfers between devices: 0.01 us -> 53.7 us  [shards(): lax.all_to_all(out.reshape(-1, 8, 128), ('mode', 'band'), split_axis=0, c...]
    all_to_all x2 -> x0, blocking collectives: 43.3 us -> none  [the longest x1 23.2 us: shards(): lax.all_to_all(tiles, 'band', split_axis=0, concat_axis=0, tiled=True)]
    all_to_all x0 -> x2, starting transfers between devices: none -> 26.4 us  [the longest x1 19.3 us: shards(): lax.all_to_all(heights, 'band', split_axis=0, concat_axis=0, tiled=True)]
    all_to_all x0 -> x2, waiting for transfers between devices: none -> 25.8 us  [the longest x1 15 us: shards(): lax.all_to_all(tiles, 'band', split_axis=0, concat_axis=0, tiled=True)]
    all_gather x0 -> x1, blocking collectives: none -> 16.5 us  [shards(): return lax.all_gather(own, 'mode', axis=0, tiled=True).astype(F32)]
    all_to_all x1, starting transfers between devices: 24.3 us -> 12 us  [shards(): lax.all_to_all(out.reshape(-1, 8, 128), ('mode', 'band'), split_axis=0, c...]
    ppermute x18 -> x0, waiting for transfers between devices: 4.24 us -> none  [moved(): return lax.ppermute(part, 'band', [(b, target(b)) for b in range(bands)])]
  transfers between devices with their start and end apart: 19 -> 3, of which waited for: 4 -> 3; matrix products, arithmetic and copies ran while one was open for 1% -> 0% of each run, Pallas kernels for 3% -> 4%
where the time goes in v4:
time: 152 us
  waiting for transfers between devices  79.5 us (52%)
  starting transfers between devices  38.4 us (25%)
  blocking collectives  16.5 us (11%)
  Pallas kernels  14.7 us (10%)
  other arithmetic  2.01 us (1%)
    all_to_all x1, waiting for transfers between devices, shards(): lax.all_to_all(out.reshape(-1, 8, 128), ('mode', 'band'), split_axis=0, c...  53.7 us
    all_to_all x1, starting transfers between devices, shards(): lax.all_to_all(heights, 'band', split_axis=0, concat_axis=0, tiled=True)  19.3 us
    all_gather x1, blocking collectives, shards(): return lax.all_gather(own, 'mode', axis=0, tiled=True).astype(F32)  16.5 us
    all_to_all x1, waiting for transfers between devices, shards(): lax.all_to_all(tiles, 'band', split_axis=0, concat_axis=0, tiled=True)  15 us
    all_to_all x1, starting transfers between devices, shards(): lax.all_to_all(out.reshape(-1, 8, 128), ('mode', 'band'), split_axis=0, c...  12 us
    all_to_all x1, waiting for transfers between devices, shards(): lax.all_to_all(heights, 'band', split_axis=0, concat_axis=0, tiled=True)  10.8 us
    all_to_all x1, starting transfers between devices, shards(): lax.all_to_all(tiles, 'band', split_axis=0, concat_axis=0, tiled=True)  7.17 us
    pallas_call x1, Pallas kernels, second_stage(): pl.pallas_call(second_kernel, out_shape=jax.ShapeDtypeStruct((bands, 8, 1...  5.38 us
  transfers between devices with their start and end apart: 3, of which 3 were waited for; matrix products, arithmetic and copies ran while one was open for 0% of the time, Pallas kernels for 4%

profile of v4, /device:TPU:1, one launch (start us, length us, event | category | flops | bytes accessed | tf_op | source)
XLA Modules:
  0.0 151.9 jit_solution(4337351490349796889)
XLA Ops:
  0.0 0.6 pad_add_fusion.2.mine_ref
  0.6 2.5 %heights_out.1 = bf16[64,8,128]{2,1,0:T(8,128)(2,1)} custom-call(s32[2]{0:T(128)} %pad_add_fusion.2.mine_ref, s32[64,64]{1,0:T(8,128)} %footprint_ref.1, bf16[64,4096]{1,0:T(8,128)(2,1)} %figure_ref.1), custom_call_target="tpu_custom_call" | custom-call | tf_op jit(solution)/shard_map/heights_out/pallas_call | solution.py:157
  3.1 19.3 %all-to-all-start.1 = ((bf16[64,8,128]{2,1,0:T(8,128)(2,1)}), bf16[64,8,128]{2,1,0:T(8,128)(2,1)S(1)}, u32[]{:S(2)}, u32[]{:S(2)}) async-start(bf16[64,8,128]{2,1,0:T(8,128)(2,1)} %heights_out.1), calls=%async_computation.1 | async-start | bytes 262144 | tf_op jit(solution)/shard_map/all_to_all | solution.py:366
  22.4 4.3 %first.1 = bf16[8,64,8,128]{3,2,1,0:T(8,128)(2,1)} custom-call(bf16[4096,128]{1,0:T(8,128)(2,1)} %bitcast.20, bf16[3,2,128,128]{3,2,1,0:T(8,128)(2,1)} %approach_ref.1), custom_call_target="tpu_custom_call" | custom-call | flops 805306368 | bytes 2097152 | tf_op jit(solution)/shard_map/first/pallas_call | solution.py:103
  26.7 10.8 %all-to-all-done.1.tiles_ref = bf16[64,8,128]{2,1,0:T(8,128)(2,1)S(1)} async-done(((bf16[64,8,128]{2,1,0:T(8,128)(2,1)}), bf16[64,8,128]{2,1,0:T(8,128)(2,1)S(1)}, u32[]{:S(2)}, u32[]{:S(2)}) %all-to-all-start.1) | async-done | bytes 131104 | tf_op jit(solution)/shard_map/all_to_all | solution.py:366
  37.4 0.0 copy-start.4
  37.5 0.0 copy-start.1
  37.5 12.0 %all-to-all-start = ((bf16[512,8,128]{2,1,0:T(8,128)(2,1)}), bf16[512,8,128]{2,1,0:T(8,128)(2,1)S(1)}, u32[]{:S(2)}, u32[]{:S(2)}) async-start(bf16[512,8,128]{2,1,0:T(8,128)(2,1)} %bitcast.19), calls=%async_computation | async-start | bytes 2097152 | tf_op jit(solution)/shard_map/all_to_all | solution.py:368
  49.4 0.0 copy-start.2
  49.4 0.0 copy-done.4
  49.4 0.1 select_reduce_fusion
  49.6 0.2 fusion.2
  49.8 1.3 phases.1
  51.1 53.7 %all-to-all-done = bf16[512,8,128]{2,1,0:T(8,128)(2,1)S(1)} async-done(((bf16[512,8,128]{2,1,0:T(8,128)(2,1)}), bf16[512,8,128]{2,1,0:T(8,128)(2,1)S(1)}, u32[]{:S(2)}, u32[]{:S(2)}) %all-to-all-start) | async-done | bytes 1048608 | tf_op jit(solution)/shard_map/all_to_all | solution.py:368
  104.8 0.0 copy-done.1
  104.8 0.0 copy-done.3
  104.8 0.0 copy-done.2
  104.8 0.6 copy-done
  105.5 5.4 %second.1 = bf16[64,8,128]{2,1,0:T(8,128)(2,1)} custom-call(s32[2,64]{1,0:T(2,128)S(1)} %pad_add_fusion.1.index_ref, s32[2]{0:T(128)S(1)} %copy-done, bf16[8,64,8,128]{3,2,1,0:T(8,128)(2,1)S(1)} %bitcast.18, bf16[3,2,128,128]{3,2,1,0:T(8,128)(2,1)S(1)} %copy-done.2, bf16[3,2,128,128]{3,2,1,0:T(8,128)(2,1)S(1)} %copy-done.3, ...), custom_call_target="tpu_custom_call" | custom-call | flops 2415919104 | bytes 1048576 | tf_op jit(solution)/shard_map/second/pallas_call | solution.py:295
  110.8 7.2 %all-to-all-start.2 = ((bf16[64,8,128]{2,1,0:T(8,128)(2,1)}), bf16[64,8,128]{2,1,0:T(8,128)(2,1)S(1)}, u32[]{:S(2)}, u32[]{:S(2)}) async-start(bf16[64,8,128]{2,1,0:T(8,128)(2,1)} %second.1), calls=%async_computation.2 | async-start | bytes 262144 | tf_op jit(solution)/shard_map/all_to_all | solution.py:388
  118.1 15.0 %all-to-all-done.2.given_ref = bf16[64,8,128]{2,1,0:T(8,128)(2,1)S(1)} async-done(((bf16[64,8,128]{2,1,0:T(8,128)(2,1)}), bf16[64,8,128]{2,1,0:T(8,128)(2,1)S(1)}, u32[]{:S(2)}, u32[]{:S(2)}) %all-to-all-start.2) | async-done | bytes 131104 | tf_op jit(solution)/shard_map/all_to_all | solution.py:388
  133.1 1.2 collect.1
  134.3 16.5 %all_gather.3 = bf16[64,4096]{1,0:T(8,128)(2,1)S(1)} all-gather(bf16[8,4096]{1,0:T(8,128)(2,1)S(1)} %collect.1), channel_id=1, replica_groups=mesh['mode'=8,'band'=64] {'mode'}, dimensions={0}, use_global_device_ids=true | all-gather | bytes 589824 | tf_op jit(solution)/shard_map/all_gather | solution.py:390
  150.9 1.0 convert_element_type.21
  (10 shorter events, 0.1 us)
Async XLA Ops:
  3.1 34.3 %all-to-all-start.1 = ((bf16[64,8,128]{2,1,0:T(8,128)(2,1)}), bf16[64,8,128]{2,1,0:T(8,128)(2,1)S(1)}, u32[]{:S(2)}, u32[]{:S(2)}) async-start(bf16[64,8,128]{2,1,0:T(8,128)(2,1)} %heights_out.1), calls=%async_computation.1 | async-start | bytes 262144 | tf_op jit(solution)/shard_map/all_to_all | solution.py:366
  37.4 12.0 %copy-start.4 = (s32[64,64]{1,0:T(8,128)S(1)}, s32[64,64]{1,0:T(8,128)}, u32[]{:S(2)}) copy-start(s32[64,64]{1,0:T(8,128)} %footprint_ref.1) | copy-start | bytes 49156
  37.5 67.4 %copy-start.1 = (bf16[64,4096]{1,0:T(8,128)(2,1)S(1)}, bf16[64,4096]{1,0:T(8,128)(2,1)}, u32[]{:S(2)}) copy-start(bf16[64,4096]{1,0:T(8,128)(2,1)} %target_ref.1) | copy-start | bytes 1572868
  37.5 67.4 %copy-start.3 = (bf16[3,2,128,128]{3,2,1,0:T(8,128)(2,1)S(1)}, bf16[3,2,128,128]{3,2,1,0:T(8,128)(2,1)}, u32[]{:S(2)}) copy-start(bf16[3,2,128,128]{3,2,1,0:T(8,128)(2,1)} %focus_ref.1) | copy-start | bytes 589828
  37.5 67.4 %all-to-all-start = ((bf16[512,8,128]{2,1,0:T(8,128)(2,1)}), bf16[512,8,128]{2,1,0:T(8,128)(2,1)S(1)}, u32[]{:S(2)}, u32[]{:S(2)}) async-start(bf16[512,8,128]{2,1,0:T(8,128)(2,1)} %bitcast.19), calls=%async_computation | async-start | bytes 2097152 | tf_op jit(solution)/shard_map/all_to_all | solution.py:368
  49.4 55.4 %copy-start.2 = (bf16[3,2,128,128]{3,2,1,0:T(8,128)(2,1)S(1)}, bf16[3,2,128,128]{3,2,1,0:T(8,128)(2,1)}, u32[]{:S(2)}) copy-start(bf16[3,2,128,128]{3,2,1,0:T(8,128)(2,1)} %approach_ref.1) | copy-start | bytes 589828
  104.8 0.6 copy-start
  110.8 22.2 %all-to-all-start.2 = ((bf16[64,8,128]{2,1,0:T(8,128)(2,1)}), bf16[64,8,128]{2,1,0:T(8,128)(2,1)S(1)}, u32[]{:S(2)}, u32[]{:S(2)}) async-start(bf16[64,8,128]{2,1,0:T(8,128)(2,1)} %second.1), calls=%async_computation.2 | async-start | bytes 262144 | tf_op jit(solution)/shard_map/all_to_all | solution.py:388

commit v5 on v4

v5 whole, which is shorter than its diff:
```python
import functools

import jax
import jax.numpy as jnp
from jax import lax
from jax.experimental import pallas as pl
from jax.experimental.pallas import tpu as pltpu
from jax.sharding import PartitionSpec as P

TILE = 128
HALF = 64
MIRROR_TILE = 64
PHASE_FACTOR = 4.0
F32 = jnp.float32
BF16 = jnp.bfloat16


def whole(*_):
    return pl.BlockSpec(memory_space=pltpu.VMEM)


def write_weights(tiles_ref, w_ref, split):
    for o in range(3):
        re = tiles_ref[o, 0].astype(F32)
        im = tiles_ref[o, 1].astype(F32)
        upper = jnp.concatenate([re, im], axis=1).astype(BF16)
        lower = jnp.concatenate([-im, re], axis=1).astype(BF16)
        if split:
            w_ref[o, 0:64] = upper[0:64]
            w_ref[o, 64:128] = lower[0:64]
            w_ref[o, 128:192] = upper[64:128]
            w_ref[o, 192:256] = lower[64:128]
        else:
            w_ref[o, 0:128] = upper
            w_ref[o, 128:256] = lower


def banded_rows(x_ref, w_ref, row, count, rows, flip=False):
    total = None
    for o in range(3):
        x = x_ref[pl.ds(pl.multiple_of(row + o * rows, 64), count)]
        if flip:
            part = lax.dot_general(x, w_ref[2 - o], (((1,), (1,)), ((), ())), preferred_element_type=F32)
        else:
            part = jnp.dot(x, w_ref[o], preferred_element_type=F32)
        total = part if total is None else total + part
    return total


def first_kernel(field_ref, tiles_ref, footprint_ref, figure_ref, out_ref, field_buf, figure_buf, out_buf, wide_ref,
                 spread_ref, rows_ref, pick_ref, chunk_ref, x_ref, w_ref, in_sem, out_sem):
    count_tiles = field_ref.shape[0] // 128
    bands, blocks = footprint_ref.shape
    rows = 64
    pitch = 2 * count_tiles + 1
    parts = 4
    lines = rows // parts
    size = lines * 2 * count_tiles
    figure_load = pltpu.make_async_copy(figure_ref, figure_buf, in_sem.at[parts])
    figure_load.start()
    loads = [
        pltpu.make_async_copy(
            field_ref.at[pl.ds(i * size, size)], field_buf.at[pl.ds(i * size, size)], in_sem.at[i]
        )
        for i in range(parts)
    ]
    for load in loads:
        load.start()
    write_weights(tiles_ref, w_ref, False)
    x_ref[0:rows] = jnp.zeros((rows, 256), BF16)
    x_ref[(count_tiles + 1) * rows : (count_tiles + 2) * rows] = jnp.zeros((rows, 256), BF16)
    chunk_ref[pl.ds(9, 8 * bands, stride=10)] = jnp.zeros((8 * bands, 128), F32)

    mode, band = lax.axis_index("mode"), lax.axis_index("band")
    figure_load.wait()
    for p in range(blocks // 2):
        x = figure_buf[:, p * 128 : (p + 1) * 128].astype(F32)
        for g in range(8):
            spread_ref[pl.ds(p * 72 + g * 9, 8)] = x[g * 8 : (g + 1) * 8]
        mine = spread_ref[pl.ds(p * 72 + mode, 8, stride=9)]
        rows_ref[pl.ds(2 * p * 9, 8)] = mine
        rows_ref[pl.ds((2 * p + 1) * 9, 8)] = pltpu.roll(mine, 64, 1)
    for i in range(8):
        pick_ref[:, i * 128 : (i + 1) * 128] = rows_ref[pl.ds(i, blocks, stride=9)].astype(BF16)
    footprint = footprint_ref[...]
    column = lax.broadcasted_iota(jnp.int32, (bands, blocks), 1)
    code = (column * blocks + (footprint & (blocks - 1))).astype(F32)
    here = (footprint >> (blocks.bit_length() - 1)) == band
    low = jnp.min(jnp.where(here, code, float(blocks * blocks)), axis=1, keepdims=True).astype(jnp.int32)
    high = jnp.max(jnp.where(here, code, 0.0), axis=1, keepdims=True).astype(jnp.int32)
    picked = []
    for c, chosen in enumerate((low, high)):
        hot = column == ((chosen & (blocks - 1)) ^ c)
        hot = jnp.where(hot, 1.0, 0.0).astype(BF16)
        picked.append(jnp.dot(hot, pick_ref[...], preferred_element_type=F32))
    lane = lax.broadcasted_iota(jnp.int32, (bands, 128), 1)
    for i in range(8):
        at = slice(i * 128, (i + 1) * 128)
        chunk_ref[pl.ds(i * bands * 10 + 8, bands, stride=10)] = jnp.where(lane < 64, picked[0][:, at], picked[1][:, at])

    for u in range(rows):
        if u % lines == 0:
            loads[u // lines].wait()
        wide_ref[u * pitch : u * pitch + 2 * count_tiles] = field_buf[
            u * 2 * count_tiles : (u + 1) * 2 * count_tiles
        ].astype(F32)
    for j in range(count_tiles):
        for c in range(2):
            x_ref[(j + 1) * rows : (j + 2) * rows, c * 128 : (c + 1) * 128] = wide_ref[
                pl.ds(2 * j + c, rows, stride=pitch)
            ].astype(BF16)
    step = 16
    stores = []
    for q in range(count_tiles // step):
        got = banded_rows(x_ref, w_ref, q * (step * rows), step * rows, rows)
        for t in range(step):
            mine = got[t * rows : (t + 1) * rows]
            stacked = jnp.concatenate([mine[:, 0:128], mine[:, 128:256]], axis=0)
            turned = jnp.transpose(stacked)
            at = (q * step + t) * 2
            for h in range(2):
                for i in range(8):
                    from_row = h * 64 + i * 8
                    chunk_ref[pl.ds((i * bands + at + h) * 10, 8)] = turned[from_row : from_row + 8]
        span = 2 * step * 10
        for i in range(8):
            at = i * bands * 10 + q * span
            out_buf[at : at + span] = chunk_ref[at : at + span].astype(BF16)
            store = pltpu.make_async_copy(
                out_buf.at[pl.ds(at, span)], out_ref.at[pl.ds(at, span)], out_sem.at[q * 8 + i]
            )
            store.start()
            stores.append(store)
    for store in stores:
        store.wait()


def first_stage(field, tiles, footprint, figure):
    rows, length = field.shape[1], field.shape[3]
    count = length // TILE
    bands, blocks = footprint.shape
    field = field.reshape(rows, 2, count, TILE).transpose(0, 2, 1, 3).reshape(rows * count * 2, TILE)
    shape = (8 * bands * 10, TILE)
    return pl.pallas_call(
        first_kernel,
        out_shape=jax.ShapeDtypeStruct(shape, BF16),
        in_specs=[pl.BlockSpec(memory_space=pl.ANY), whole(), whole(), pl.BlockSpec(memory_space=pl.ANY)],
        out_specs=pl.BlockSpec(memory_space=pl.ANY),
        scratch_shapes=[
            pltpu.VMEM(field.shape, BF16),
            pltpu.VMEM(figure.shape, BF16),
            pltpu.VMEM(shape, BF16),
            pltpu.VMEM((rows * (2 * count + 1), 128), F32),
            pltpu.VMEM((blocks // 2 * 72, 128), F32),
            pltpu.VMEM((blocks * 9, 128), F32),
            pltpu.VMEM((blocks, 8 * 128), BF16),
            pltpu.VMEM(shape, F32),
            pltpu.VMEM(((count + 2) * rows, 256), BF16),
            pltpu.VMEM((3, 256, 256), BF16),
            pltpu.SemaphoreType.DMA((5,)),
            pltpu.SemaphoreType.DMA((8 * (count // 16),)),
        ],
        cost_estimate=pl.CostEstimate(flops=2 * rows * count * 768 * 256, bytes_accessed=1 << 21, transcendentals=0),
        name="first",
    )(field, tiles, footprint, figure)


def both_ways(wide_ref, at, x):
    wide_ref[2 * at] = x
    wide_ref[2 * at + 1] = pltpu.roll(x, 64, 1)


def second_kernel(index_ref, given_ref, approach_ref, focus_ref, target_ref, out_ref,
                  got_ref, wide_ref, heights_ref, cos_ref, sin_ref, want_ref, x_ref, y_ref, g_ref, wp_ref, wf_ref, sem):
    pairs = cos_ref.shape[0]
    bands = 2 * pairs
    rows = 64
    parts = 4
    size = given_ref.shape[0] // parts
    loads = [
        pltpu.make_async_copy(given_ref.at[pl.ds(i * size, size)], got_ref.at[pl.ds(i * size, size)], sem.at[i])
        for i in range(parts)
    ]
    mode = lax.axis_index("mode")
    loads.append(
        pltpu.make_async_copy(target_ref.at[pl.ds(pl.multiple_of(mode * 8, 8), 8)], want_ref, sem.at[parts])
    )
    for load in loads:
        load.start()
    write_weights(approach_ref, wp_ref, True)
    write_weights(focus_ref, wf_ref, False)
    blank = jnp.zeros((rows, 256), BF16)
    for ref in (x_ref, y_ref, g_ref):
        ref[0:rows] = blank
        ref[(pairs + 1) * rows : (pairs + 2) * rows] = blank
    for i in range(parts):
        loads[i].wait()
        wide_ref[i * size : (i + 1) * size] = got_ref[i * size : (i + 1) * size].astype(F32)
    loads[parts].wait()

    for p in range(pairs):
        for h in range(2):
            x = [wide_ref[pl.ds((m * bands + 2 * p + h) * 10, 8)] for m in range(8)]
            x_ref[(p + 1) * rows : (p + 2) * rows, h * 128 : (h + 1) * 128] = jnp.concatenate(x, axis=0).astype(BF16)
    for s in range(bands):
        both_ways(heights_ref, s, wide_ref[pl.ds(s * 10 + 8, 8, stride=bands * 10)])
    lane = lax.broadcasted_iota(jnp.int32, (8, 128), 1)

    def mirror_pair(p, carry):
        a, b = heights_ref[index_ref[2, 2 * p]], heights_ref[index_ref[2, 2 * p + 1]]
        phase = PHASE_FACTOR * jnp.where(lane < 64, a, b)
        cos_ref[p] = jnp.cos(phase)
        sin_ref[p] = jnp.sin(phase)
        return carry

    lax.fori_loop(0, pairs, mirror_pair, 0, unroll=4)
    step = 16

    def mirror(q, carry):
        row = q * (step * rows)
        a2 = banded_rows(x_ref, wp_ref, row, step * rows, rows).astype(BF16).astype(F32)
        re = a2[:, 0:128].reshape(step, 8, 8, 128)
        im = a2[:, 128:256].reshape(step, 8, 8, 128)
        cos = cos_ref[pl.ds(q * step, step)][:, None]
        sin = sin_ref[pl.ds(q * step, step)][:, None]
        to = pl.ds(pl.multiple_of(row + rows, 64), step * rows)
        y_ref[to, 0:128] = (re * cos - im * sin).reshape(step * rows, 128).astype(BF16)
        y_ref[to, 128:256] = (re * sin + im * cos).reshape(step * rows, 128).astype(BF16)
        return carry

    lax.fori_loop(0, pairs // step, mirror, 0)

    def detect(q, carry):
        row = q * (step * rows)
        a4 = banded_rows(y_ref, wf_ref, row, step * rows, rows)
        re = a4[:, 0:128].reshape(step, 8, 8, 128)
        im = a4[:, 128:256].reshape(step, 8, 8, 128)
        power = jnp.sum(re * re + im * im, axis=1)
        to = pl.ds(pl.multiple_of(row + rows, 64), step * rows)
        for t in range(step):
            at = pl.ds(pl.multiple_of((q * step + t) * 128, 128), 128)
            left = (power[t] - want_ref[:, at].astype(F32))[None]
            to = pl.ds(pl.multiple_of(row + rows + t * rows, 64), rows)
            g_ref[to, 0:128] = (re[t] * left).reshape(rows, 128).astype(BF16)
            g_ref[to, 128:256] = (im[t] * left).reshape(rows, 128).astype(BF16)
        return carry

    lax.fori_loop(0, pairs // step, detect, 0)
    out_ref[...] = jnp.zeros_like(out_ref)

    def adjoint(q, carry):
        row = q * (step * rows)
        g3 = banded_rows(g_ref, wf_ref, row, step * rows, rows, flip=True)
        own = pl.ds(pl.multiple_of(row + rows, 64), step * rows)
        re = y_ref[own, 0:128].astype(F32)
        im = y_ref[own, 128:256].astype(F32)
        terms = g3[:, 128:256] * re - g3[:, 0:128] * im
        sens = 2.0 * PHASE_FACTOR * jnp.sum(terms.reshape(step, 8, 8, 128), axis=1)
        for t in range(step):
            turned = pltpu.roll(sens[t], 64, 1)
            for h in range(2):
                j = (q * step + t) * 2 + h
                s, c = index_ref[0, j], index_ref[1, j]
                tile = jnp.where(c != h, turned, sens[t])
                out_ref[s] = jnp.where((lane < 64) == (c == 0), tile, out_ref[s].astype(F32)).astype(BF16)
        return carry

    lax.fori_loop(0, pairs // step, adjoint, 0)


def second_stage(index, got, approach, focus, target, bands):
    pairs = bands // 2
    anywhere = pl.BlockSpec(memory_space=pl.ANY)
    return pl.pallas_call(
        second_kernel,
        out_shape=jax.ShapeDtypeStruct((bands, 8, 128), BF16),
        in_specs=[pl.BlockSpec(memory_space=pltpu.SMEM), anywhere, whole(), whole(), anywhere],
        out_specs=whole(),
        scratch_shapes=[
            pltpu.VMEM(got.shape, BF16),
            pltpu.VMEM(got.shape, F32),
            pltpu.VMEM((2 * bands, 8, 128), F32),
            pltpu.VMEM((pairs, 8, 128), F32),
            pltpu.VMEM((pairs, 8, 128), F32),
            pltpu.VMEM((8, target.shape[1]), BF16),
        ]
        + [pltpu.VMEM(((pairs + 2) * 64, 256), BF16)] * 3
        + [pltpu.VMEM((3, 256, 256), BF16)] * 2
        + [pltpu.SemaphoreType.DMA((5,))],
        cost_estimate=pl.CostEstimate(flops=6 * 64 * pairs * 768 * 256, bytes_accessed=1 << 20, transcendentals=0),
        compiler_params=pltpu.CompilerParams(vmem_limit_bytes=32 << 20),
        name="second",
    )(index, got, approach, focus, target)


def collect_kernel(index_ref, given_ref, out_ref, tiles_ref, wide_ref, sem, *sums):
    lane = lax.broadcasted_iota(jnp.int32, (8, 128), 1)
    pairs = out_ref.shape[1] // 128
    bands = tiles_ref.shape[0]
    load = pltpu.make_async_copy(given_ref, tiles_ref, sem)
    load.start()
    for part in sums:
        part[...] = jnp.zeros_like(part)
    load.wait()
    for d in range(bands):
        both_ways(wide_ref, d, tiles_ref[d].astype(F32))
    for d in range(bands):
        for c in range(2):
            part = sums[2 * (d % 2) + c]
            k = index_ref[c, d]
            part[k] += wide_ref[2 * d + ((k & 1) ^ c)]
    for p in range(pairs):
        low = sums[0][2 * p] + sums[1][2 * p] + sums[2][2 * p] + sums[3][2 * p]
        high = sums[0][2 * p + 1] + sums[1][2 * p + 1] + sums[2][2 * p + 1] + sums[3][2 * p + 1]
        out_ref[:, p * 128 : (p + 1) * 128] = jnp.where(lane < 64, low, high).astype(out_ref.dtype)


def collect(index, tiles, dtype):
    bands = tiles.shape[0]
    return pl.pallas_call(
        collect_kernel,
        out_shape=jax.ShapeDtypeStruct((8, bands * 64), dtype),
        in_specs=[pl.BlockSpec(memory_space=pltpu.SMEM), pl.BlockSpec(memory_space=pl.ANY)],
        out_specs=whole(),
        scratch_shapes=[
            pltpu.VMEM(tiles.shape, BF16),
            pltpu.VMEM((2 * bands, 8, 128), F32),
            pltpu.SemaphoreType.DMA,
        ]
        + [pltpu.VMEM((bands + 8, 8, 128), F32)] * 4,
        compiler_params=pltpu.CompilerParams(vmem_limit_bytes=8 << 20),
        name="collect",
    )(index, tiles)


def shards(mode_field, figure, target, footprint, approach_tiles, focus_tiles):
    band = lax.axis_index("band").astype(jnp.int32)
    bands, blocks = footprint.shape
    out = first_stage(mode_field, approach_tiles, footprint, figure)
    sent = out.reshape(-1, 5, 2, TILE).transpose(0, 2, 1, 3).reshape(-1, 2, 5 * TILE)
    got = lax.all_to_all(sent, ("mode", "band"), split_axis=0, concat_axis=0, tiled=True)
    got = got.reshape(-1, 2, 5, TILE).transpose(0, 2, 1, 3).reshape(out.shape)
    source_band = lax.div(footprint, blocks)
    code = lax.broadcasted_iota(jnp.int32, footprint.shape, 1) * blocks + lax.rem(footprint, blocks)
    here = source_band == band
    low = jnp.min(jnp.where(here, code, blocks * blocks), axis=1)
    high = jnp.max(jnp.where(here, code, -1), axis=1)
    add_index = jnp.stack(
        [
            jnp.where(high >= 0, low & (blocks - 1), blocks),
            jnp.where(high > low, high & (blocks - 1), blocks),
        ]
    )
    my_band = lax.dynamic_index_in_dim(source_band, band, 0, keepdims=False)
    column = jnp.arange(blocks, dtype=jnp.int32)
    same = (my_band[:, None] == my_band[None, :]) & (column[None, :] < column[:, None])
    my_slot = jnp.any(same, axis=1).astype(jnp.int32)
    beam_index = jnp.stack([my_band, my_slot, 2 * my_band + (my_slot ^ (column & 1))])
    tiles = second_stage(beam_index, got, approach_tiles, focus_tiles, target, bands)
    tiles = lax.all_to_all(tiles, "band", split_axis=0, concat_axis=0, tiled=True)
    own = collect(add_index, tiles, BF16)
    return lax.all_gather(own, "mode", axis=0, tiled=True).astype(F32)


def solution(mesh):
    in_specs = (P("mode", "band", None, None), P("band", None), P("band", None), P(), P(), P())
    out_specs = P("band", None)
    return jax.shard_map(shards, mesh=mesh, in_specs=in_specs, out_specs=out_specs, check_vma=False)
```

time: 152 us -> 144 us (0.947)
  starting transfers between devices: 38.4 us -> 31.3 us
  waiting for transfers between devices: 79.5 us -> 81.2 us
    all_to_all x2 -> x1, starting transfers between devices: 31.2 us -> 24.3 us  [shards(): lax.all_to_all(sent, ('mode', 'band'), split_axis=0, concat_axis=0, tiled...]
    pallas_call x2 -> x0, Pallas kernels: 3.79 us -> none  [the longest x1 2.5 us: heights_out(): pl.pallas_call(heights_out_kernel, out_shape=jax.ShapeDtypeStruct((bands,...]
    all_to_all x2 -> x1, waiting for transfers between devices: 64.4 us -> 66.1 us  [shards(): lax.all_to_all(sent, ('mode', 'band'), split_axis=0, concat_axis=0, tiled...]
  transfers between devices with their start and end apart: 3 -> 2, of which waited for: 3 -> 2; matrix products, arithmetic and copies ran while one was open for 0% -> 0% of each run, Pallas kernels for 4% -> 0%
where the time goes in v5:
time: 144 us
  waiting for transfers between devices  81.2 us (56%)
  starting transfers between devices  31.3 us (22%)
  blocking collectives  16.4 us (11%)
  Pallas kernels  13.3 us (9%)
    all_to_all x1, waiting for transfers between devices, shards(): lax.all_to_all(sent, ('mode', 'band'), split_axis=0, concat_axis=0, tiled...  66.1 us
    all_to_all x1, starting transfers between devices, shards(): lax.all_to_all(sent, ('mode', 'band'), split_axis=0, concat_axis=0, tiled...  24.3 us
    all_gather x1, blocking collectives, shards(): return lax.all_gather(own, 'mode', axis=0, tiled=True).astype(F32)  16.4 us
    all_to_all x1, waiting for transfers between devices, shards(): lax.all_to_all(tiles, 'band', split_axis=0, concat_axis=0, tiled=True)  15.1 us
    all_to_all x1, starting transfers between devices, shards(): lax.all_to_all(tiles, 'band', split_axis=0, concat_axis=0, tiled=True)  7.03 us
    pallas_call x1, Pallas kernels, second_stage(): pl.pallas_call(second_kernel, out_shape=jax.ShapeDtypeStruct((bands, 8, 1...  6.82 us
    pallas_call x1, Pallas kernels, first_stage(): pl.pallas_call(first_kernel, out_shape=jax.ShapeDtypeStruct(shape, BF16),...  5.28 us
  transfers between devices with their start and end apart: 2, of which 2 were waited for; matrix products, arithmetic and copies ran while one was open for 0% of the time, Pallas kernels for 0%

profile of v5, /device:TPU:1, one launch (start us, length us, event | category | flops | bytes accessed | tf_op | source)
XLA Modules:
  0.0 143.9 jit_solution(1608880768090763169)
XLA Ops:
  0.0 5.3 %first.1 = bf16[5120,128]{1,0:T(8,128)(2,1)} custom-call(bf16[4096,128]{1,0:T(8,128)(2,1)} %bitcast.27, bf16[3,2,128,128]{3,2,1,0:T(8,128)(2,1)} %approach_ref.1, s32[64,64]{1,0:T(8,128)} %footprint_ref.1, bf16[64,4096]{1,0:T(8,128)(2,1)} %figure_ref.1), custom_call_target="tpu_custom_call" | custom-call | flops 805306368 | bytes 2097152 | tf_op jit(solution)/shard_map/first/pallas_call | solution.py:144
  5.3 0.0 copy-start.3
  5.3 0.0 copy-start
  5.3 0.0 copy-start.1
  5.3 0.0 copy-start.2
  5.3 24.3 %all-to-all-start = ((bf16[512,2,640]{2,1,0:T(2,128)(2,1)}), bf16[512,2,640]{2,1,0:T(2,128)(2,1)S(1)}, u32[]{:S(2)}, u32[]{:S(2)}) async-start(bf16[512,2,640]{2,1,0:T(2,128)(2,1)} %bitcast.26), calls=%async_computation | async-start | bytes 2621440 | tf_op jit(solution)/shard_map/all_to_all | solution.py:341
  29.7 0.0 copy-done.3
  29.7 0.1 select_reduce_fusion
  29.8 0.2 fusion.2
  30.1 66.1 %all-to-all-done = bf16[512,2,640]{2,1,0:T(2,128)(2,1)S(1)} async-done(((bf16[512,2,640]{2,1,0:T(2,128)(2,1)}), bf16[512,2,640]{2,1,0:T(2,128)(2,1)S(1)}, u32[]{:S(2)}, u32[]{:S(2)}) %all-to-all-start) | async-done | bytes 1310752 | tf_op jit(solution)/shard_map/all_to_all | solution.py:341
  96.1 0.0 copy-done
  96.2 0.0 copy-done.1
  96.2 0.0 copy-done.2
  96.2 6.8 %second.1 = bf16[64,8,128]{2,1,0:T(8,128)(2,1)} custom-call(s32[3,64]{1,0:T(4,128)S(1)} %pad_add_fusion.index_ref, bf16[5120,128]{1,0:T(8,128)(2,1)S(1)} %bitcast.25, bf16[3,2,128,128]{3,2,1,0:T(8,128)(2,1)S(1)} %copy-done, bf16[3,2,128,128]{3,2,1,0:T(8,128)(2,1)S(1)} %copy-done.2, bf16[64,4096]{1,0:T(8,128)(2,1)S(1)} %copy-done.1), custom_call_target="tpu_custom_call" | custom-call | flops 2415919104 | bytes 1048576 | tf_op jit(solution)/shard_map/second/pallas_call | solution.py:274
  103.0 7.0 %all-to-all-start.1 = ((bf16[64,8,128]{2,1,0:T(8,128)(2,1)}), bf16[64,8,128]{2,1,0:T(8,128)(2,1)S(1)}, u32[]{:S(2)}, u32[]{:S(2)}) async-start(bf16[64,8,128]{2,1,0:T(8,128)(2,1)} %second.1), calls=%async_computation.1 | async-start | bytes 262144 | tf_op jit(solution)/shard_map/all_to_all | solution.py:360
  110.1 15.1 %all-to-all-done.1.given_ref = bf16[64,8,128]{2,1,0:T(8,128)(2,1)S(1)} async-done(((bf16[64,8,128]{2,1,0:T(8,128)(2,1)}), bf16[64,8,128]{2,1,0:T(8,128)(2,1)S(1)}, u32[]{:S(2)}, u32[]{:S(2)}) %all-to-all-start.1) | async-done | bytes 131104 | tf_op jit(solution)/shard_map/all_to_all | solution.py:360
  125.2 1.2 collect.1
  126.4 16.4 %all_gather.3 = bf16[64,4096]{1,0:T(8,128)(2,1)S(1)} all-gather(bf16[8,4096]{1,0:T(8,128)(2,1)S(1)} %collect.1), channel_id=1, replica_groups=mesh['mode'=8,'band'=64] {'mode'}, dimensions={0}, use_global_device_ids=true | all-gather | bytes 589824 | tf_op jit(solution)/shard_map/all_gather | solution.py:362
  142.9 1.0 convert_element_type.22
  (8 shorter events, 0.1 us)
Async XLA Ops:
  5.3 24.4 %copy-start.3 = (s32[64,64]{1,0:T(8,128)S(1)}, s32[64,64]{1,0:T(8,128)}, u32[]{:S(2)}) copy-start(s32[64,64]{1,0:T(8,128)} %footprint_ref.1) | copy-start | bytes 49156
  5.3 90.9 %copy-start = (bf16[3,2,128,128]{3,2,1,0:T(8,128)(2,1)S(1)}, bf16[3,2,128,128]{3,2,1,0:T(8,128)(2,1)}, u32[]{:S(2)}) copy-start(bf16[3,2,128,128]{3,2,1,0:T(8,128)(2,1)} %approach_ref.1) | copy-start | bytes 589828
  5.3 90.8 %copy-start.1 = (bf16[64,4096]{1,0:T(8,128)(2,1)S(1)}, bf16[64,4096]{1,0:T(8,128)(2,1)}, u32[]{:S(2)}) copy-start(bf16[64,4096]{1,0:T(8,128)(2,1)} %target_ref.1) | copy-start | bytes 1572868
  5.3 90.8 %copy-start.2 = (bf16[3,2,128,128]{3,2,1,0:T(8,128)(2,1)S(1)}, bf16[3,2,128,128]{3,2,1,0:T(8,128)(2,1)}, u32[]{:S(2)}) copy-start(bf16[3,2,128,128]{3,2,1,0:T(8,128)(2,1)} %focus_ref.1) | copy-start | bytes 589828
  5.3 90.8 %all-to-all-start = ((bf16[512,2,640]{2,1,0:T(2,128)(2,1)}), bf16[512,2,640]{2,1,0:T(2,128)(2,1)S(1)}, u32[]{:S(2)}, u32[]{:S(2)}) async-start(bf16[512,2,640]{2,1,0:T(2,128)(2,1)} %bitcast.26), calls=%async_computation | async-start | bytes 2621440 | tf_op jit(solution)/shard_map/all_to_all | solution.py:341
  103.0 22.2 %all-to-all-start.1 = ((bf16[64,8,128]{2,1,0:T(8,128)(2,1)}), bf16[64,8,128]{2,1,0:T(8,128)(2,1)S(1)}, u32[]{:S(2)}, u32[]{:S(2)}) async-start(bf16[64,8,128]{2,1,0:T(8,128)(2,1)} %second.1), calls=%async_computation.1 | async-start | bytes 262144 | tf_op jit(solution)/shard_map/all_to_all | solution.py:360

commit v6 on v5

--- a/solution.py
+++ b/solution.py
@@ -13,6 +13,10 @@
 PHASE_FACTOR = 4.0
 F32 = jnp.float32
 BF16 = jnp.bfloat16
+
+
+def place(mode, band, modes, bands):
+    return (mode + modes // 2) % modes * bands + (band + bands // 2) % bands
 
 
 def whole(*_):
@@ -96,7 +100,10 @@
     lane = lax.broadcasted_iota(jnp.int32, (bands, 128), 1)
     for i in range(8):
         at = slice(i * 128, (i + 1) * 128)
-        chunk_ref[pl.ds(i * bands * 10 + 8, bands, stride=10)] = jnp.where(lane < 64, picked[0][:, at], picked[1][:, at])
+        mine = jnp.where(lane < 64, picked[0][:, at], picked[1][:, at])
+        for part in (0, bands // 2):
+            to = place(i, part, 8, bands) * 10 + 8
+            chunk_ref[pl.ds(to, bands // 2, stride=10)] = mine[part : part + bands // 2]
 
     for u in range(rows):
         if u % lines == 0:
@@ -121,10 +128,10 @@
             for h in range(2):
                 for i in range(8):
                     from_row = h * 64 + i * 8
-                    chunk_ref[pl.ds((i * bands + at + h) * 10, 8)] = turned[from_row : from_row + 8]
+                    chunk_ref[pl.ds(place(i, at + h, 8, bands) * 10, 8)] = turned[from_row : from_row + 8]
         span = 2 * step * 10
         for i in range(8):
-            at = i * bands * 10 + q * span
+            at = place(i, 2 * step * q, 8, bands) * 10
             out_buf[at : at + span] = chunk_ref[at : at + span].astype(BF16)
             store = pltpu.make_async_copy(
                 out_buf.at[pl.ds(at, span)], out_ref.at[pl.ds(at, span)], out_sem.at[q * 8 + i]
@@ -200,10 +207,11 @@
 
     for p in range(pairs):
         for h in range(2):
-            x = [wide_ref[pl.ds((m * bands + 2 * p + h) * 10, 8)] for m in range(8)]
+            x = [wide_ref[pl.ds(place(m, 2 * p + h, 8, bands) * 10, 8)] for m in range(8)]
             x_ref[(p + 1) * rows : (p + 2) * rows, h * 128 : (h + 1) * 128] = jnp.concatenate(x, axis=0).astype(BF16)
     for s in range(bands):
-        both_ways(heights_ref, s, wide_ref[pl.ds(s * 10 + 8, 8, stride=bands * 10)])
+        x = wide_ref[pl.ds(place(4, s, 8, bands) * 10 + 8, 8, stride=bands * 10)]
+        both_ways(heights_ref, s, pltpu.roll(x, 4, 0))
     lane = lax.broadcasted_iota(jnp.int32, (8, 128), 1)
 
     def mirror_pair(p, carry):
@@ -338,7 +346,8 @@
     bands, blocks = footprint.shape
     out = first_stage(mode_field, approach_tiles, footprint, figure)
     sent = out.reshape(-1, 5, 2, TILE).transpose(0, 2, 1, 3).reshape(-1, 2, 5 * TILE)
-    got = lax.all_to_all(sent, ("mode", "band"), split_axis=0, concat_axis=0, tiled=True)
+    order = sorted(range(8 * bands), key=lambda k: place(k // bands, k % bands, 8, bands))
+    got = lax.all_to_all(sent, ("mode", "band"), split_axis=0, concat_axis=0, tiled=True, axis_index_groups=[order])
     got = got.reshape(-1, 2, 5, TILE).transpose(0, 2, 1, 3).reshape(out.shape)
     source_band = lax.div(footprint, blocks)
     code = lax.broadcasted_iota(jnp.int32, footprint.shape, 1) * blocks + lax.rem(footprint, blocks)

time: 144 us -> 144 us (level)
  waiting for transfers between devices: 81.2 us -> 83.1 us
  starting transfers between devices: 31.3 us -> 29.8 us
    all_to_all x1, waiting for transfers between devices: 66.1 us -> 67.9 us  [shards(): lax.all_to_all(sent, ('mode', 'band'), split_axis=0, concat_axis=0, tiled...]
    all_to_all x1, starting transfers between devices: 7.03 us -> 5.53 us  [shards(): lax.all_to_all(tiles, 'band', split_axis=0, concat_axis=0, tiled=True)]
where the time goes in v6:
time: 144 us
  waiting for transfers between devices  83.1 us (58%)
  starting transfers between devices  29.8 us (21%)
  blocking collectives  16.4 us (11%)
  Pallas kernels  13.4 us (9%)
    all_to_all x1, waiting for transfers between devices, shards(): lax.all_to_all(sent, ('mode', 'band'), split_axis=0, concat_axis=0, tiled...  67.9 us
    all_to_all x1, starting transfers between devices, shards(): lax.all_to_all(sent, ('mode', 'band'), split_axis=0, concat_axis=0, tiled...  24.3 us
    all_gather x1, blocking collectives, shards(): return lax.all_gather(own, 'mode', axis=0, tiled=True).astype(F32)  16.4 us
    all_to_all x1, waiting for transfers between devices, shards(): lax.all_to_all(tiles, 'band', split_axis=0, concat_axis=0, tiled=True)  15.2 us
    pallas_call x1, Pallas kernels, second_stage(): pl.pallas_call(second_kernel, out_shape=jax.ShapeDtypeStruct((bands, 8, 1...  6.83 us
    all_to_all x1, starting transfers between devices, shards(): lax.all_to_all(tiles, 'band', split_axis=0, concat_axis=0, tiled=True)  5.53 us
    pallas_call x1, Pallas kernels, first_stage(): pl.pallas_call(first_kernel, out_shape=jax.ShapeDtypeStruct(shape, BF16),...  5.3 us
  transfers between devices with their start and end apart: 2, of which 2 were waited for; matrix products, arithmetic and copies ran while one was open for 0% of the time, Pallas kernels for 0%

profile of v6, /device:TPU:1, one launch (start us, length us, event | category | flops | bytes accessed | tf_op | source)
XLA Modules:
  0.0 144.2 jit_solution(5056114373496155942)
XLA Ops:
  0.0 5.3 %first.1 = bf16[5120,128]{1,0:T(8,128)(2,1)} custom-call(bf16[4096,128]{1,0:T(8,128)(2,1)} %bitcast.27, bf16[3,2,128,128]{3,2,1,0:T(8,128)(2,1)} %approach_ref.1, s32[64,64]{1,0:T(8,128)} %footprint_ref.1, bf16[64,4096]{1,0:T(8,128)(2,1)} %figure_ref.1), custom_call_target="tpu_custom_call" | custom-call | flops 805306368 | bytes 2097152 | tf_op jit(solution)/shard_map/first/pallas_call | solution.py:151
  5.3 0.0 copy-start.3
  5.3 0.0 copy-start
  5.3 0.0 copy-start.1
  5.3 0.0 copy-start.2
  5.4 24.3 %all-to-all-start = ((bf16[512,2,640]{2,1,0:T(2,128)(2,1)}), bf16[512,2,640]{2,1,0:T(2,128)(2,1)S(1)}, u32[]{:S(2)}, u32[]{:S(2)}) async-start(bf16[512,2,640]{2,1,0:T(2,128)(2,1)} %bitcast.26), calls=%async_computation | async-start | bytes 2621440 | tf_op jit(solution)/shard_map/all_to_all | solution.py:350
  29.7 0.0 copy-done.3
  29.7 0.1 select_reduce_fusion
  29.8 0.2 fusion.2
  30.1 67.9 %all-to-all-done = bf16[512,2,640]{2,1,0:T(2,128)(2,1)S(1)} async-done(((bf16[512,2,640]{2,1,0:T(2,128)(2,1)}), bf16[512,2,640]{2,1,0:T(2,128)(2,1)S(1)}, u32[]{:S(2)}, u32[]{:S(2)}) %all-to-all-start) | async-done | bytes 1310752 | tf_op jit(solution)/shard_map/all_to_all | solution.py:350
  98.0 0.0 copy-done
  98.0 0.0 copy-done.1
  98.0 0.0 copy-done.2
  98.0 6.8 %second.1 = bf16[64,8,128]{2,1,0:T(8,128)(2,1)} custom-call(s32[3,64]{1,0:T(4,128)S(1)} %pad_add_fusion.index_ref, bf16[5120,128]{1,0:T(8,128)(2,1)S(1)} %bitcast.25, bf16[3,2,128,128]{3,2,1,0:T(8,128)(2,1)S(1)} %copy-done, bf16[3,2,128,128]{3,2,1,0:T(8,128)(2,1)S(1)} %copy-done.2, bf16[64,4096]{1,0:T(8,128)(2,1)S(1)} %copy-done.1), custom_call_target="tpu_custom_call" | custom-call | flops 2415919104 | bytes 1048576 | tf_op jit(solution)/shard_map/second/pallas_call | solution.py:282
  104.8 5.5 %all-to-all-start.1 = ((bf16[64,8,128]{2,1,0:T(8,128)(2,1)}), bf16[64,8,128]{2,1,0:T(8,128)(2,1)S(1)}, u32[]{:S(2)}, u32[]{:S(2)}) async-start(bf16[64,8,128]{2,1,0:T(8,128)(2,1)} %second.1), calls=%async_computation.1 | async-start | bytes 262144 | tf_op jit(solution)/shard_map/all_to_all | solution.py:369
  110.4 15.2 %all-to-all-done.1.given_ref = bf16[64,8,128]{2,1,0:T(8,128)(2,1)S(1)} async-done(((bf16[64,8,128]{2,1,0:T(8,128)(2,1)}), bf16[64,8,128]{2,1,0:T(8,128)(2,1)S(1)}, u32[]{:S(2)}, u32[]{:S(2)}) %all-to-all-start.1) | async-done | bytes 131104 | tf_op jit(solution)/shard_map/all_to_all | solution.py:369
  125.6 1.2 collect.1
  126.8 16.4 %all_gather.3 = bf16[64,4096]{1,0:T(8,128)(2,1)S(1)} all-gather(bf16[8,4096]{1,0:T(8,128)(2,1)S(1)} %collect.1), channel_id=1, replica_groups=mesh['mode'=8,'band'=64] {'mode'}, dimensions={0}, use_global_device_ids=true | all-gather | bytes 589824 | tf_op jit(solution)/shard_map/all_gather | solution.py:371
  143.2 1.0 convert_element_type.22
  (8 shorter events, 0.1 us)
Async XLA Ops:
  5.3 24.4 %copy-start.3 = (s32[64,64]{1,0:T(8,128)S(1)}, s32[64,64]{1,0:T(8,128)}, u32[]{:S(2)}) copy-start(s32[64,64]{1,0:T(8,128)} %footprint_ref.1) | copy-start | bytes 49156
  5.3 92.7 %copy-start = (bf16[3,2,128,128]{3,2,1,0:T(8,128)(2,1)S(1)}, bf16[3,2,128,128]{3,2,1,0:T(8,128)(2,1)}, u32[]{:S(2)}) copy-start(bf16[3,2,128,128]{3,2,1,0:T(8,128)(2,1)} %approach_ref.1) | copy-start | bytes 589828
  5.3 92.7 %copy-start.1 = (bf16[64,4096]{1,0:T(8,128)(2,1)S(1)}, bf16[64,4096]{1,0:T(8,128)(2,1)}, u32[]{:S(2)}) copy-start(bf16[64,4096]{1,0:T(8,128)(2,1)} %target_ref.1) | copy-start | bytes 1572868
  5.3 92.6 %copy-start.2 = (bf16[3,2,128,128]{3,2,1,0:T(8,128)(2,1)S(1)}, bf16[3,2,128,128]{3,2,1,0:T(8,128)(2,1)}, u32[]{:S(2)}) copy-start(bf16[3,2,128,128]{3,2,1,0:T(8,128)(2,1)} %focus_ref.1) | copy-start | bytes 589828
  5.4 92.6 %all-to-all-start = ((bf16[512,2,640]{2,1,0:T(2,128)(2,1)}), bf16[512,2,640]{2,1,0:T(2,128)(2,1)S(1)}, u32[]{:S(2)}, u32[]{:S(2)}) async-start(bf16[512,2,640]{2,1,0:T(2,128)(2,1)} %bitcast.26), calls=%async_computation | async-start | bytes 2621440 | tf_op jit(solution)/shard_map/all_to_all | solution.py:350
  104.8 20.7 %all-to-all-start.1 = ((bf16[64,8,128]{2,1,0:T(8,128)(2,1)}), bf16[64,8,128]{2,1,0:T(8,128)(2,1)S(1)}, u32[]{:S(2)}, u32[]{:S(2)}) async-start(bf16[64,8,128]{2,1,0:T(8,128)(2,1)} %second.1), calls=%async_computation.1 | async-start | bytes 262144 | tf_op jit(solution)/shard_map/all_to_all | solution.py:369

commit v7 on v5

--- a/solution.py
+++ b/solution.py
@@ -45,6 +45,24 @@
             part = jnp.dot(x, w_ref[o], preferred_element_type=F32)
         total = part if total is None else total + part
     return total
+
+
+def cos_sin(x):
+    n = jnp.floor(x * 0.6366197723675814 + 0.5)
+    r = x - n * 1.5703125
+    r = r - n * 4.837512969970703e-4
+    r = r - n * 7.549789948768648e-8
+    r2 = r * r
+    sin = r + r * r2 * (-1.6666654611e-1 + r2 * (8.3321608736e-3 - r2 * 1.9515295891e-4))
+    cos = 1.0 - 0.5 * r2 + r2 * r2 * (4.166664568298827e-2 + r2 * (-1.388731625493765e-3 + r2 * 2.443315711809948e-5))
+    quarter = n.astype(jnp.int32)
+    odd = (quarter & 1) == 1
+    cos_out = jnp.where(odd, sin, cos)
+    sin_out = jnp.where(odd, cos, sin)
+    return (
+        jnp.where(((quarter + 1) & 2) != 0, -cos_out, cos_out),
+        jnp.where((quarter & 2) != 0, -sin_out, sin_out),
+    )
 
 
 def first_kernel(field_ref, tiles_ref, footprint_ref, figure_ref, out_ref, field_buf, figure_buf, out_buf, wide_ref,
@@ -171,9 +189,9 @@
 
 
 def second_kernel(index_ref, given_ref, approach_ref, focus_ref, target_ref, out_ref,
-                  got_ref, wide_ref, heights_ref, cos_ref, sin_ref, want_ref, x_ref, y_ref, g_ref, wp_ref, wf_ref, sem):
-    pairs = cos_ref.shape[0]
-    bands = 2 * pairs
+                  got_ref, wide_ref, turn_ref, heights_ref, want_ref, x_ref, y_ref, g_ref, wp_ref, wf_ref, sem):
+    bands = out_ref.shape[0]
+    pairs = bands // 2
     rows = 64
     parts = 4
     size = given_ref.shape[0] // parts
@@ -202,18 +220,13 @@
         for h in range(2):
             x = [wide_ref[pl.ds((m * bands + 2 * p + h) * 10, 8)] for m in range(8)]
             x_ref[(p + 1) * rows : (p + 2) * rows, h * 128 : (h + 1) * 128] = jnp.concatenate(x, axis=0).astype(BF16)
+    for m in range(8):
+        for g in range(bands // 8):
+            at = (m * bands + 8 * g) * 10 + 8
+            turn_ref[pl.ds(8 * g * 9 + m, 8, stride=9)] = wide_ref[pl.ds(at, 8, stride=10)]
     for s in range(bands):
-        both_ways(heights_ref, s, wide_ref[pl.ds(s * 10 + 8, 8, stride=bands * 10)])
+        both_ways(heights_ref, s, turn_ref[pl.ds(9 * s, 8)])
     lane = lax.broadcasted_iota(jnp.int32, (8, 128), 1)
-
-    def mirror_pair(p, carry):
-        a, b = heights_ref[index_ref[2, 2 * p]], heights_ref[index_ref[2, 2 * p + 1]]
-        phase = PHASE_FACTOR * jnp.where(lane < 64, a, b)
-        cos_ref[p] = jnp.cos(phase)
-        sin_ref[p] = jnp.sin(phase)
-        return carry
-
-    lax.fori_loop(0, pairs, mirror_pair, 0, unroll=4)
     step = 16
 
     def mirror(q, carry):
@@ -221,8 +234,13 @@
         a2 = banded_rows(x_ref, wp_ref, row, step * rows, rows).astype(BF16).astype(F32)
         re = a2[:, 0:128].reshape(step, 8, 8, 128)
         im = a2[:, 128:256].reshape(step, 8, 8, 128)
-        cos = cos_ref[pl.ds(q * step, step)][:, None]
-        sin = sin_ref[pl.ds(q * step, step)][:, None]
+        waves = []
+        for t in range(step):
+            a = heights_ref[index_ref[2, 2 * (q * step + t)]]
+            b = heights_ref[index_ref[2, 2 * (q * step + t) + 1]]
+            waves.append(cos_sin(PHASE_FACTOR * jnp.where(lane < 64, a, b)))
+        cos = jnp.stack([wave[0] for wave in waves])[:, None]
+        sin = jnp.stack([wave[1] for wave in waves])[:, None]
         to = pl.ds(pl.multiple_of(row + rows, 64), step * rows)
         y_ref[to, 0:128] = (re * cos - im * sin).reshape(step * rows, 128).astype(BF16)
         y_ref[to, 128:256] = (re * sin + im * cos).reshape(step * rows, 128).astype(BF16)
@@ -279,9 +297,8 @@
         scratch_shapes=[
             pltpu.VMEM(got.shape, BF16),
             pltpu.VMEM(got.shape, F32),
+            pltpu.VMEM((9 * bands, 128), F32),
             pltpu.VMEM((2 * bands, 8, 128), F32),
-            pltpu.VMEM((pairs, 8, 128), F32),
-            pltpu.VMEM((pairs, 8, 128), F32),
             pltpu.VMEM((8, target.shape[1]), BF16),
         ]
         + [pltpu.VMEM(((pairs + 2) * 64, 256), BF16)] * 3

time: 144 us -> 143 us (level)
  no operation moved by 1% of the time
where the time goes in v7:
time: 143 us
  waiting for transfers between devices  81.2 us (57%)
  starting transfers between devices  31.3 us (22%)
  blocking collectives  16.4 us (11%)
  Pallas kernels  12.6 us (9%)
    all_to_all x1, waiting for transfers between devices, shards(): lax.all_to_all(sent, ('mode', 'band'), split_axis=0, concat_axis=0, tiled...  66.1 us
    all_to_all x1, starting transfers between devices, shards(): lax.all_to_all(sent, ('mode', 'band'), split_axis=0, concat_axis=0, tiled...  24.3 us
    all_gather x1, blocking collectives, shards(): return lax.all_gather(own, 'mode', axis=0, tiled=True).astype(F32)  16.4 us
    all_to_all x1, waiting for transfers between devices, shards(): lax.all_to_all(tiles, 'band', split_axis=0, concat_axis=0, tiled=True)  15.1 us
    all_to_all x1, starting transfers between devices, shards(): lax.all_to_all(tiles, 'band', split_axis=0, concat_axis=0, tiled=True)  7.04 us
    pallas_call x1, Pallas kernels, second_stage(): pl.pallas_call(second_kernel, out_shape=jax.ShapeDtypeStruct((bands, 8, 1...  6.13 us
    pallas_call x1, Pallas kernels, first_stage(): pl.pallas_call(first_kernel, out_shape=jax.ShapeDtypeStruct(shape, BF16),...  5.28 us
  transfers between devices with their start and end apart: 2, of which 2 were waited for; matrix products, arithmetic and copies ran while one was open for 0% of the time, Pallas kernels for 0%

profile of v7, /device:TPU:1, one launch (start us, length us, event | category | flops | bytes accessed | tf_op | source)
XLA Modules:
  0.0 143.2 jit_solution(7394300105877810321)
XLA Ops:
  0.0 5.3 %first.1 = bf16[5120,128]{1,0:T(8,128)(2,1)} custom-call(bf16[4096,128]{1,0:T(8,128)(2,1)} %bitcast.27, bf16[3,2,128,128]{3,2,1,0:T(8,128)(2,1)} %approach_ref.1, s32[64,64]{1,0:T(8,128)} %footprint_ref.1, bf16[64,4096]{1,0:T(8,128)(2,1)} %figure_ref.1), custom_call_target="tpu_custom_call" | custom-call | flops 805306368 | bytes 2097152 | tf_op jit(solution)/shard_map/first/pallas_call | solution.py:162
  5.3 0.0 copy-start.3
  5.3 0.0 copy-start
  5.3 0.0 copy-start.1
  5.3 0.0 copy-start.2
  5.3 24.3 %all-to-all-start = ((bf16[512,2,640]{2,1,0:T(2,128)(2,1)}), bf16[512,2,640]{2,1,0:T(2,128)(2,1)S(1)}, u32[]{:S(2)}, u32[]{:S(2)}) async-start(bf16[512,2,640]{2,1,0:T(2,128)(2,1)} %bitcast.26), calls=%async_computation | async-start | bytes 2621440 | tf_op jit(solution)/shard_map/all_to_all | solution.py:358
  29.7 0.0 copy-done.3
  29.7 0.1 select_reduce_fusion
  29.8 0.2 fusion.2
  30.1 66.1 %all-to-all-done = bf16[512,2,640]{2,1,0:T(2,128)(2,1)S(1)} async-done(((bf16[512,2,640]{2,1,0:T(2,128)(2,1)}), bf16[512,2,640]{2,1,0:T(2,128)(2,1)S(1)}, u32[]{:S(2)}, u32[]{:S(2)}) %all-to-all-start) | async-done | bytes 1310752 | tf_op jit(solution)/shard_map/all_to_all | solution.py:358
  96.1 0.0 copy-done
  96.2 0.0 copy-done.1
  96.2 0.0 copy-done.2
  96.2 6.1 %second.1 = bf16[64,8,128]{2,1,0:T(8,128)(2,1)} custom-call(s32[3,64]{1,0:T(4,128)S(1)} %pad_add_fusion.index_ref, bf16[5120,128]{1,0:T(8,128)(2,1)S(1)} %bitcast.25, bf16[3,2,128,128]{3,2,1,0:T(8,128)(2,1)S(1)} %copy-done, bf16[3,2,128,128]{3,2,1,0:T(8,128)(2,1)S(1)} %copy-done.2, bf16[64,4096]{1,0:T(8,128)(2,1)S(1)} %copy-done.1), custom_call_target="tpu_custom_call" | custom-call | flops 2415919104 | bytes 1048576 | tf_op jit(solution)/shard_map/second/pallas_call | solution.py:292
  102.3 7.0 %all-to-all-start.1 = ((bf16[64,8,128]{2,1,0:T(8,128)(2,1)}), bf16[64,8,128]{2,1,0:T(8,128)(2,1)S(1)}, u32[]{:S(2)}, u32[]{:S(2)}) async-start(bf16[64,8,128]{2,1,0:T(8,128)(2,1)} %second.1), calls=%async_computation.1 | async-start | bytes 262144 | tf_op jit(solution)/shard_map/all_to_all | solution.py:377
  109.4 15.1 %all-to-all-done.1.given_ref = bf16[64,8,128]{2,1,0:T(8,128)(2,1)S(1)} async-done(((bf16[64,8,128]{2,1,0:T(8,128)(2,1)}), bf16[64,8,128]{2,1,0:T(8,128)(2,1)S(1)}, u32[]{:S(2)}, u32[]{:S(2)}) %all-to-all-start.1) | async-done | bytes 131104 | tf_op jit(solution)/shard_map/all_to_all | solution.py:377
  124.5 1.2 collect.1
  125.8 16.4 %all_gather.3 = bf16[64,4096]{1,0:T(8,128)(2,1)S(1)} all-gather(bf16[8,4096]{1,0:T(8,128)(2,1)S(1)} %collect.1), channel_id=1, replica_groups=mesh['mode'=8,'band'=64] {'mode'}, dimensions={0}, use_global_device_ids=true | all-gather | bytes 589824 | tf_op jit(solution)/shard_map/all_gather | solution.py:379
  142.2 1.0 convert_element_type.22
  (8 shorter events, 0.1 us)
Async XLA Ops:
  5.3 24.4 %copy-start.3 = (s32[64,64]{1,0:T(8,128)S(1)}, s32[64,64]{1,0:T(8,128)}, u32[]{:S(2)}) copy-start(s32[64,64]{1,0:T(8,128)} %footprint_ref.1) | copy-start | bytes 49156
  5.3 90.9 %copy-start = (bf16[3,2,128,128]{3,2,1,0:T(8,128)(2,1)S(1)}, bf16[3,2,128,128]{3,2,1,0:T(8,128)(2,1)}, u32[]{:S(2)}) copy-start(bf16[3,2,128,128]{3,2,1,0:T(8,128)(2,1)} %approach_ref.1) | copy-start | bytes 589828
  5.3 90.8 %copy-start.1 = (bf16[64,4096]{1,0:T(8,128)(2,1)S(1)}, bf16[64,4096]{1,0:T(8,128)(2,1)}, u32[]{:S(2)}) copy-start(bf16[64,4096]{1,0:T(8,128)(2,1)} %target_ref.1) | copy-start | bytes 1572868
  5.3 90.8 %copy-start.2 = (bf16[3,2,128,128]{3,2,1,0:T(8,128)(2,1)S(1)}, bf16[3,2,128,128]{3,2,1,0:T(8,128)(2,1)}, u32[]{:S(2)}) copy-start(bf16[3,2,128,128]{3,2,1,0:T(8,128)(2,1)} %focus_ref.1) | copy-start | bytes 589828
  5.3 90.8 %all-to-all-start = ((bf16[512,2,640]{2,1,0:T(2,128)(2,1)}), bf16[512,2,640]{2,1,0:T(2,128)(2,1)S(1)}, u32[]{:S(2)}, u32[]{:S(2)}) async-start(bf16[512,2,640]{2,1,0:T(2,128)(2,1)} %bitcast.26), calls=%async_computation | async-start | bytes 2621440 | tf_op jit(solution)/shard_map/all_to_all | solution.py:358
  102.3 22.2 %all-to-all-start.1 = ((bf16[64,8,128]{2,1,0:T(8,128)(2,1)}), bf16[64,8,128]{2,1,0:T(8,128)(2,1)S(1)}, u32[]{:S(2)}, u32[]{:S(2)}) async-start(bf16[64,8,128]{2,1,0:T(8,128)(2,1)} %second.1), calls=%async_computation.1 | async-start | bytes 262144 | tf_op jit(solution)/shard_map/all_to_all | solution.py:377

commit v8 on v7

--- a/solution.py
+++ b/solution.py
@@ -65,8 +65,8 @@
     )
 
 
-def first_kernel(field_ref, tiles_ref, footprint_ref, figure_ref, out_ref, field_buf, figure_buf, out_buf, wide_ref,
-                 spread_ref, rows_ref, pick_ref, chunk_ref, x_ref, w_ref, in_sem, out_sem):
+def first_kernel(field_ref, tiles_hbm, footprint_hbm, figure_ref, out_ref, tiles_ref, footprint_ref, field_buf,
+                 figure_buf, out_buf, wide_ref, spread_ref, rows_ref, pick_ref, chunk_ref, x_ref, w_ref, in_sem, out_sem):
     count_tiles = field_ref.shape[0] // 128
     bands, blocks = footprint_ref.shape
     rows = 64
@@ -74,8 +74,11 @@
     parts = 4
     lines = rows // parts
     size = lines * 2 * count_tiles
+    tiles_load = pltpu.make_async_copy(tiles_hbm, tiles_ref, in_sem.at[parts + 1])
+    footprint_load = pltpu.make_async_copy(footprint_hbm, footprint_ref, in_sem.at[parts + 2])
     figure_load = pltpu.make_async_copy(figure_ref, figure_buf, in_sem.at[parts])
-    figure_load.start()
+    for load in (tiles_load, footprint_load, figure_load):
+        load.start()
     loads = [
         pltpu.make_async_copy(
             field_ref.at[pl.ds(i * size, size)], field_buf.at[pl.ds(i * size, size)], in_sem.at[i]
@@ -84,12 +87,14 @@
     ]
     for load in loads:
         load.start()
-    write_weights(tiles_ref, w_ref, False)
     x_ref[0:rows] = jnp.zeros((rows, 256), BF16)
     x_ref[(count_tiles + 1) * rows : (count_tiles + 2) * rows] = jnp.zeros((rows, 256), BF16)
     chunk_ref[pl.ds(9, 8 * bands, stride=10)] = jnp.zeros((8 * bands, 128), F32)
+    tiles_load.wait()
+    write_weights(tiles_ref, w_ref, False)
 
     mode, band = lax.axis_index("mode"), lax.axis_index("band")
+    footprint_load.wait()
     figure_load.wait()
     for p in range(blocks // 2):
         x = figure_buf[:, p * 128 : (p + 1) * 128].astype(F32)
@@ -162,20 +167,22 @@
     return pl.pallas_call(
         first_kernel,
         out_shape=jax.ShapeDtypeStruct(shape, BF16),
-        in_specs=[pl.BlockSpec(memory_space=pl.ANY), whole(), whole(), pl.BlockSpec(memory_space=pl.ANY)],
+        in_specs=[pl.BlockSpec(memory_space=pl.ANY)] * 4,
         out_specs=pl.BlockSpec(memory_space=pl.ANY),
         scratch_shapes=[
+            pltpu.VMEM(tiles.shape, BF16),
+            pltpu.VMEM(footprint.shape, jnp.int32),
             pltpu.VMEM(field.shape, BF16),
             pltpu.VMEM(figure.shape, BF16),
             pltpu.VMEM(shape, BF16),
-            pltpu.VMEM((rows * (2 * count + 1), 128), F32),
-            pltpu.VMEM((blocks // 2 * 72, 128), F32),
-            pltpu.VMEM((blocks * 9, 128), F32),
+            pltpu.VMEM(((rows + 1) * (2 * count + 1) + 7, 128), F32),
+            pltpu.VMEM(((blocks // 2 + 1) * 72, 128), F32),
+            pltpu.VMEM((blocks * 9 + 16, 128), F32),
             pltpu.VMEM((blocks, 8 * 128), BF16),
-            pltpu.VMEM(shape, F32),
+            pltpu.VMEM((shape[0] + 16, 128), F32),
             pltpu.VMEM(((count + 2) * rows, 256), BF16),
             pltpu.VMEM((3, 256, 256), BF16),
-            pltpu.SemaphoreType.DMA((5,)),
+            pltpu.SemaphoreType.DMA((7,)),
             pltpu.SemaphoreType.DMA((8 * (count // 16),)),
         ],
         cost_estimate=pl.CostEstimate(flops=2 * rows * count * 768 * 256, bytes_accessed=1 << 21, transcendentals=0),
@@ -188,33 +195,22 @@
     wide_ref[2 * at + 1] = pltpu.roll(x, 64, 1)
 
 
-def second_kernel(index_ref, given_ref, approach_ref, focus_ref, target_ref, out_ref,
-                  got_ref, wide_ref, turn_ref, heights_ref, want_ref, x_ref, y_ref, g_ref, wp_ref, wf_ref, sem):
+def second_kernel(index_ref, got_ref, approach_ref, focus_ref, target_ref, out_ref, wide_ref,
+                  turn_ref, heights_ref, want_ref, x_ref, y_ref, g_ref, wp_ref, wf_ref, sem):
     bands = out_ref.shape[0]
     pairs = bands // 2
     rows = 64
-    parts = 4
-    size = given_ref.shape[0] // parts
-    loads = [
-        pltpu.make_async_copy(given_ref.at[pl.ds(i * size, size)], got_ref.at[pl.ds(i * size, size)], sem.at[i])
-        for i in range(parts)
-    ]
     mode = lax.axis_index("mode")
-    loads.append(
-        pltpu.make_async_copy(target_ref.at[pl.ds(pl.multiple_of(mode * 8, 8), 8)], want_ref, sem.at[parts])
-    )
-    for load in loads:
-        load.start()
+    load = pltpu.make_async_copy(target_ref.at[pl.ds(pl.multiple_of(mode * 8, 8), 8)], want_ref, sem)
+    load.start()
     write_weights(approach_ref, wp_ref, True)
     write_weights(focus_ref, wf_ref, False)
     blank = jnp.zeros((rows, 256), BF16)
     for ref in (x_ref, y_ref, g_ref):
         ref[0:rows] = blank
         ref[(pairs + 1) * rows : (pairs + 2) * rows] = blank
-    for i in range(parts):
-        loads[i].wait()
-        wide_ref[i * size : (i + 1) * size] = got_ref[i * size : (i + 1) * size].astype(F32)
-    loads[parts].wait()
+    wide_ref[0 : got_ref.shape[0]] = got_ref[...].astype(F32)
+    load.wait()
 
     for p in range(pairs):
         for h in range(2):
@@ -292,33 +288,29 @@
     return pl.pallas_call(
         second_kernel,
         out_shape=jax.ShapeDtypeStruct((bands, 8, 128), BF16),
-        in_specs=[pl.BlockSpec(memory_space=pltpu.SMEM), anywhere, whole(), whole(), anywhere],
+        in_specs=[pl.BlockSpec(memory_space=pltpu.SMEM), whole(), whole(), whole(), anywhere],
         out_specs=whole(),
         scratch_shapes=[
-            pltpu.VMEM(got.shape, BF16),
-            pltpu.VMEM(got.shape, F32),
-            pltpu.VMEM((9 * bands, 128), F32),
+            pltpu.VMEM((got.shape[0] + 16, 128), F32),
+            pltpu.VMEM((9 * bands + 16, 128), F32),
             pltpu.VMEM((2 * bands, 8, 128), F32),
             pltpu.VMEM((8, target.shape[1]), BF16),
         ]
         + [pltpu.VMEM(((pairs + 2) * 64, 256), BF16)] * 3
         + [pltpu.VMEM((3, 256, 256), BF16)] * 2
-        + [pltpu.SemaphoreType.DMA((5,))],
+        + [pltpu.SemaphoreType.DMA],
         cost_estimate=pl.CostEstimate(flops=6 * 64 * pairs * 768 * 256, bytes_accessed=1 << 20, transcendentals=0),
         compiler_params=pltpu.CompilerParams(vmem_limit_bytes=32 << 20),
         name="second",
     )(index, got, approach, focus, target)
 
 
-def collect_kernel(index_ref, given_ref, out_ref, tiles_ref, wide_ref, sem, *sums):
+def collect_kernel(index_ref, tiles_ref, out_ref, wide_ref, *sums):
     lane = lax.broadcasted_iota(jnp.int32, (8, 128), 1)
     pairs = out_ref.shape[1] // 128
     bands = tiles_ref.shape[0]
-    load = pltpu.make_async_copy(given_ref, tiles_ref, sem)
-    load.start()
     for part in sums:
         part[...] = jnp.zeros_like(part)
-    load.wait()
     for d in range(bands):
         both_ways(wide_ref, d, tiles_ref[d].astype(F32))
     for d in range(bands):
@@ -337,13 +329,9 @@
     return pl.pallas_call(
         collect_kernel,
         out_shape=jax.ShapeDtypeStruct((8, bands * 64), dtype),
-        in_specs=[pl.BlockSpec(memory_space=pltpu.SMEM), pl.BlockSpec(memory_space=pl.ANY)],
+        in_specs=[pl.BlockSpec(memory_space=pltpu.SMEM), whole()],
         out_specs=whole(),
-        scratch_shapes=[
-            pltpu.VMEM(tiles.shape, BF16),
-            pltpu.VMEM((2 * bands, 8, 128), F32),
-            pltpu.SemaphoreType.DMA,
-        ]
+        scratch_shapes=[pltpu.VMEM((2 * bands, 8, 128), F32)]
         + [pltpu.VMEM((bands + 8, 8, 128), F32)] * 4,
         compiler_params=pltpu.CompilerParams(vmem_limit_bytes=8 << 20),
         name="collect",

time: 143 us -> 142 us (level)
  no operation moved by 1% of the time
where the time goes in v8:
time: 142 us
  waiting for transfers between devices  81.2 us (57%)
  starting transfers between devices  31.3 us (22%)
  blocking collectives  16.4 us (12%)
  Pallas kernels  11.2 us (8%)
    all_to_all x1, waiting for transfers between devices, shards(): lax.all_to_all(sent, ('mode', 'band'), split_axis=0, concat_axis=0, tiled...  66.1 us
    all_to_all x1, starting transfers between devices, shards(): lax.all_to_all(sent, ('mode', 'band'), split_axis=0, concat_axis=0, tiled...  24.3 us
    all_gather x1, blocking collectives, shards(): return lax.all_gather(own, 'mode', axis=0, tiled=True).astype(F32)  16.4 us
    all_to_all x1, waiting for transfers between devices, shards(): lax.all_to_all(tiles, 'band', split_axis=0, concat_axis=0, tiled=True)  15.1 us
    all_to_all x1, starting transfers between devices, shards(): lax.all_to_all(tiles, 'band', split_axis=0, concat_axis=0, tiled=True)  7.03 us
    pallas_call x1, Pallas kernels, second_stage(): pl.pallas_call(second_kernel, out_shape=jax.ShapeDtypeStruct((bands, 8, 1...  5.68 us
    pallas_call x1, Pallas kernels, first_stage(): pl.pallas_call(first_kernel, out_shape=jax.ShapeDtypeStruct(shape, BF16),...  4.48 us
  transfers between devices with their start and end apart: 2, of which 2 were waited for; matrix products, arithmetic and copies ran while one was open for 0% of the time, Pallas kernels for 0%

profile of v8, /device:TPU:1, one launch (start us, length us, event | category | flops | bytes accessed | tf_op | source)
XLA Modules:
  0.0 141.7 jit_solution(4082403018046525618)
XLA Ops:
  0.0 4.5 %first.1 = bf16[5120,128]{1,0:T(8,128)(2,1)} custom-call(bf16[4096,128]{1,0:T(8,128)(2,1)} %bitcast.27, bf16[3,2,128,128]{3,2,1,0:T(8,128)(2,1)} %approach_ref.1, s32[64,64]{1,0:T(8,128)} %footprint_hbm.1, bf16[64,4096]{1,0:T(8,128)(2,1)} %figure_ref.1), custom_call_target="tpu_custom_call" | custom-call | flops 805306368 | bytes 2097152 | tf_op jit(solution)/shard_map/first/pallas_call | solution.py:167
  4.5 0.0 copy-start.3
  4.5 0.0 copy-start
  4.5 0.0 copy-start.1
  4.5 0.0 copy-start.2
  4.5 24.3 %all-to-all-start = ((bf16[512,2,640]{2,1,0:T(2,128)(2,1)}), bf16[512,2,640]{2,1,0:T(2,128)(2,1)S(1)}, u32[]{:S(2)}, u32[]{:S(2)}) async-start(bf16[512,2,640]{2,1,0:T(2,128)(2,1)} %bitcast.26), calls=%async_computation | async-start | bytes 2621440 | tf_op jit(solution)/shard_map/all_to_all | solution.py:346
  28.9 0.0 copy-done.3
  28.9 0.1 select_reduce_fusion
  29.0 0.2 fusion.2
  29.3 66.1 %all-to-all-done = bf16[512,2,640]{2,1,0:T(2,128)(2,1)S(1)} async-done(((bf16[512,2,640]{2,1,0:T(2,128)(2,1)}), bf16[512,2,640]{2,1,0:T(2,128)(2,1)S(1)}, u32[]{:S(2)}, u32[]{:S(2)}) %all-to-all-start) | async-done | bytes 1310752 | tf_op jit(solution)/shard_map/all_to_all | solution.py:346
  95.3 0.0 copy-done
  95.4 0.0 copy-done.1
  95.4 0.0 copy-done.2
  95.4 5.7 %second.1 = bf16[64,8,128]{2,1,0:T(8,128)(2,1)} custom-call(s32[3,64]{1,0:T(4,128)S(1)} %pad_add_fusion.index_ref, bf16[5120,128]{1,0:T(8,128)(2,1)S(1)} %bitcast.25, bf16[3,2,128,128]{3,2,1,0:T(8,128)(2,1)S(1)} %copy-done, bf16[3,2,128,128]{3,2,1,0:T(8,128)(2,1)S(1)} %copy-done.2, bf16[64,4096]{1,0:T(8,128)(2,1)S(1)} %copy-done.1), custom_call_target="tpu_custom_call" | custom-call | flops 2415919104 | bytes 1048576 | tf_op jit(solution)/shard_map/second/pallas_call | solution.py:288
  101.0 7.0 %all-to-all-start.1 = ((bf16[64,8,128]{2,1,0:T(8,128)(2,1)}), bf16[64,8,128]{2,1,0:T(8,128)(2,1)S(1)}, u32[]{:S(2)}, u32[]{:S(2)}) async-start(bf16[64,8,128]{2,1,0:T(8,128)(2,1)} %second.1), calls=%async_computation.1 | async-start | bytes 262144 | tf_op jit(solution)/shard_map/all_to_all | solution.py:365
  108.1 15.1 %all-to-all-done.1.tiles_ref = bf16[64,8,128]{2,1,0:T(8,128)(2,1)S(1)} async-done(((bf16[64,8,128]{2,1,0:T(8,128)(2,1)}), bf16[64,8,128]{2,1,0:T(8,128)(2,1)S(1)}, u32[]{:S(2)}, u32[]{:S(2)}) %all-to-all-start.1) | async-done | bytes 131104 | tf_op jit(solution)/shard_map/all_to_all | solution.py:365
  123.2 1.0 collect.1
  124.2 16.4 %all_gather.3 = bf16[64,4096]{1,0:T(8,128)(2,1)S(1)} all-gather(bf16[8,4096]{1,0:T(8,128)(2,1)S(1)} %collect.1), channel_id=1, replica_groups=mesh['mode'=8,'band'=64] {'mode'}, dimensions={0}, use_global_device_ids=true | all-gather | bytes 589824 | tf_op jit(solution)/shard_map/all_gather | solution.py:367
  140.7 1.0 convert_element_type.22
  (8 shorter events, 0.1 us)
Async XLA Ops:
  4.5 24.4 %copy-start.3 = (s32[64,64]{1,0:T(8,128)S(1)}, s32[64,64]{1,0:T(8,128)}, u32[]{:S(2)}) copy-start(s32[64,64]{1,0:T(8,128)} %footprint_hbm.1) | copy-start | bytes 49156
  4.5 90.9 %copy-start = (bf16[3,2,128,128]{3,2,1,0:T(8,128)(2,1)S(1)}, bf16[3,2,128,128]{3,2,1,0:T(8,128)(2,1)}, u32[]{:S(2)}) copy-start(bf16[3,2,128,128]{3,2,1,0:T(8,128)(2,1)} %approach_ref.1) | copy-start | bytes 589828
  4.5 90.8 %copy-start.1 = (bf16[64,4096]{1,0:T(8,128)(2,1)S(1)}, bf16[64,4096]{1,0:T(8,128)(2,1)}, u32[]{:S(2)}) copy-start(bf16[64,4096]{1,0:T(8,128)(2,1)} %target_ref.1) | copy-start | bytes 1572868
  4.5 90.8 %copy-start.2 = (bf16[3,2,128,128]{3,2,1,0:T(8,128)(2,1)S(1)}, bf16[3,2,128,128]{3,2,1,0:T(8,128)(2,1)}, u32[]{:S(2)}) copy-start(bf16[3,2,128,128]{3,2,1,0:T(8,128)(2,1)} %focus_ref.1) | copy-start | bytes 589828
  4.5 90.8 %all-to-all-start = ((bf16[512,2,640]{2,1,0:T(2,128)(2,1)}), bf16[512,2,640]{2,1,0:T(2,128)(2,1)S(1)}, u32[]{:S(2)}, u32[]{:S(2)}) async-start(bf16[512,2,640]{2,1,0:T(2,128)(2,1)} %bitcast.26), calls=%async_computation | async-start | bytes 2621440 | tf_op jit(solution)/shard_map/all_to_all | solution.py:346
  101.0 22.2 %all-to-all-start.1 = ((bf16[64,8,128]{2,1,0:T(8,128)(2,1)}), bf16[64,8,128]{2,1,0:T(8,128)(2,1)S(1)}, u32[]{:S(2)}, u32[]{:S(2)}) async-start(bf16[64,8,128]{2,1,0:T(8,128)(2,1)} %second.1), calls=%async_computation.1 | async-start | bytes 262144 | tf_op jit(solution)/shard_map/all_to_all | solution.py:365
